TPU v7x, 32 devices: a whole 2x2x4 slice. The times are simulated.
32 devices in a mesh: dp: 32 (over z, y, x, core).
Axes of the slice: x: 2, y: 2, z: 4, core: 2. Of those that a mesh axis runs over, the one named last changes fastest.
Arguments:
- tokens: bfloat16 [32, 1024, 768], P('dp'), may hold values from -6 to 6
- memory: bfloat16 [32, 1024, 768], P('dp'), may hold values from -6 to 6
- out_grad: bfloat16 [32, 1024, 768], P('dp'), may hold values from -6 to 6
- dec_len: int32 [32], P('dp'), may hold values from 192 to 1024, as said below
- mem_len: int32 [32], P('dp'), may hold values from 512 to 1024, as said below
- group_bounds: int32 [5], replicated, may hold values from 0 to 32, as said below
- self_norm_gain: float32 [768], replicated, may hold values from 0.5 to 1.5
- self_norm_bias: float32 [768], replicated, may hold values from -1.2 to 1.2
- self_query: bfloat16 [768, 768], replicated, may hold values from -0.21875 to 0.21875
- self_query_bias: float32 [768], replicated, may hold values from -1.2 to 1.2
- self_key: bfloat16 [768, 768], replicated, may hold values from -0.21875 to 0.21875
- self_value: bfloat16 [768, 768], replicated, may hold values from -0.21875 to 0.21875
- self_value_bias: float32 [768], replicated, may hold values from -1.2 to 1.2
- self_output: bfloat16 [768, 768], replicated, may hold values from -0.875 to 0.875
- self_output_bias: float32 [768], replicated, may hold values from -1.2 to 1.2
- position_bias: float32 [12, 256], replicated, may hold values from -3 to 3
- head_scale: float32 [12], replicated, may hold values from 0.5 to 1.5
- self_post_gain: float32 [768], replicated, may hold values from 0.5 to 1.5
- self_post_bias: float32 [768], replicated, may hold values from -1.2 to 1.2
- cross_norm_gain: float32 [768], replicated, may hold values from 0.5 to 1.5
- cross_norm_bias: float32 [768], replicated, may hold values from -1.2 to 1.2
- cross_query: bfloat16 [768, 768], replicated, may hold values from -0.21875 to 0.21875
- cross_query_bias: float32 [768], replicated, may hold values from -1.2 to 1.2
- cross_key: bfloat16 [768, 768], replicated, may hold values from -0.21875 to 0.21875
- cross_value: bfloat16 [768, 768], replicated, may hold values from -0.21875 to 0.21875
- cross_value_bias: float32 [768], replicated, may hold values from -1.2 to 1.2
- cross_output: bfloat16 [768, 768], replicated, may hold values from -0.875 to 0.875
- cross_output_bias: float32 [768], replicated, may hold values from -1.2 to 1.2
- cross_post_gain: float32 [768], replicated, may hold values from 0.5 to 1.5
- cross_post_bias: float32 [768], replicated, may hold values from -1.2 to 1.2
- feed_norm_gain: float32 [768], replicated, may hold values from 0.5 to 1.5
- feed_norm_bias: float32 [768], replicated, may hold values from -1.2 to 1.2
- feed_inner: bfloat16 [768, 3072], replicated, may hold values from -0.21875 to 0.21875
- feed_inner_bias: float32 [3072], replicated, may hold values from -3 to 3
- feed_mid_gain: float32 [3072], replicated, may hold values from 0.5 to 1.5
- feed_mid_bias: float32 [3072], replicated, may hold values from -1.2 to 1.2
- feed_outer: bfloat16 [3072, 768], replicated, may hold values from -0.109375 to 0.109375
- feed_outer_bias: float32 [768], replicated, may hold values from -1.2 to 1.2
Outputs:
- layer_out: bfloat16 [32, 1024, 768], P('dp')
- grad_tokens: float32 [32, 1024, 768], P('dp')
- grad_memory: float32 [32, 1024, 768], P('dp')
- grad_self_norm_gain: float32 [768], P('dp')
- grad_self_norm_bias: float32 [768], P('dp')
- grad_self_query: float32 [768, 768], P('dp')
- grad_self_query_bias: float32 [768], P('dp')
- grad_self_key: float32 [768, 768], P('dp')
- grad_self_value: float32 [768, 768], P('dp')
- grad_self_value_bias: float32 [768], P('dp')
- grad_self_output: float32 [768, 768], P('dp')
- grad_self_output_bias: float32 [768], P('dp')
- grad_position_bias: float32 [12, 256], P(None, 'dp')
- grad_head_scale: float32 [12], replicated
- grad_self_post_gain: float32 [768], P('dp')
- grad_self_post_bias: float32 [768], P('dp')
- grad_cross_norm_gain: float32 [768], P('dp')
- grad_cross_norm_bias: float32 [768], P('dp')
- grad_cross_query: float32 [768, 768], P('dp')
- grad_cross_query_bias: float32 [768], P('dp')
- grad_cross_key: float32 [768, 768], P('dp')
- grad_cross_value: float32 [768, 768], P('dp')
- grad_cross_value_bias: float32 [768], P('dp')
- grad_cross_output: float32 [768, 768], P('dp')
- grad_cross_output_bias: float32 [768], P('dp')
- grad_cross_post_gain: float32 [768], P('dp')
- grad_cross_post_bias: float32 [768], P('dp')
- grad_feed_norm_gain: float32 [768], P('dp')
- grad_feed_norm_bias: float32 [768], P('dp')
- grad_feed_inner: float32 [768, 3072], P('dp')
- grad_feed_inner_bias: float32 [3072], P('dp')
- grad_feed_mid_gain: float32 [3072], P('dp')
- grad_feed_mid_bias: float32 [3072], P('dp')
- grad_feed_outer: float32 [3072, 768], P('dp')
- grad_feed_outer_bias: float32 [768], P('dp')
Inputs may be any that keep to these rules, and one draw needn't show every extreme that they name: `group_bounds`: Increasing; entry 0 is 0 and the last entry is the number of devices; every task group holds one device or more, group k the devices from entry k to entry k + 1 minus one. `dec_len`: the rows beyond an item's length are padding. `mem_len`: the rows beyond an item's length are padding.
All inputs are finite; a program needn't handle non-finite values.
Results may differ from a plain program's by a relative error of at most 0.028.
Values sent between devices are 32-bit elements; how exact they have to be, the bound alone decides.
No kernel may reach another device: no remote copies, remote signals or barrier semaphores. Data moves between devices by JAX's collectives and lax.ppermute only.
A program may use at most 448 MiB of HBM per device.

v0:
```python
import functools
import jax, jax.numpy as jnp
from jax import lax
from jax.experimental import pallas as pl
from jax.experimental.pallas import tpu as pltpu
from jax.sharding import PartitionSpec as P
F32=jnp.float32; BF=jnp.bfloat16
LOG2E=1.4426950408889634
NEG=-1e30
TILE=256
SMEM=pl.BlockSpec(memory_space=pltpu.SMEM)
def cost(flops,nbytes,trans=0):
    return pl.CostEstimate(flops=int(flops)*200,bytes_accessed=int(nbytes)*200,transcendentals=int(trans))
def nt(a,b): return lax.dot_general(a,b,(((1,),(1,)),((),())),preferred_element_type=F32)
def nn(a,b): return lax.dot_general(a,b,(((1,),(0,)),((),())),preferred_element_type=F32)
def tn(a,b): return lax.dot_general(a,b,(((0,),(0,)),((),())),preferred_element_type=F32)
def params(n, mb=56, sem=None):
    return pltpu.CompilerParams(dimension_semantics=("arbitrary",)*n, vmem_limit_bytes=mb<<20)

def head_lanes(rows, h):
    lane=lax.broadcasted_iota(jnp.int32,(rows,128),1)
    return (lane<64) if h==0 else (lane>=64)

def mask_keys(k, limit, h):
    rows=k.shape[0]
    lane=lax.broadcasted_iota(jnp.int32,(rows,128),1)
    row=lax.broadcasted_iota(jnp.int32,(rows,128),0)
    spare=64 if h==0 else 0
    pen=jnp.where((lane==spare)&(row>=limit), NEG, 0.0)
    own=head_lanes(rows,h)
    return jnp.where(own,k.astype(F32),pen).astype(BF)
def mask_queries(q, h):
    rows=q.shape[0]
    lane=lax.broadcasted_iota(jnp.int32,(rows,128),1)
    spare=64 if h==0 else 0
    one=jnp.where(lane==spare,1.0,0.0)
    return jnp.where(head_lanes(rows,h),q.astype(F32),one).astype(BF)

def toeplitz(bias_row):
    r=jnp.concatenate([bias_row-bias_row[:,255:256], jnp.zeros((1,256),F32)],axis=1)
    x=jnp.broadcast_to(r,(TILE,512))
    return pltpu.roll(x,0,1,stride=1,stride_axis=0)

def fwd_kernel(causal, limit_ref, hs_ref, bias_ref, q_ref, k_ref, v_ref, o_ref, lse_ref, km, qm, vt, s_scr, p_scr, t_scr):
    S=q_ref.shape[0]; M=k_ref.shape[0]
    limit=limit_ref[0]
    vtf=v_ref[...].astype(F32).T
    ones=jnp.ones((16,M),BF)
    for h in range(2):
        km[h]=mask_keys(k_ref[...],limit,h)
        qm[h]=mask_queries(q_ref[...],h)
        vt[h,0:64]=vtf[h*64:(h+1)*64].astype(BF)
        vt[h,64:80]=ones
        if causal:
            t=toeplitz(bias_ref[pl.ds(2*pl.program_id(0)+h,1),:])
            kk=lax.broadcasted_iota(jnp.int32,(TILE,512),0)
            qq=lax.broadcasted_iota(jnp.int32,(TILE,512),1)
            t_scr[h]=jnp.where(qq>=kk,t,NEG)
    nq=S//TILE; nk=M//TILE
    for i in range(nq):
        qs=slice(i*TILE,(i+1)*TILE)
        accs=[]
        for h in range(2):
            tiles=range(i+1) if causal else range(nk)
            m=None
            for j in tiles:
                s=nt(km[h,j*TILE:(j+1)*TILE],qm[h,qs])
                if causal and j==i: s=s+t_scr[h,:,0:256]
                if causal and j==i-1: s=s+t_scr[h,:,256:512]
                s_scr[h,j*TILE:(j+1)*TILE]=s
                mj=jnp.max(s,axis=0,keepdims=True)
                m=mj if m is None else jnp.maximum(m,mj)
            m2=m*LOG2E
            n=len(tiles)*TILE
            for j in tiles:
                p_scr[h,j*TILE:(j+1)*TILE]=jnp.exp2(s_scr[h,j*TILE:(j+1)*TILE]*LOG2E-m2).astype(BF)
            acc=nn(vt[h,:,0:n],p_scr[h,0:n])
            l=acc[64:65]
            lse_ref[0,h:h+1,qs]=m2+jnp.log2(l)
            accs.append(acc[0:64]*((hs_ref[2*pl.program_id(0)+h] if causal else 1.0)/l))
        ot=jnp.concatenate(accs,axis=0)
        o_ref[qs]=ot.T.astype(BF)

def attn_fwd(causal, limit, hs, bias, q, k, v):
    S,D=q.shape; M=k.shape[0]
    pairs=D//128
    grid_spec=pltpu.PrefetchScalarGridSpec(
        num_scalar_prefetch=1, grid=(pairs,),
        in_specs=[SMEM,
                  pl.BlockSpec(bias.shape,lambda p,*_:(0,0)),
                  pl.BlockSpec((S,128),lambda p,*_:(0,p)),
                  pl.BlockSpec((M,128),lambda p,*_:(0,p)),
                  pl.BlockSpec((M,128),lambda p,*_:(0,p))],
        out_specs=[pl.BlockSpec((S,128),lambda p,*_:(0,p)),
                   pl.BlockSpec((1,2,S),lambda p,*_:(p,0,0))],
        scratch_shapes=[pltpu.VMEM((2,M,128),BF),pltpu.VMEM((2,S,128),BF),pltpu.VMEM((2,80,M),BF),
                        pltpu.VMEM((2,M,TILE),F32),pltpu.VMEM((2,M,TILE),BF),pltpu.VMEM((2,TILE,512),F32)])
    return pl.pallas_call(functools.partial(fwd_kernel,causal),grid_spec=grid_spec,
        out_shape=(jax.ShapeDtypeStruct((S,D),BF),jax.ShapeDtypeStruct((pairs,2,S),F32)),
        compiler_params=params(1),name="attn_fwd",
        cost_estimate=cost(4*S*M*D*(1 if causal else 2),8*S*D,S*M*D//128))(limit,hs,bias,q,k,v)

def bwd_kernel(causal, p0, chained, limit_ref, hs_ref, bias_ref, q_ref, k_ref, v_ref, go_ref, a_ref, lse_ref, *rest):
    if chained: rest=rest[5 if causal else 4:]
    pair=pl.program_id(0)+p0
    if causal:
        gq_ref, gk_ref, gv_ref, ds_ref, gb_ref, km, qm, q0, vm, gom, kt, p_scr, gs_scr, gqt, dl, t_scr, d_scr, far = rest
    else:
        gq_ref, gk_ref, gv_ref, ds_ref, km, qm, q0, vm, gom, kt, p_scr, gs_scr, gqt, dl = rest
    S=q_ref.shape[0]; M=k_ref.shape[0]
    nq=S//TILE; nk=M//TILE
    limit=limit_ref[0]
    kt[...]=k_ref[...].astype(F32).T.astype(BF)
    sel=jnp.concatenate([jnp.where(head_lanes(1,h),1.0,0.0) for h in range(2)]+[jnp.zeros((14,128),F32)],axis=0).astype(BF)
    x=go_ref[...].astype(F32)*a_ref[...].astype(F32)
    if causal:
        lane=lax.broadcasted_iota(jnp.int32,(1,128),1)
        x=x*(1.0/jnp.where(lane<64,jnp.full((1,128),hs_ref[2*pair],F32),jnp.full((1,128),hs_ref[2*pair+1],F32)))
    hi=x.astype(BF); lo=(x-hi.astype(F32)).astype(BF)
    dd=nt(sel,hi)+nt(sel,lo)
    dl[...]=dd[0:8]
    ds_ref[0]=jnp.broadcast_to(jnp.sum(dd[0:2],axis=1,keepdims=True),(2,128))
    zero=jnp.zeros((),F32)
    for h in range(2):
        km[h]=mask_keys(k_ref[...],limit,h)
        qm[h]=mask_queries(q_ref[...],h)
        own=head_lanes(S,h)
        q0[h]=jnp.where(own,q_ref[...].astype(F32),zero).astype(BF)
        gom[h]=jnp.where(own,go_ref[...].astype(F32),zero).astype(BF)
        vm[h]=jnp.where(head_lanes(M,h),v_ref[...].astype(F32),zero).astype(BF)
        if causal:
            t=toeplitz(bias_ref[pl.ds(2*pair+h,1),:])*LOG2E
            kk=lax.broadcasted_iota(jnp.int32,(TILE,512),0)
            qq=lax.broadcasted_iota(jnp.int32,(TILE,512),1)
            t_scr[h]=jnp.where(qq>=kk,t,NEG)
    if causal:
        d_scr[...]=jnp.zeros_like(d_scr); far[...]=jnp.zeros_like(far)
    gqt[...]=jnp.zeros_like(gqt)
    def block(j):
        js=slice(j*TILE,(j+1)*TILE)
        i0=j if causal else 0
        for h in range(2):
            for i in range(i0,nq):
                qs=slice(i*TILE,(i+1)*TILE)
                s=nt(km[h,js],qm[h,qs])*LOG2E
                if causal and i-j<2:
                    s=s+t_scr[h,:,(i-j)*TILE:(i-j+1)*TILE]
                p=jnp.exp2(s-lse_ref[0,h:h+1,qs])
                gs=p*(nt(vm[h,js],go_ref[qs])-dl[h:h+1,qs])
                p_scr[h,:,qs]=p.astype(BF)
                gs_scr[h,:,qs]=gs.astype(BF)
                if causal:
                    if i-j<2:
                        d_scr[h,:,(i-j)*TILE:(i-j+1)*TILE]+=gs
                    else:
                        far[h]+=jnp.sum(gs.reshape(TILE//8,8,TILE),axis=0)
            gqt[h*64:(h+1)*64,i0*TILE:]+=nn(kt[h*64:(h+1)*64,js],gs_scr[h,:,i0*TILE:])
        gv_ref[js]=(nn(p_scr[0,:,i0*TILE:],gom[0,i0*TILE:])+nn(p_scr[1,:,i0*TILE:],gom[1,i0*TILE:])).astype(BF)
        gk_ref[js]=(nn(gs_scr[0,:,i0*TILE:],q0[0,i0*TILE:])+nn(gs_scr[1,:,i0*TILE:],q0[1,i0*TILE:])).astype(BF)
    for j in range(nk):
        if causal:
            block(j)
        else:
            @pl.when(j*TILE<limit)
            def _(): block(j)
            @pl.when(j*TILE>=limit)
            def _():
                gv_ref[j*TILE:(j+1)*TILE]=jnp.zeros((TILE,128),BF)
                gk_ref[j*TILE:(j+1)*TILE]=jnp.zeros((TILE,128),BF)
    gq_ref[...]=gqt[...].T.astype(BF)
    if causal:
        for h in range(2):
            acc=jnp.zeros((8,512),F32)
            for g in range(TILE//8):
                acc=acc+pltpu.roll(d_scr[h,8*g:8*g+8],(512-8*g)%512,1)
            near=jnp.zeros((1,512),F32)
            for r in range(8):
                near=near+pltpu.roll(acc[r:r+1],(512-r)%512,1)
            lane=lax.broadcasted_iota(jnp.int32,(1,512),1)
            tail=jnp.sum(jnp.where(lane>=255,near,0.0),axis=1,keepdims=True)+jnp.sum(jnp.sum(far[h],axis=0,keepdims=True),axis=1,keepdims=True)
            gb_ref[0,h:h+1,:]=jnp.where(lane[:,:256]==255,tail,near[:,:256])

def attn_bwd(causal, limit, hs, bias, q, k, v, go, a, lse, p0, count, before=None):
    S,D=q.shape; M=k.shape[0]
    pairs=D//128
    col=pl.BlockSpec((S,128),lambda p,*_:(0,p+p0))
    colm=pl.BlockSpec((M,128),lambda p,*_:(0,p+p0))
    outs=[col,colm,colm,pl.BlockSpec((1,2,128),lambda p,*_:(p+p0,0,0))]
    shapes=[jax.ShapeDtypeStruct((S,D),BF),jax.ShapeDtypeStruct((M,D),BF),jax.ShapeDtypeStruct((M,D),BF),jax.ShapeDtypeStruct((pairs,2,128),F32)]
    scr=[pltpu.VMEM((2,M,128),BF),pltpu.VMEM((2,S,128),BF),pltpu.VMEM((2,S,128),BF),pltpu.VMEM((2,M,128),BF),pltpu.VMEM((2,S,128),BF),
         pltpu.VMEM((128,M),BF),pltpu.VMEM((2,TILE,S),BF),pltpu.VMEM((2,TILE,S),BF),pltpu.VMEM((128,S),F32),pltpu.VMEM((8,S),F32)]
    if causal:
        outs.append(pl.BlockSpec((1,2,256),lambda p,*_:(p+p0,0,0))); shapes.append(jax.ShapeDtypeStruct((pairs,2,256),F32))
        scr+=[pltpu.VMEM((2,TILE,512),F32),pltpu.VMEM((2,TILE,512),F32),pltpu.VMEM((2,8,TILE),F32)]
    extra=() if before is None else tuple(before)
    grid_spec=pltpu.PrefetchScalarGridSpec(
        num_scalar_prefetch=1, grid=(count,),
        in_specs=[SMEM,pl.BlockSpec(bias.shape,lambda p,*_:(0,0)),
                  col,colm,colm,col,col,pl.BlockSpec((1,2,S),lambda p,*_:(p+p0,0,0))]+[pl.BlockSpec(memory_space=pl.ANY)]*len(extra),
        out_specs=outs, scratch_shapes=scr)
    return pl.pallas_call(functools.partial(bwd_kernel,causal,p0,before is not None),grid_spec=grid_spec,out_shape=tuple(shapes),
        input_output_aliases={9+i:i for i in range(len(extra))},
        cost_estimate=cost(10*S*M*D*(1 if causal else 2)*count//pairs,16*S*D*count//pairs,S*M*D//128),
        compiler_params=params(1),name="attn_bwd")(limit,hs,bias,q,k,v,go,a,lse,*extra)
EPS=1e-5
TASKS=4
def norm_rows(v):
    c=v-jnp.mean(v,axis=-1,keepdims=True)
    inv=lax.rsqrt(jnp.mean(c*c,axis=-1,keepdims=True)+EPS)
    return c*inv,inv
def norm_back(e,n,inv,g):
    s=e*g
    return (s-jnp.mean(s,axis=-1,keepdims=True)-n*jnp.mean(s*n,axis=-1,keepdims=True))*inv
def col_sum(v): return jnp.sum(v,axis=0,keepdims=True)

def vec(ref):
    return ref[...].reshape(1,-1)
def whole(shape):
    return pl.BlockSpec(shape,lambda *_:(0,)*len(shape),pipeline_mode=pl.Buffered(1))
def rows_of(rows,cols):
    return pl.BlockSpec((rows,cols),lambda i,*_:(i,0))

def pre_kernel(x_ref,m_ref,g_ref,b_ref,wq,qb,wk,wv,vb,ck,cv,cvb,q_o,k_o,v_o,k2_o,v2_o):
    n,_=norm_rows(x_ref[...].astype(F32))
    h=(n*vec(g_ref)+vec(b_ref)).astype(BF)
    q_o[...]=((nn(h,wq[...])+vec(qb))*0.125).astype(BF)
    k_o[...]=nn(h,wk[...]).astype(BF)
    v_o[...]=(nn(h,wv[...])+vec(vb)).astype(BF)
    m=m_ref[...]
    k2_o[...]=nn(m,ck[...]).astype(BF)
    v2_o[...]=(nn(m,cv[...])+vec(cvb)).astype(BF)

def pre(x,m,g,b,wq,qb,wk,wv,vb,ck,cv,cvb,T=256):
    S,D=x.shape
    r=rows_of(T,D); w=whole((D,D)); u=whole((D,))
    o=jax.ShapeDtypeStruct((S,D),BF)
    return pl.pallas_call(pre_kernel,grid=(S//T,),in_specs=[r,r,u,u,w,u,w,w,u,w,w,u],out_specs=[r]*5,out_shape=[o]*5,
        compiler_params=params(1),name="pre",cost_estimate=cost(10*S*D*D,10*D*D+14*S*D))(x,m,g,b,wq,qb,wk,wv,vb,ck,cv,cvb)

def post_kernel(a_ref,x_ref,wo,bo,pg,pb,ng,nb,wq,qb,x1_o,q2_o,n_o,inv_o):
    n,inv=norm_rows(nn(a_ref[...],wo[...])+vec(bo))
    n_o[...]=n.astype(BF); inv_o[...]=inv
    x1=x_ref[...].astype(F32)+(n*vec(pg)+vec(pb))
    x1_o[...]=x1
    n2,_=norm_rows(x1)
    h=(n2*vec(ng)+vec(nb)).astype(BF)
    q2_o[...]=((nn(h,wq[...])+vec(qb))*0.125).astype(BF)

def post(a,x,wo,bo,pg,pb,ng,nb,wq,qb,T=256):
    S,D=x.shape
    r=rows_of(T,D); w=whole((D,D)); u=whole((D,))
    o=jax.ShapeDtypeStruct((S,D),BF)
    return pl.pallas_call(post_kernel,grid=(S//T,),in_specs=[r,r,w,u,u,u,u,u,w,u],
        out_specs=[r,r,r,rows_of(T,1)],out_shape=[jax.ShapeDtypeStruct((S,D),F32),o,o,jax.ShapeDtypeStruct((S,1),F32)],
        compiler_params=params(1),name="post",cost_estimate=cost(4*S*D*D,4*D*D+12*S*D))(a,x,wo,bo,pg,pb,ng,nb,wq,qb)

SQH=0.7071067811865476
ERFC=(-1.26551223,1.00002368,0.37409196,0.09678418,-0.18628806,0.27886807,-1.13520398,1.48851587,-0.82215223,0.17087277)
def gelu_parts(f):
    z=jnp.abs(f)*SQH
    t=1.0/(1.0+0.5*z)
    poly=jnp.full_like(t,ERFC[9]*LOG2E)
    for c in ERFC[8::-1]:
        poly=poly*t+c*LOG2E
    zz=z*z*LOG2E
    half=0.5*t*jnp.exp2(poly-zz)
    phi=jnp.where(f<0.0,half,1.0-half)
    dens=jnp.exp2(-zz)*0.3989422804014327
    return f*phi, phi+f*dens

CH=256
def mid_kernel(n,dec_ref,gb_ref,idx_ref,all_ref,a2_ref,x1_ref,og_ref,cwo,wi,wout,cbo,cpg,cpb,fng,fnb,bi,mg,mb,bo,
               lo_o,gx2_o,go2_o,u_o,gf_o,h3_o,g3_o,gb2_o,v1_o,v3_o,fac_o,ge,dg,gus):
    T,D=a2_ref.shape; FF=wi.shape[1]
    bi_v=vec(bi); mg_v=vec(mg); mb_v=vec(mb)
    step=pl.program_id(0)
    row=step*T+lax.broadcasted_iota(jnp.int32,(T,1),0)
    valid=row<dec_ref[0]
    n_b,inv_b=norm_rows(nn(a2_ref[...],cwo[...])+vec(cbo))
    x2=x1_ref[...]+(n_b*vec(cpg)+vec(cpb))
    n_x,inv_x=norm_rows(x2)
    h3=(n_x*vec(fng)+vec(fnb)).astype(BF)
    h3_o[...]=h3
    part=jnp.zeros((T,128),F32)
    for c in range(0,FF,CH):
        f=nn(h3,wi[:,c:c+CH])+bi_v[:,c:c+CH]
        a,d=gelu_parts(f)
        ge[:,c:c+CH]=a
        dg[:,c:c+CH]=d
        for l in range(0,CH,128): part=part+a[:,l:l+128]
    mean=jnp.sum(part,axis=1,keepdims=True)*(1.0/FF)
    part=jnp.zeros((T,128),F32)
    for c in range(0,FF,CH):
        e=ge[:,c:c+CH]-mean
        e=e*e
        for l in range(0,CH,128): part=part+e[:,l:l+128]
    inv=lax.rsqrt(jnp.sum(part,axis=1,keepdims=True)*(1.0/FF)+EPS)
    g3=jnp.where(valid,og_ref[...].astype(F32),0.0)
    g3b=g3.astype(BF)
    g3_o[...]=g3b
    s1=jnp.zeros((T,128),F32); s2=jnp.zeros((T,128),F32)
    @pl.when(step==0)
    def _():
        v1_o[...]=jnp.zeros_like(v1_o); v3_o[...]=jnp.zeros_like(v3_o)
        owner=lax.broadcasted_iota(jnp.int32,(n,8,128),0)
        task=sum((owner>=gb_ref[k]).astype(jnp.int32) for k in range(1,TASKS))
        mine=sum((idx_ref[0]>=gb_ref[k]).astype(jnp.int32) for k in range(1,TASKS))
        fac_o[...]=n/jnp.sum(jnp.where(task==mine,all_ref[...],0.0),axis=0)
    for c in range(0,FF,CH):
        cs=slice(c,c+CH)
        n=(ge[:,cs]-mean)*inv
        ge[:,cs]=n
        u_o[:,cs]=(n*mg_v[:,cs]+mb_v[:,cs]).astype(BF)
        gu=nt(g3b,wout[cs,:])
        en=gu*n
        v3_o[0:1,cs]+=col_sum(en)
        v3_o[1:2,cs]+=col_sum(gu)
        eg=gu*mg_v[:,cs]
        gus[:,cs]=eg
        egn=eg*n
        for l in range(0,CH,128):
            s1=s1+eg[:,l:l+128]; s2=s2+egn[:,l:l+128]
    m1=jnp.sum(s1,axis=1,keepdims=True)*(1.0/FF); m2=jnp.sum(s2,axis=1,keepdims=True)*(1.0/FF)
    out=x2+(nn(u_o[...],wout[...])+vec(bo))
    lo_o[...]=jnp.where(valid,out,0.0).astype(BF)
    for c in range(0,FF,CH):
        cs=slice(c,c+CH)
        gf=((gus[:,cs]-m1-ge[:,cs]*m2)*inv*dg[:,cs]).astype(BF)
        gf_o[:,cs]=gf
        v3_o[2:3,cs]+=col_sum(gf.astype(F32))
    gh=nt(gf_o[...],wi[...])
    v1_o[0:1]+=col_sum(gh*n_x); v1_o[1:2]+=col_sum(gh)
    gx2=g3+norm_back(gh,n_x,inv_x,vec(fng))
    gx2_o[...]=gx2
    v1_o[2:3]+=col_sum(g3)
    v1_o[3:4]+=col_sum(gx2*n_b); v1_o[4:5]+=col_sum(gx2)
    gb2=norm_back(gx2,n_b,inv_b,vec(cpg)).astype(BF)
    gb2_o[...]=gb2
    v1_o[5:6]+=col_sum(gb2.astype(F32))
    go2_o[...]=nt(gb2,cwo[...]).astype(BF)

def mid(n,dec,gb,idx,all_dec,a2,x1,og,cwo,wi,wout,cbo,cpg,cpb,fng,fnb,bi,mg,mb,bo,T=256):
    S,D=x1.shape; FF=wi.shape[1]
    r=rows_of(T,D); rf=rows_of(T,FF); u=whole((D,)); uf=whole((FF,))
    sd=jax.ShapeDtypeStruct
    acc=lambda s: pl.BlockSpec(s,lambda *_:(0,0))
    return pl.pallas_call(functools.partial(mid_kernel,n),grid=(S//T,),
        in_specs=[SMEM,SMEM,SMEM,whole((n,8,128)),r,r,r,whole((D,D)),whole((D,FF)),whole((FF,D)),u,u,u,u,u,uf,uf,uf,u],
        out_specs=[r,r,r,rf,rf,r,r,r,acc((8,D)),acc((8,FF)),acc((8,128))],
        out_shape=[sd((S,D),BF),sd((S,D),F32),sd((S,D),BF),sd((S,FF),BF),sd((S,FF),BF),sd((S,D),BF),sd((S,D),BF),sd((S,D),BF),sd((8,D),F32),sd((8,FF),F32),sd((8,128),F32)],
        scratch_shapes=[pltpu.VMEM((T,FF),F32)]*3,
        compiler_params=params(1,58),name="mid",
        cost_estimate=cost(8*S*D*FF+4*S*D*D,4*D*FF+2*D*D+S*D*20+4*S*FF,S*FF*3))(dec,gb,idx,all_dec,a2,x1,og,cwo,wi,wout,cbo,cpg,cpb,fng,fnb,bi,mg,mb,bo)

def head_row(hs_ref,D,H):
    lane=lax.broadcasted_iota(jnp.int32,(1,D),1)//(D//H)
    v=jnp.zeros((1,D),F32)
    for h in range(H): v=jnp.where(lane==h,hs_ref[h],v)
    return v
def cross_back_kernel(hs_ref,gq_ref,x1_ref,gx2_ref,n_ref,inv_ref,gv_ref,cwq,wo,cng,cnb,spg,
                      gx1_o,go1_o,h2_o,gqs_o,gb1_o,v_o):
    @pl.when(pl.program_id(0)==0)
    def _(): v_o[...]=jnp.zeros_like(v_o)
    gq=gq_ref[...]*jnp.asarray(0.125,BF)
    gqs_o[...]=gq
    n,inv=norm_rows(x1_ref[...])
    h2_o[...]=(n*vec(cng)+vec(cnb)).astype(BF)
    gh=nt(gq,cwq[...])
    v_o[0:1]+=col_sum(gh*n); v_o[1:2]+=col_sum(gh)
    v_o[2:3]+=col_sum(gq.astype(F32)); v_o[3:4]+=col_sum(gv_ref[...].astype(F32))
    gx1=gx2_ref[...]+norm_back(gh,n,inv,vec(cng))
    gx1_o[...]=gx1
    nb=n_ref[...].astype(F32)
    v_o[4:5]+=col_sum(gx1*nb); v_o[5:6]+=col_sum(gx1)
    gb1=norm_back(gx1,nb,inv_ref[...],vec(spg)).astype(BF)
    gb1_o[...]=gb1
    v_o[6:7]+=col_sum(gb1.astype(F32))
    go1_o[...]=(nt(gb1,wo[...])*head_row(hs_ref,gb1.shape[1],hs_ref.shape[0])).astype(BF)

def cross_back(hs,gq,x1,gx2,n,inv,gv,cwq,wo,cng,cnb,spg,T=256):
    S,D=x1.shape
    r=rows_of(T,D); w=whole((D,D)); u=whole((D,))
    sd=jax.ShapeDtypeStruct
    return pl.pallas_call(cross_back_kernel,grid=(S//T,),in_specs=[SMEM,r,r,r,r,rows_of(T,1),r,w,w,u,u,u],
        out_specs=[r,r,r,r,r,pl.BlockSpec((8,D),lambda *_:(0,0))],
        out_shape=[sd((S,D),F32)]+[sd((S,D),BF)]*4+[sd((8,D),F32)],
        compiler_params=params(1),name="cross_back",cost_estimate=cost(4*S*D*D,4*D*D+28*S*D))(hs,gq,x1,gx2,n,inv,gv,cwq,wo,cng,cnb,spg)

def self_norm_kernel(x_ref,gq_ref,gv_ref,g_ref,b_ref,h_o,gqs_o,v_o):
    @pl.when(pl.program_id(0)==0)
    def _(): v_o[...]=jnp.zeros_like(v_o)
    n,_=norm_rows(x_ref[...].astype(F32))
    h_o[...]=(n*vec(g_ref)+vec(b_ref)).astype(BF)
    gq=gq_ref[...]*jnp.asarray(0.125,BF)
    gqs_o[...]=gq
    v_o[0:1]+=col_sum(gq.astype(F32)); v_o[1:2]+=col_sum(gv_ref[...].astype(F32))
def self_norm(x,gq,gv,g,b,T=256):
    S,D=x.shape
    r=rows_of(T,D); u=whole((D,)); sd=jax.ShapeDtypeStruct
    return pl.pallas_call(self_norm_kernel,grid=(S//T,),in_specs=[r,r,r,u,u],out_specs=[r,r,pl.BlockSpec((8,D),lambda *_:(0,0))],
        out_shape=[sd((S,D),BF)]*2+[sd((8,D),F32)],compiler_params=params(1),name="self_norm",cost_estimate=cost(S*D*20,S*D*10))(x,gq,gv,g,b)

def tail_kernel(fac_ref,hs_ref,x_ref,gx1_ref,gq_ref,gk_ref,gv_ref,wq,wk,wv,g_ref,va,vb,vc,vf,gb,ds,gt_o,v_o):
    D=x_ref.shape[1]; H=hs_ref.shape[0]
    fac=fac_ref[0:1,0:1]
    @pl.when(pl.program_id(0)==0)
    def _():
        v_o[...]=jnp.zeros_like(v_o)
        v_o[0:8]=va[...]*fac
        v_o[8:16]=vb[...]*fac
        v_o[16:18]=vc[0:2]*fac
        for k in range(3):
            for c in range(vf.shape[1]//D):
                v_o[24+4*k+c:25+4*k+c]=vf[k:k+1,c*D:(c+1)*D]*fac
        for h in range(H):
            v_o[36+h:37+h,0:256]=gb[h//2,h%2:h%2+1,:]*fac
            v_o[36+h:37+h,256:384]=ds[h//2,h%2:h%2+1,:]*fac*(1.0/jnp.full((1,1),hs_ref[h],F32))
    n,inv=norm_rows(x_ref[...].astype(F32))
    gh=nt(gq_ref[...],wq[...])+nt(gk_ref[...],wk[...])+nt(gv_ref[...],wv[...])
    v_o[18:19]+=col_sum(gh*n)*fac; v_o[19:20]+=col_sum(gh)*fac
    gt_o[...]=gx1_ref[...]+norm_back(gh,n,inv,vec(g_ref))
def tail(fac,hs,x,gx1,gq,gk,gv,wq,wk,wv,g,va,vb,vc,vf,gb,ds,T=256):
    S,D=x.shape
    r=rows_of(T,D); w=whole((D,D)); u=whole((D,)); sd=jax.ShapeDtypeStruct
    return pl.pallas_call(tail_kernel,grid=(S//T,),in_specs=[whole((8,128)),SMEM]+[r]*5+[w]*3+[u]+[whole(v.shape) for v in (va,vb,vc,vf,gb,ds)],
        out_specs=[r,pl.BlockSpec((48,D),lambda *_:(0,0))],
        out_shape=[sd((S,D),F32)]+[sd((48,D),F32)],compiler_params=params(1),name="tail",cost_estimate=cost(10*S*D*D,10*D*D+S*D*24))(fac,hs,x,gx1,gq,gk,gv,wq,wk,wv,g,va,vb,vc,vf,gb,ds)

def memory_kernel(k_ref,v_ref,ck,cv,o):
    o[...]=nt(k_ref[...],ck[...])+nt(v_ref[...],cv[...])
def memory_grad(gk,gv,ck,cv,T=256):
    S,D=gk.shape
    r=rows_of(T,D); w=whole((D,D))
    return pl.pallas_call(memory_kernel,grid=(S//T,),in_specs=[r,r,w,w],out_specs=r,out_shape=jax.ShapeDtypeStruct((S,D),F32),
        compiler_params=params(1),name="memory",cost_estimate=cost(4*S*D*D,4*D*D+S*D*8))(gk,gv,ck,cv)

ROWS=(18,19,16,17,14,12,13,8,9,10,11,5,3,4,0,1,2)
def pick_kernel(n,idx_ref,v,*outs):
    D=v.shape[1]; w=D//n; idx=idx_ref[0]
    x=pltpu.roll(v[0:24],lax.rem(D-w*idx,D),1)
    for r,o in zip(ROWS,outs): o[...]=x[r:r+1,:w].reshape(w)
    each=n//4; wide=4*D//n
    shift=lax.rem(D-wide*lax.rem(idx,each),D)
    for k in range(3):
        y=pltpu.roll(v[pl.ds(24+4*k+idx//each,1),:],shift,1)
        outs[17+k][...]=y[:,:wide].reshape(wide)
    H=outs[20].shape[0]; b=256//n
    z=pltpu.roll(v[36:36+H,0:256],lax.rem(256-b*idx,256),1)
    outs[20][...]=z[:,:b]
    eye=lax.broadcasted_iota(jnp.int32,(H,128),0)==lax.broadcasted_iota(jnp.int32,(H,128),1)
    outs[21][...]=col_sum(jnp.where(eye,v[36:36+H,256:384],0.0))[:,:H].reshape(H)
def pick(n,idx,v,H):
    D=v.shape[1]; sd=jax.ShapeDtypeStruct
    shapes=[sd((D//n,),F32)]*17+[sd((4*D//n,),F32)]*3+[sd((H,256//n),F32),sd((H,),F32)]
    return pl.pallas_call(functools.partial(pick_kernel,n),in_specs=[SMEM,pl.BlockSpec(v.shape)],out_shape=shapes,
        compiler_params=params(0),name="pick")(idx,v)

def part_rows(scr,core,keep_o,send_o):
    groups,r=keep_o.shape[:2]
    for t in range(groups):
        if r%8==0:
            keep_o[t]=scr[pl.ds((2*t+core)*r,r),:]
            send_o[t]=scr[pl.ds((2*t+1-core)*r,r),:]
        else:
            even=scr[2*t*r:(2*t+1)*r,:]
            odd=scr[(2*t+1)*r:(2*t+2)*r,:]
            keep_o[t]=jnp.where(core==0,even,odd)
            send_o[t]=jnp.where(core==0,odd,even)
def wrow_kernel(core_ref,fac_ref,l_ref,r_ref,keep_o,send_o,scr):
    scr[...]=tn(l_ref[...],r_ref[...])*fac_ref[0:1,0:1]
    part_rows(scr,core_ref[0],keep_o,send_o)
def wgrad_rows(core,fac,lhs,rhs,n,B=768):
    S,M=lhs.shape; N=rhs.shape[1]; r=M//n; steps=M//B; groups=B//r//2
    o=pl.BlockSpec((groups,r,N),lambda i:(i,0,0)); sh=jax.ShapeDtypeStruct((n//2,r,N),F32)
    return pl.pallas_call(wrow_kernel,grid=(steps,),
        in_specs=[SMEM,whole((8,128)),pl.BlockSpec((S,B),lambda i:(0,i)),whole((S,N))],
        out_specs=[o,o],scratch_shapes=[pltpu.VMEM((B,N),F32)],out_shape=[sh,sh],compiler_params=params(1),name="wgrad",
        cost_estimate=cost(4*S*M*N,2*S*(M+N)+4*M*N))(core,fac,lhs,rhs)
def wcol_kernel(plan,core_ref,fac_ref,*refs):
    ins=refs[:-3]; keep_o,send_o,scr=refs[-3:]
    step=pl.program_id(0)
    for l,r,first,last in plan:
        @pl.when((step>=first)&(step<last))
        def _(): scr[...]=tn(ins[l][...],ins[r][...])*fac_ref[0:1,0:1]
    part_rows(scr,core_ref[0],keep_o,send_o)
def wgrad_cols(core,fac,pairs,n,B=768):
    ins=[]; specs=[]; plan=[]; at=0; seen={}
    S,M=pairs[0][0].shape
    for lhs,rhs in pairs:
        if id(lhs) not in seen:
            seen[id(lhs)]=len(ins); ins.append(lhs); specs.append(whole((S,M)))
        steps=rhs.shape[1]//B
        plan.append((seen[id(lhs)],len(ins),at,at+steps))
        ins.append(rhs)
        specs.append(pl.BlockSpec((S,B),functools.partial(lambda at,steps,i:(0,jnp.clip(i-at,0,steps-1)),at,steps)))
        at+=steps
    N=at*B; r=M//n
    o=pl.BlockSpec((n//2,r,B),lambda i:(0,0,i)); sh=jax.ShapeDtypeStruct((n//2,r,N),F32)
    return pl.pallas_call(functools.partial(wcol_kernel,plan),grid=(at,),in_specs=[SMEM,whole((8,128))]+specs,
        out_specs=[o,o],scratch_shapes=[pltpu.VMEM((M,B),F32)],out_shape=[sh,sh],compiler_params=params(1),name="wgrad",
        cost_estimate=cost(4*S*M*N,2*S*M*len(ins)+4*M*N))(core,fac,*ins)

def halve_kernel(bit_ref,km,ko,gm,go,keep_o,send_o):
    send_o[...]=ko[:,0]+go[:,0]
    keep_o[...]=km[:,0]+gm[:,0]
def halve(bit,keep,got,part=0,parts=1):
    A,_,B,r,C=keep.shape
    C=C//parts
    K=max(1,A//4)
    mine=pl.BlockSpec((K,1,B,r,C),lambda i,b:(i,b[0],0,0,part)); other=pl.BlockSpec((K,1,B,r,C),lambda i,b:(i,1-b[0],0,0,part))
    o=pl.BlockSpec((K,B,r,C),lambda i,b:(i,0,0,0)); sh=jax.ShapeDtypeStruct((A,B,r,C),F32)
    gs=pltpu.PrefetchScalarGridSpec(num_scalar_prefetch=1,grid=(A//K,),in_specs=[mine,other,mine,other],out_specs=[o,o])
    return pl.pallas_call(halve_kernel,grid_spec=gs,out_shape=[sh,sh],compiler_params=params(1),name="halve",
        cost_estimate=cost(1000,1000))(bit,keep,keep,got,got)

def deal_kernel(z_ref,k0,k1,k2,k3,g0,g1,g2,g3,o0,o1,o2,o3):
    for k,g,o in ((k0,g0,o0),(k1,g1,o1),(k2,g2,o2),(k3,g3,o3)):
        o[...]=k[0]+g[0]
def deal(z,keep,got):
    _,r,C=keep.shape
    spec=lambda m: pl.BlockSpec((1,r,C),lambda i,z,m=m:(z[0]^m,0,0))
    o=pl.BlockSpec((r,C),lambda i,z:(0,0)); sh=jax.ShapeDtypeStruct((r,C),F32)
    gs=pltpu.PrefetchScalarGridSpec(num_scalar_prefetch=1,grid=(1,),in_specs=[spec(m) for m in range(4)]*2,out_specs=[o]*4)
    return pl.pallas_call(deal_kernel,grid_spec=gs,out_shape=[sh]*4,compiler_params=params(1),name="deal",
        cost_estimate=cost(1000,1000))(z,*([keep]*4),*([got]*4))

def finish_kernel(plan,*refs):
    ins=refs[:-len(plan)]; outs=refs[-len(plan):]
    for o,pieces in zip(outs,plan):
        at=0
        for c,lo,hi in pieces:
            o[:,at:at+hi-lo]=(ins[4*c][:,lo:hi]+ins[4*c+1][:,lo:hi])+(ins[4*c+2][:,lo:hi]+ins[4*c+3][:,lo:hi])
            at+=hi-lo
def finish(chains,plan):
    ins=[v for c in chains for v in c.last]
    shapes=[jax.ShapeDtypeStruct((ins[4*p[0][0]].shape[0],sum(hi-lo for _,lo,hi in p)),F32) for p in plan]
    return pl.pallas_call(functools.partial(finish_kernel,plan),in_specs=[pl.BlockSpec(v.shape) for v in ins],out_shape=shapes,
        compiler_params=params(0),name="finish",cost_estimate=cost(1000,1000))(*ins)

def swap(x,n,bit):
    return lax.ppermute(x,"dp",[(j,j^(1<<bit)) for j in range(n)])
def after(token,*vals):
    return lax.optimization_barrier(tuple(vals)+tuple(token))[:len(vals)]
class Halving:
    def __init__(self,n,index,keep,send,order):
        self.n,self.index,self.order=n,index,list(order)
        self.live=list(range(n.bit_length()-2,0,-1))
        self.keep=keep; self.got=swap(send,n,0); self.part=(0,1)
    def split(self,orders):
        chains=[]
        for k,order in enumerate(orders):
            h=object.__new__(Halving)
            h.n,h.index,h.order,h.live=self.n,self.index,list(order),list(self.live)
            h.keep,h.got,h.part=self.keep,self.got,(k,len(orders))
            chains.append(h)
        return chains
    def step(self,token):
        keep,got=after(token,self.keep,self.got)
        b=self.order.pop(0)
        axis=self.live.index(b)
        self.live.remove(b)
        shape=(2**axis,2,2**(len(self.live)-axis))+keep.shape[-2:]
        bit=((self.index>>b)&1).reshape(1).astype(jnp.int32)
        self.keep,send=halve(bit,keep.reshape(shape),got.reshape(shape),*self.part)
        self.part=(0,1)
        self.got=swap(send,self.n,b)
        return send

    def last_step(self,token,zs):
        keep,got=after(token,self.keep,self.got)
        z=((self.index>>zs[0])&3).reshape(1).astype(jnp.int32)
        shape=(4,)+keep.shape[-2:]
        own,*sends=deal(z,keep.reshape(shape),got.reshape(shape))
        n=self.n
        self.last=[own]+[lax.ppermute(s,"dp",[(j,j^((m+1)<<zs[0])) for j in range(n)]) for m,s in enumerate(sends)]
        return own

def shards(n,tokens,memory,out_grad,dec_len,mem_len,group_bounds,
           self_norm_gain,self_norm_bias,self_query,self_query_bias,self_key,self_value,self_value_bias,self_output,self_output_bias,
           position_bias,head_scale,self_post_gain,self_post_bias,cross_norm_gain,cross_norm_bias,cross_query,cross_query_bias,
           cross_key,cross_value,cross_value_bias,cross_output,cross_output_bias,cross_post_gain,cross_post_bias,
           feed_norm_gain,feed_norm_bias,feed_inner,feed_inner_bias,feed_mid_gain,feed_mid_bias,feed_outer,feed_outer_bias):
    bits=n.bit_length()-1
    xs,ys,zs=([1],[2],[3,4]) if bits==5 else ([1,2],[3,4],list(range(5,bits)))
    order_a=xs+ys; order_b=ys+xs
    index=lax.axis_index("dp")
    idx=index.reshape(1).astype(jnp.int32)
    core=idx&1
    x=tokens[0]; m=memory[0]; og=out_grad[0]
    S,D=x.shape
    H=head_scale.shape[0]; pairs=H//2
    all_dec=lax.all_to_all(jnp.broadcast_to(dec_len.astype(F32).reshape(1,1,1),(n,8,128)),"dp",0,0,tiled=True)
    q1,k1,v1,k2,v2=pre(x,m,self_norm_gain,self_norm_bias,self_query,self_query_bias,self_key,self_value,self_value_bias,cross_key,cross_value,cross_value_bias)
    a1,lse1=attn_fwd(True,dec_len,head_scale,position_bias,q1,k1,v1)
    x1,q2,nb1,ib1=post(a1,x,self_output,self_output_bias,self_post_gain,self_post_bias,cross_norm_gain,cross_norm_bias,cross_query,cross_query_bias)
    a2,lse2=attn_fwd(False,mem_len,head_scale,position_bias,q2,k2,v2)
    lo,gx2,go2,u,gf,h3,g3,gb2,va,vf,fac=mid(n,dec_len,group_bounds,idx,all_dec,a2,x1,og,cross_output,feed_inner,feed_outer,cross_output_bias,cross_post_gain,cross_post_bias,feed_norm_gain,feed_norm_bias,feed_inner_bias,feed_mid_gain,feed_mid_bias,feed_outer_bias)
    keep,send=wgrad_cols(core,fac,[(h3,gf),(a2,gb2)],n)
    fi=Halving(n,index,keep,send,order_b)
    u,=after([send],u)
    keep,send=wgrad_rows(core,fac,u,g3,n)
    fo=Halving(n,index,keep,send,order_a)
    t=[fi.step([send])]
    t=[fo.step(t)]
    go2,=after(t,go2)
    back=attn_bwd(False,mem_len,head_scale,position_bias,q2,k2,v2,go2,a2,lse2,0,pairs)
    gq2,gk2,gv2,_=back
    gx1,go1,h2,gqs2,gb1,vb=cross_back(head_scale,gq2,x1,gx2,nb1,ib1,gv2,cross_query,self_output,cross_norm_gain,cross_norm_bias,self_post_gain)
    t=[fo.step([vb])]
    h2,=after(t,h2)
    keep,send=wgrad_cols(core,fac,[(h2,gqs2),(m,gv2),(m,gk2),(a1,gb1)],n)
    g2=Halving(n,index,keep,send,[])
    t=[fi.step([send])]
    go1,=after(t,go1)
    half=pairs//2
    back=attn_bwd(True,dec_len,head_scale,position_bias,q1,k1,v1,go1,a1,lse1,0,half)
    while fo.order: t=[fo.step([back[3]])]
    t=[fo.last_step([back[3]],zs)]
    ga,gb_=g2.split([order_a,order_b])
    t=[ga.step(t)]
    t=[gb_.step(t)]
    go1,=after(t,go1)
    gq1,gk1,gv1,ds,gb=attn_bwd(True,dec_len,head_scale,position_bias,q1,k1,v1,go1,a1,lse1,half,pairs-half,back)
    h1,gqs1,vc=self_norm(x,gq1,gv1,self_norm_gain,self_norm_bias)
    while fi.order: t=[fi.step([vc])]
    t=[fi.last_step([vc],zs)]
    h1,=after(t+fo.last[1:]+[ga.got,gb_.got],h1)
    t=[ga.step([vc,h1])]
    t=[gb_.step(t)]
    h1,=after(t,h1)
    keep,send=wgrad_cols(core,fac,[(h1,gqs1),(h1,gv1),(h1,gk1)],n)
    g3_=Halving(n,index,keep,send,[])
    gx1,=after([send],gx1)
    gt,packed=tail(fac,head_scale,x,gx1,gqs1,gk1,gv1,self_query,self_key,self_value,self_norm_gain,va,vb,vc,vf,gb,ds)
    sa,sb=g3_.split([order_a,order_b])
    t=[sa.step([packed])]
    t=[sb.step(t)]
    gk2,=after(t+fi.last[1:],gk2)
    bit=0
    other=swap(packed,n,bit)
    gm=memory_grad(gk2,gv2,cross_key,cross_value)
    t=[gm]
    def add_up(t,packed,other,bit):
        packed,other=after(t,packed,other)
        packed=packed+other
        bit+=1
        if (1<<bit)<n: other=swap(packed,n,bit)
        return packed,other,bit
    packed,other,bit=add_up(t,packed,other,bit)
    t=[packed]
    for c in (ga,gb_):
        while c.order: t=[c.step(t)]
        t=[c.last_step(t,zs)]
    packed,other,bit=add_up(t,packed,other,bit)
    t=[packed]
    while sa.order or sb.order:
        for c in (sa,sb): t=[c.step(t)]
        if (1<<bit)<n:
            packed,other,bit=add_up(t,packed,other,bit)
            t=[packed]
    for c in (sa,sb): t=[c.last_step(t,zs)]
    while (1<<bit)<n:
        packed,other,bit=add_up(t,packed,other,bit)
        t=[packed]
    small=pick(n,idx,packed,H)
    FF=feed_inner.shape[1]; M=D+D//2
    g_fo,g_fi,g_co,g_cq,g_cv,g_ck,g_so,g_sq,g_sv,g_sk=finish([fo,fi,ga,gb_,sa,sb],[
        [(0,0,D)],[(1,0,FF)],[(1,FF,FF+D)],[(2,0,D)],[(2,D,2*D)],[(3,0,D)],[(3,D,2*D)],
        [(4,0,D)],[(4,D,M),(5,0,D//2)],[(5,D//2,M)]])
    (sng,snb,sqb,svb,sob,spg,spb,cng,cnb,cqb,cvb,cob,cpg,cpb,fng,fnb,fob,fmg,fmb,fib,gpos,ghs)=small
    fo_b=fob
    return (lo[None],gt[None],gm[None],
        sng,snb,g_sq,sqb,g_sk,g_sv,svb,g_so,sob,gpos,ghs,spg,spb,cng,cnb,g_cq,cqb,g_ck,g_cv,cvb,g_co,cob,cpg,cpb,
        fng,fnb,g_fi,fib,fmg,fmb,g_fo,fo_b)

def solution(mesh):
    n=mesh.shape["dp"]
    vec=P("dp"); mat=P("dp",None); cube=P("dp",None,None)
    return jax.shard_map(functools.partial(shards,n),mesh=mesh,in_specs=(cube,cube,cube,vec,vec)+(P(),)*33,
        out_specs=(cube,cube,cube,vec,vec,mat,vec,mat,mat,vec,mat,vec,P(None,"dp"),P(),vec,vec,vec,vec,mat,vec,
                   mat,mat,vec,mat,vec,vec,vec,vec,vec,mat,vec,vec,vec,mat,vec),check_vma=False)
```

profile of v0, /device:TPU:0, one launch (start us, length us, event | category | flops | bytes accessed | tf_op | source)
XLA Modules:
  0.0 473.4 jit_solution(7952187616023655615)
XLA Ops:
  2.0 7.4 %all-to-all-start = ((f32[32,8,128]{2,1,0:T(8,128)}), f32[32,8,128]{2,1,0:T(8,128)}, u32[]{:S(2)}, u32[]{:S(2)}) async-start(f32[32,8,128]{2,1,0:T(8,128)} %broadcast_in_dim.17), calls=%async_computation | async-start | bytes 262144 | tf_op jit(solution)/shard_map/all_to_all | solution.py:592
  10.1 11.9 %pre.1 = (bf16[1024,768]{1,0:T(8,128)(2,1)}, bf16[1024,768]{1,0:T(8,128)(2,1)}, bf16[1024,768]{1,0:T(8,128)(2,1)}, bf16[1024,768]{1,0:T(8,128)(2,1)}, bf16[1024,768]{1,0:T(8,128)(2,1)}) custom-call(bf16[1024,768]{1,0:T(8,128)(2,1)} %bitcast.112, bf16[1024,768]{1,0:T(8,128)(2,1)} %bitcast.110, f32[768]{0:T(1024)} %g_ref.5, f32[768]{0:T(1024)} %b_ref.3, ...), custom_call_target="tpu_custom_call" | custom-call | flops 1207959552000 | bytes 3381657600 | tf_op jit(solution)/shard_map/pre/pallas_call | solution.py:237
  22.0 22.6 %attn_fwd.2 = (bf16[1024,768]{1,0:T(8,128)(2,1)}, f32[6,2,1024]{2,1,0:T(2,128)}) custom-call(s32[1]{0:T(128)S(6)} %copy.90.limit_ref.dec_ref, f32[12]{0:T(128)} %hs_ref.13, f32[12,256]{1,0:T(8,128)} %bias_ref.9, bf16[1024,768]{1,0:T(8,128)(2,1)} %get-tuple-element.226.q_ref, bf16[1024,768]{1,0:T(8,128)(2,1)} %get-tuple-element.227.k_ref, ...), custom_call_target="tpu_custom_call" | custom-call | flops 644245094400 | bytes 1258291200 | tf_op jit(solution)/shard_map/attn_fwd/pallas_call | solution.py:98
  44.6 9.4 %post.1 = (f32[1024,768]{1,0:T(8,128)}, bf16[1024,768]{1,0:T(8,128)(2,1)}, bf16[1024,768]{1,0:T(8,128)(2,1)}, f32[1024,1]{1,0:T(8,128)}) custom-call(bf16[1024,768]{1,0:T(8,128)(2,1)} %get-tuple-element.229.a_ref.refs_5_, bf16[1024,768]{1,0:T(8,128)(2,1)} %bitcast.113, bf16[768,768]{1,0:T(8,128)(2,1)} %wo.3, f32[768]{0:T(1024)} %bo.2, f32[768]{0:T(1024)} %spg.1, ...), custom_call_target="tpu_custom_call" | custom-call | flops 483183820800 | bytes 2359296000 | tf_op jit(solution)/shard_map/post/pallas_call | solution.py:253
  53.9 27.1 %attn_fwd.3 = (bf16[1024,768]{1,0:T(8,128)(2,1)}, f32[6,2,1024]{2,1,0:T(2,128)}) custom-call(s32[1]{0:T(128)S(6)} %copy.91.limit_ref, f32[12]{0:T(128)} %hs_ref.13, f32[12,256]{1,0:T(8,128)} %bias_ref.9, bf16[1024,768]{1,0:T(8,128)(2,1)} %get-tuple-element.230.q_ref, bf16[1024,768]{1,0:T(8,128)(2,1)} %get-tuple-element.231.k_ref, ...), custom_call_target="tpu_custom_call" | custom-call | flops 1288490188800 | bytes 1258291200 | tf_op jit(solution)/shard_map/attn_fwd/pallas_call | solution.py:98
  81.1 57.0 %mid.1 = (bf16[1024,768]{1,0:T(8,128)(2,1)}, f32[1024,768]{1,0:T(8,128)}, bf16[1024,768]{1,0:T(8,128)(2,1)}, bf16[1024,3072]{1,0:T(8,128)(2,1)}, bf16[1024,3072]...) custom-call(s32[1]{0:T(128)S(6)} %copy.90.limit_ref.dec_ref, ...), custom_call_target="tpu_custom_call" | custom-call | flops 4348654387200 | bytes 7785676800 | tf_op jit(solution)/shard_map/mid/pallas_call | solution.py:347
  138.1 13.6 %wgrad.4 = (f32[16,24,3840]{2,1,0:T(8,128)}, f32[16,24,3840]{2,1,0:T(8,128)}) custom-call(s32[1]{0:T(128)S(6)} %and.10.core_ref, f32[8,128]{1,0:T(8,128)} %get-tuple-element.236.fac_ref, bf16[1024,768]{1,0:T(8,128)(2,1)} %get-tuple-element.239.refs_0_, bf16[1024,3072]{1,0:T(8,128)(2,1)} %get-tuple-element.240.refs_1_, ...), custom_call_target="tpu_custom_call" | custom-call | flops 2415919104000 | bytes 3617587200 | tf_op jit(solution)/shard_map/wgrad/pallas_call | solution.py:499
  151.9 10.4 %wgrad.5 = (f32[16,96,768]{2,1,0:T(8,128)}, f32[16,96,768]{2,1,0:T(8,128)}) custom-call(s32[1]{0:T(128)S(6)} %and.10.core_ref, f32[8,128]{1,0:T(8,128)} %get-tuple-element.236.fac_ref, bf16[1024,3072]{1,0:T(8,128)(2,1)} %get-tuple-element.243.l_ref, bf16[1024,768]{1,0:T(8,128)(2,1)} %get-tuple-element.244.r_ref), custom_call_target="tpu_custom_call" | custom-call | flops 1932735283200 | bytes 3460300800 | tf_op jit(solution)/shard_map/wgrad/pallas_call | solution.py:475
  162.6 7.1 %halve.12 = (f32[4,2,24,3840]{3,2,1,0:T(8,128)}, f32[4,2,24,3840]{3,2,1,0:T(8,128)}) custom-call(s32[1]{0:T(128)} %bitcast.7.bit_ref, f32[4,2,2,24,3840]{4,3,2,1,0:T(8,128)} %bitcast.65, f32[4,2,2,24,3840]{4,3,2,1,0:T(8,128)} %bitcast.66, f32[4,2,2,24,3840]{4,3,2,1,0:T(8,128)} %bitcast.9.gm.go, f32[4,2,2,24,3840]{4,3,2,1,0:T(8,128)} %bitcast.9.gm.go), custom_call_target="tpu_custom_call" | custom-call | flops 200000 | bytes 200000 | tf_op jit(solution)/shard_map/halve/pallas_call | solution.py:513
  171.4 6.2 %halve.13 = (f32[8,1,96,768]{3,2,1,0:T(8,128)}, f32[8,1,96,768]{3,2,1,0:T(8,128)}) custom-call(s32[1]{0:T(128)} %bitcast.6.bit_ref, f32[8,2,1,96,768]{4,3,2,1,0:T(8,128)} %bitcast.71, f32[8,2,1,96,768]{4,3,2,1,0:T(8,128)} %bitcast.72, f32[8,2,1,96,768]{4,3,2,1,0:T(8,128)} %bitcast.11.gm.go, f32[8,2,1,96,768]{4,3,2,1,0:T(8,128)} %bitcast.11.gm.go), custom_call_target="tpu_custom_call" | custom-call | flops 200000 | bytes 200000 | tf_op jit(solution)/shard_map/halve/pallas_call | solution.py:513
  179.0 49.5 %attn_bwd.3 = (bf16[1024,768]{1,0:T(8,128)(2,1)}, bf16[1024,768]{1,0:T(8,128)(2,1)}, bf16[1024,768]{1,0:T(8,128)(2,1)}, f32[6,2,128]{2,1,0:T(2,128)}) custom-call(s32[1]{0:T(128)S(6)} %copy.91.limit_ref, f32[12]{0:T(128)} %hs_ref.13, f32[12,256]{1,0:T(8,128)} %bias_ref.9, bf16[1024,768]{1,0:T(8,128)(2,1)} %get-tuple-element.230.q_ref, ...), custom_call_target="tpu_custom_call" | custom-call | flops 3221225472000 | bytes 2516582400 | tf_op jit(solution)/shard_map/attn_bwd/pallas_call | solution.py:201
  228.5 11.7 %cross_back.1 = (f32[1024,768]{1,0:T(8,128)}, bf16[1024,768]{1,0:T(8,128)(2,1)}, bf16[1024,768]{1,0:T(8,128)(2,1)}, bf16[1024,768]{1,0:T(8,128)(2,1)}, bf16[1024,768]{1,0:T(8,128)(2,1)}, /*index=5*/f32[8,768]{1,0:T(8,128)}) custom-call(f32[12]{0:T(128)} %hs_ref.13, bf16[1024,768]{1,0:T(8,128)(2,1)} %get-tuple-element.256.gq_ref, ...), custom_call_target="tpu_custom_call" | custom-call | flops 483183820800 | bytes 4875878400 | tf_op jit(solution)/shard_map/cross_back/pallas_call | solution.py:384
  240.2 4.3 halve.14
  245.3 12.4 %wgrad.6 = (f32[16,24,3072]{2,1,0:T(8,128)}, f32[16,24,3072]{2,1,0:T(8,128)}) custom-call(s32[1]{0:T(128)S(6)} %and.10.core_ref, f32[8,128]{1,0:T(8,128)} %get-tuple-element.236.fac_ref, bf16[1024,768]{1,0:T(8,128)(2,1)} %get-tuple-element.270.refs_0_, bf16[1024,768]{1,0:T(8,128)(2,1)} %get-tuple-element.271.refs_1_, bf16[1024,768]{1,0:T(8,128)(2,1)} %bitcast.111, ...), custom_call_target="tpu_custom_call" | custom-call | flops 1932735283200 | bytes 4089446400 | tf_op jit(solution)/shard_map/wgrad/pallas_call | solution.py:499
  257.7 4.7 %halve.15 = (f32[4,1,24,3840]{3,2,1,0:T(8,128)}, f32[4,1,24,3840]{3,2,1,0:T(8,128)}) custom-call(s32[1]{0:T(128)} %bitcast.6.bit_ref, f32[4,2,1,24,3840]{4,3,2,1,0:T(8,128)} %bitcast.73, f32[4,2,1,24,3840]{4,3,2,1,0:T(8,128)} %bitcast.74, f32[4,2,1,24,3840]{4,3,2,1,0:T(8,128)} %bitcast.15.gm.go, f32[4,2,1,24,3840]{4,3,2,1,0:T(8,128)} %bitcast.15.gm.go), custom_call_target="tpu_custom_call" | custom-call | flops 200000 | bytes 200000 | tf_op jit(solution)/shard_map/halve/pallas_call | solution.py:513
  262.5 16.0 %attn_bwd.4 = (bf16[1024,768]{1,0:T(8,128)(2,1)}, bf16[1024,768]{1,0:T(8,128)(2,1)}, bf16[1024,768]{1,0:T(8,128)(2,1)}, f32[6,2,128]{2,1,0:T(2,128)}, f32[6,2,256]{2,1,0:T(2,128)}) custom-call(s32[1]{0:T(128)S(6)} %copy.90.limit_ref.dec_ref, f32[12]{0:T(128)} %hs_ref.13, f32[12,256]{1,0:T(8,128)} %bias_ref.9, bf16[1024,768]{1,0:T(8,128)(2,1)} %get-tuple-element.226.q_ref, ...), custom_call_target="tpu_custom_call" | custom-call | flops 805306368000 | bytes 1258291200 | tf_op jit(solution)/shard_map/attn_bwd/pallas_call | solution.py:201
  278.5 2.6 deal.6
  285.1 4.4 halve.16
  289.4 4.3 halve.17
  297.0 16.2 %attn_bwd.5 = (bf16[1024,768]{1,0:T(8,128)(2,1)}, bf16[1024,768]{1,0:T(8,128)(2,1)}, bf16[1024,768]{1,0:T(8,128)(2,1)}, f32[6,2,128]{2,1,0:T(2,128)}, f32[6,2,256]{2,1,0:T(2,128)}) custom-call(s32[1]{0:T(128)S(6)} %copy.90.limit_ref.dec_ref, f32[12]{0:T(128)} %hs_ref.13, ...), custom_call_target="tpu_custom_call", output_to_operand_aliasing={{0}: (9, {}), {1}: (10, {}), {2}: (11, {}), {3}: (12, {}), ... | custom-call | flops 805306368000 | bytes 1258291200 | tf_op jit(solution)/shard_map/attn_bwd/pallas_call | solution.py:201
  313.8 5.1 %self_norm.1 = (bf16[1024,768]{1,0:T(8,128)(2,1)}, bf16[1024,768]{1,0:T(8,128)(2,1)}, f32[8,768]{1,0:T(8,128)}) custom-call(bf16[1024,768]{1,0:T(8,128)(2,1)} %bitcast.114, bf16[1024,768]{1,0:T(8,128)(2,1)} %get-tuple-element.297.gq_ref, bf16[1024,768]{1,0:T(8,128)(2,1)} %get-tuple-element.298.gv_ref.refs_2_, f32[768]{0:T(1024)} %g_ref.5, f32[768]{0:T(1024)} %b_ref.3), custom_call_target="tpu_custom_call" | custom-call | flops 3145728000 | bytes 1572864000 | tf_op jit(solution)/shard_map/self_norm/pallas_call | solution.py:400
  318.9 2.9 deal.7
  322.4 3.4 collective-permute-start.14
  326.2 3.7 halve.18
  329.9 3.8 halve.19
  333.7 9.2 %wgrad.7 = (f32[16,24,2304]{2,1,0:T(8,128)}, f32[16,24,2304]{2,1,0:T(8,128)}) custom-call(s32[1]{0:T(128)S(6)} %and.10.core_ref, f32[8,128]{1,0:T(8,128)} %get-tuple-element.236.fac_ref, bf16[1024,768]{1,0:T(8,128)(2,1)} %get-tuple-element.317.refs_0_, bf16[1024,768]{1,0:T(8,128)(2,1)} %get-tuple-element.318.refs_1_.gq_ref, ...), custom_call_target="tpu_custom_call" | custom-call | flops 1449551462400 | bytes 2673868800 | tf_op jit(solution)/shard_map/wgrad/pallas_call | solution.py:499
  342.9 10.4 %tail.1 = (f32[1024,768]{1,0:T(8,128)}, f32[48,768]{1,0:T(8,128)}) custom-call(f32[8,128]{1,0:T(8,128)} %get-tuple-element.236.fac_ref, f32[12]{0:T(128)} %hs_ref.13, bf16[1024,768]{1,0:T(8,128)(2,1)} %bitcast.115, f32[1024,768]{1,0:T(8,128)} %get-tuple-element.321.gx1_ref, bf16[1024,768]{1,0:T(8,128)(2,1)} %get-tuple-element.318.refs_1_.gq_ref, ...), custom_call_target="tpu_custom_call" | custom-call | flops 1207959552000 | bytes 4954521600 | tf_op jit(solution)/shard_map/tail/pallas_call | solution.py:425
  354.7 4.1 halve.20
  358.8 4.1 halve.21
  366.2 6.9 %memory.1 = f32[1024,768]{1,0:T(8,128)} custom-call(bf16[1024,768]{1,0:T(8,128)(2,1)} %get-tuple-element.338.refs_4_.k_ref, bf16[1024,768]{1,0:T(8,128)(2,1)} %get-tuple-element.260.gv_ref.refs_3_.v_ref, bf16[768,768]{1,0:T(8,128)(2,1)} %ck.3, bf16[768,768]{1,0:T(8,128)(2,1)} %cv.3), custom_call_target="tpu_custom_call" | custom-call | flops 483183820800 | bytes 1730150400 | tf_op jit(solution)/shard_map/memory/pallas_call | solution.py:434
  374.8 2.2 deal.8
  376.9 2.6 collective-permute-done.18
  379.5 2.2 deal.9
  381.7 18.6 %collective-permute-done.17 = f32[48,768]{1,0:T(8,128)S(1)} collective-permute-done((f32[48,768]{1,0:T(8,128)S(1)}, f32[48,768]{1,0:T(8,128)S(1)}, u32[]{:S(2)}, u32[]{:S(2)}) %collective-permute-start.17) | collective-permute-done | bytes 147488 | tf_op jit(solution)/shard_map/ppermute | solution.py:541
  400.4 3.6 halve.22
  405.3 3.5 halve.23
  409.9 4.0 collective-permute-start.30
  415.4 3.1 collective-permute-done.20
  418.4 3.4 collective-permute-start.32
  421.9 2.6 collective-permute-start.23
  424.6 2.1 collective-permute-start.28
  426.7 2.3 collective-permute-start.29
  435.4 2.3 collective-permute-done.27.refs_9_
  438.0 3.0 collective-permute-start.38
  441.0 10.7 %collective-permute-start.33 = (f32[24,1152]{1,0:T(8,128)S(1)}, f32[24,1152]{1,0:T(8,128)S(1)}, u32[]{:S(2)}, u32[]{:S(2)}) collective-permute-start(f32[24,1152]{1,0:T(8,128)S(1)} %copy-done.25), channel_id=1, source_target_pairs={{0,8},{1,9},{2,10},{3,11},{4,12},{5,13},{6,14},{7,15},{8,0},{9,1},... | collective-permute-start | bytes 331784 | tf_op jit(solution)/shard_map/ppermute | solution.py:575
  453.5 4.3 collective-permute-start.35
  457.8 7.0 %collective-permute-done.34.refs_18_ = f32[24,1152]{1,0:T(8,128)S(1)} collective-permute-done((f32[24,1152]{1,0:T(8,128)S(1)}, f32[24,1152]{1,0:T(8,128)S(1)}, u32[]{:S(2)}, u32[]{:S(2)}) %collective-permute-start.34) | collective-permute-done | bytes 110624 | tf_op jit(solution)/shard_map/ppermute | solution.py:575
  466.1 3.3 finish.1
  (127 shorter events, 37.5 us)
Async XLA Ops:
  2.0 79.1 %all-to-all-start = ((f32[32,8,128]{2,1,0:T(8,128)}), f32[32,8,128]{2,1,0:T(8,128)}, u32[]{:S(2)}, u32[]{:S(2)}) async-start(f32[32,8,128]{2,1,0:T(8,128)} %broadcast_in_dim.17), calls=%async_computation | async-start | bytes 262144 | tf_op jit(solution)/shard_map/all_to_all | solution.py:592
  151.7 10.9 %collective-permute-start.1 = (f32[16,24,3840]{2,1,0:T(8,128)}, f32[16,24,3840]{2,1,0:T(8,128)}, u32[]{:S(2)}, u32[]{:S(2)}) collective-permute-start(f32[16,24,3840]{2,1,0:T(8,128)} %get-tuple-element.242), channel_id=1, source_target_pairs={{0,1},{1,0},{2,3},{3,2},{4,5},{5,4},{6,7},{7,6},{8,9},{9,8},{10,11... | collective-permute-start | bytes 17694728 | tf_op jit(solution)/shard_map/ppermute | solution.py:541
  162.3 9.1 %collective-permute-start = (f32[16,96,768]{2,1,0:T(8,128)}, f32[16,96,768]{2,1,0:T(8,128)}, u32[]{:S(2)}, u32[]{:S(2)}) collective-permute-start(f32[16,96,768]{2,1,0:T(8,128)} %get-tuple-element.246), channel_id=1, source_target_pairs={{0,1},{1,0},{2,3},{3,2},{4,5},{5,4},{6,7},{7,6},{8,9},{9,8},{10,11... | collective-permute-start | bytes 14155784 | tf_op jit(solution)/shard_map/ppermute | solution.py:541
  169.7 88.0 %collective-permute-start.2 = (f32[4,2,24,3840]{3,2,1,0:T(8,128)}, f32[4,2,24,3840]{3,2,1,0:T(8,128)}, u32[]{:S(2)}, u32[]{:S(2)}) collective-permute-start(f32[4,2,24,3840]{3,2,1,0:T(8,128)} %get-tuple-element.250), channel_id=1, source_target_pairs={{0,4},{1,5},{2,6},{3,7},{4,0},{5,1},{6,2},{7,3},{8,12},{9,13},{10,... | collective-permute-start | bytes 8847368 | tf_op jit(solution)/shard_map/ppermute | solution.py:541
  177.6 62.6 %collective-permute-start.3 = (f32[8,1,96,768]{3,2,1,0:T(8,128)}, f32[8,1,96,768]{3,2,1,0:T(8,128)}, u32[]{:S(2)}, u32[]{:S(2)}) collective-permute-start(f32[8,1,96,768]{3,2,1,0:T(8,128)} %get-tuple-element.253), channel_id=1, source_target_pairs={{0,2},{1,3},{2,0},{3,1},{4,6},{5,7},{6,4},{7,5},{8,10},{9,11},{10,... | collective-permute-start | bytes 7077896 | tf_op jit(solution)/shard_map/ppermute | solution.py:541
  244.5 34.0 %collective-permute-start.5 = (f32[4,1,96,768]{3,2,0,1:T(8,128)}, f32[4,1,96,768]{3,2,0,1:T(8,128)}, u32[]{:S(2)}, u32[]{:S(2)}) collective-permute-start(f32[4,1,96,768]{3,2,0,1:T(8,128)} %bitcast.117), channel_id=1, source_target_pairs={{0,4},{1,5},{2,6},{3,7},{4,0},{5,1},{6,2},{7,3},{8,12},{9,13},{10,... | collective-permute-start | bytes 3538952 | tf_op jit(solution)/shard_map/ppermute | solution.py:541
  257.7 27.4 %collective-permute-start.4 = (f32[16,24,3072]{2,1,0:T(8,128)}, f32[16,24,3072]{2,1,0:T(8,128)}, u32[]{:S(2)}, u32[]{:S(2)}) collective-permute-start(f32[16,24,3072]{2,1,0:T(8,128)} %get-tuple-element.274), channel_id=1, source_target_pairs={{0,1},{1,0},{2,3},{3,2},{4,5},{5,4},{6,7},{7,6},{8,9},{9,8},{10,11... | collective-permute-start | bytes 14155784 | tf_op jit(solution)/shard_map/ppermute | solution.py:541
  262.5 50.7 %collective-permute-start.6 = (f32[4,1,24,3840]{3,2,0,1:T(8,128)}, f32[4,1,24,3840]{3,2,0,1:T(8,128)}, u32[]{:S(2)}, u32[]{:S(2)}) collective-permute-start(f32[4,1,24,3840]{3,2,0,1:T(8,128)} %bitcast.116), channel_id=1, source_target_pairs={{0,2},{1,3},{2,0},{3,1},{4,6},{5,7},{6,4},{7,5},{8,10},{9,11},{10,... | collective-permute-start | bytes 4423688 | tf_op jit(solution)/shard_map/ppermute | solution.py:541
  281.1 40.6 %collective-permute-start.7 = (f32[96,768]{1,0:T(8,128)}, f32[96,768]{1,0:T(8,128)}, u32[]{:S(2)}, u32[]{:S(2)}) collective-permute-start(f32[96,768]{1,0:T(8,128)} %get-tuple-element.305), channel_id=1, source_target_pairs={{0,8},{1,9},{2,10},{3,11},{4,12},{5,13},{6,14},{7,15},{8,0},{9,1},... | collective-permute-start | bytes 884744 | tf_op jit(solution)/shard_map/ppermute | solution.py:575
  283.2 39.2 %collective-permute-start.8 = (f32[96,768]{1,0:T(8,128)}, f32[96,768]{1,0:T(8,128)}, u32[]{:S(2)}, u32[]{:S(2)}) collective-permute-start(f32[96,768]{1,0:T(8,128)} %get-tuple-element.306), channel_id=1, source_target_pairs={{0,16},{1,17},{2,18},{3,19},{4,20},{5,21},{6,22},{7,23},{8,24},{9,... | collective-permute-start | bytes 884744 | tf_op jit(solution)/shard_map/ppermute | solution.py:575
  293.8 32.4 %collective-permute-start.11 = (f32[4,2,24,1536]{3,2,1,0:T(8,128)}, f32[4,2,24,1536]{3,2,1,0:T(8,128)}, u32[]{:S(2)}, u32[]{:S(2)}) collective-permute-start(f32[4,2,24,1536]{3,2,1,0:T(8,128)} %get-tuple-element.291), channel_id=1, source_target_pairs={{0,4},{1,5},{2,6},{3,7},{4,0},{5,1},{6,2},{7,3},{8,12},{9,13},{10,... | collective-permute-start | bytes 3538952 | tf_op jit(solution)/shard_map/ppermute | solution.py:541
  295.0 31.2 %collective-permute-start.10 = (f32[8,1,24,1536]{3,2,1,0:T(8,128)}, f32[8,1,24,1536]{3,2,1,0:T(8,128)}, u32[]{:S(2)}, u32[]{:S(2)}) collective-permute-start(f32[8,1,24,1536]{3,2,1,0:T(8,128)} %get-tuple-element.288), channel_id=1, source_target_pairs={{0,2},{1,3},{2,0},{3,1},{4,6},{5,7},{6,4},{7,5},{8,10},{9,11},{10,... | collective-permute-start | bytes 3538952 | tf_op jit(solution)/shard_map/ppermute | solution.py:541
  313.2 12.5 %collective-permute-start.9 = (f32[96,768]{1,0:T(8,128)S(1)}, f32[96,768]{1,0:T(8,128)S(1)}, u32[]{:S(2)}, u32[]{:S(2)}) collective-permute-start(f32[96,768]{1,0:T(8,128)S(1)} %copy-done.16), channel_id=1, source_target_pairs={{0,24},{1,25},{2,26},{3,27},{4,28},{5,29},{6,30},{7,31},{8,16},{9,... | collective-permute-start | bytes 884744 | tf_op jit(solution)/shard_map/ppermute | solution.py:575
  321.8 41.1 %collective-permute-start.13 = (f32[24,3840]{1,0:T(8,128)}, f32[24,3840]{1,0:T(8,128)}, u32[]{:S(2)}, u32[]{:S(2)}) collective-permute-start(f32[24,3840]{1,0:T(8,128)} %get-tuple-element.335), channel_id=1, source_target_pairs={{0,8},{1,9},{2,10},{3,11},{4,12},{5,13},{6,14},{7,15},{8,0},{9,1},... | collective-permute-start | bytes 1105928 | tf_op jit(solution)/shard_map/ppermute | solution.py:575
  322.4 40.6 %collective-permute-start.14 = (f32[24,3840]{1,0:T(8,128)}, f32[24,3840]{1,0:T(8,128)}, u32[]{:S(2)}, u32[]{:S(2)}) collective-permute-start(f32[24,3840]{1,0:T(8,128)} %get-tuple-element.336), channel_id=1, source_target_pairs={{0,16},{1,17},{2,18},{3,19},{4,20},{5,21},{6,22},{7,23},{8,24},{9,... | collective-permute-start | bytes 1105928 | tf_op jit(solution)/shard_map/ppermute | solution.py:575
  325.7 39.3 %collective-permute-start.15 = (f32[24,3840]{1,0:T(8,128)}, f32[24,3840]{1,0:T(8,128)}, u32[]{:S(2)}, u32[]{:S(2)}) collective-permute-start(f32[24,3840]{1,0:T(8,128)} %get-tuple-element.337), channel_id=1, source_target_pairs={{0,24},{1,25},{2,26},{3,27},{4,28},{5,29},{6,30},{7,31},{8,16},{9,... | collective-permute-start | bytes 1105928 | tf_op jit(solution)/shard_map/ppermute | solution.py:575
  342.9 10.9 %collective-permute-start.12 = (f32[16,24,2304]{2,1,0:T(8,128)}, f32[16,24,2304]{2,1,0:T(8,128)}, u32[]{:S(2)}, u32[]{:S(2)}) collective-permute-start(f32[16,24,2304]{2,1,0:T(8,128)} %get-tuple-element.320), channel_id=1, source_target_pairs={{0,1},{1,0},{2,3},{3,2},{4,5},{5,4},{6,7},{7,6},{8,9},{9,8},{10,11... | collective-permute-start | bytes 10616840 | tf_op jit(solution)/shard_map/ppermute | solution.py:541
  353.3 19.9 %collective-permute-start.16 = (f32[48,768]{1,0:T(8,128)}, f32[48,768]{1,0:T(8,128)}, u32[]{:S(2)}, u32[]{:S(2)}) collective-permute-start(f32[48,768]{1,0:T(8,128)} %get-tuple-element.339), channel_id=1, source_target_pairs={{0,1},{1,0},{2,3},{3,2},{4,5},{5,4},{6,7},{7,6},{8,9},{9,8},{10,11... | collective-permute-start | bytes 442376 | tf_op jit(solution)/shard_map/ppermute | solution.py:541
  353.9 20.9 %collective-permute-start.19 = (f32[4,1,24,1536]{3,2,0,1:T(8,128)}, f32[4,1,24,1536]{3,2,0,1:T(8,128)}, u32[]{:S(2)}, u32[]{:S(2)}) collective-permute-start(f32[4,1,24,1536]{3,2,0,1:T(8,128)} %bitcast.38), channel_id=1, source_target_pairs={{0,4},{1,5},{2,6},{3,7},{4,0},{5,1},{6,2},{7,3},{8,12},{9,13},{10,... | collective-permute-start | bytes 1769480 | tf_op jit(solution)/shard_map/ppermute | solution.py:541
  362.9 16.6 %collective-permute-start.18 = (f32[4,1,24,1536]{3,2,0,1:T(8,128)}, f32[4,1,24,1536]{3,2,0,1:T(8,128)}, u32[]{:S(2)}, u32[]{:S(2)}) collective-permute-start(f32[4,1,24,1536]{3,2,0,1:T(8,128)} %bitcast.37), channel_id=1, source_target_pairs={{0,2},{1,3},{2,0},{3,1},{4,6},{5,7},{6,4},{7,5},{8,10},{9,11},{10,... | collective-permute-start | bytes 1769480 | tf_op jit(solution)/shard_map/ppermute | solution.py:541
  363.0 37.4 %collective-permute-start.22 = (f32[8,1,24,1152]{3,2,1,0:T(8,128)}, f32[8,1,24,1152]{3,2,1,0:T(8,128)}, u32[]{:S(2)}, u32[]{:S(2)}) collective-permute-start(f32[8,1,24,1152]{3,2,1,0:T(8,128)} %get-tuple-element.331), channel_id=1, source_target_pairs={{0,2},{1,3},{2,0},{3,1},{4,6},{5,7},{6,4},{7,5},{8,10},{9,11},{10,... | collective-permute-start | bytes 2654216 | tf_op jit(solution)/shard_map/ppermute | solution.py:541
  365.0 39.0 %collective-permute-start.21 = (f32[4,2,24,1152]{3,2,1,0:T(8,128)}, f32[4,2,24,1152]{3,2,1,0:T(8,128)}, u32[]{:S(2)}, u32[]{:S(2)}) collective-permute-start(f32[4,2,24,1152]{3,2,1,0:T(8,128)} %get-tuple-element.334), channel_id=1, source_target_pairs={{0,4},{1,5},{2,6},{3,7},{4,0},{5,1},{6,2},{7,3},{8,12},{9,13},{10,... | collective-permute-start | bytes 2654216 | tf_op jit(solution)/shard_map/ppermute | solution.py:541
  374.1 26.2 %collective-permute-start.17 = (f32[48,768]{1,0:T(8,128)S(1)}, f32[48,768]{1,0:T(8,128)S(1)}, u32[]{:S(2)}, u32[]{:S(2)}) collective-permute-start(f32[48,768]{1,0:T(8,128)S(1)} %add.15), channel_id=1, source_target_pairs={{0,2},{1,3},{2,0},{3,1},{4,6},{5,7},{6,4},{7,5},{8,10},{9,11},{10,... | collective-permute-start | bytes 442376 | tf_op jit(solution)/shard_map/ppermute | solution.py:541
  404.0 22.7 %copy-start.17 = (f32[24,1536]{1,0:T(8,128)S(1)}, f32[24,1536]{1,0:T(8,128)}, u32[]{:S(2)}) copy-start(f32[24,1536]{1,0:T(8,128)} %get-tuple-element.377) | copy-start | bytes 442372
  404.0 20.5 %collective-permute-start.25 = (f32[4,1,24,1152]{3,2,0,1:T(8,128)}, f32[4,1,24,1152]{3,2,0,1:T(8,128)S(1)}, u32[]{:S(2)}, u32[]{:S(2)}) collective-permute-start(f32[4,1,24,1152]{3,2,0,1:T(8,128)} %bitcast.118), channel_id=1, source_target_pairs={{0,4},{1,5},{2,6},{3,7},{4,0},{5,1},{6,2},{7,3},{8,12},{9,13},{10,... | collective-permute-start | bytes 1327112 | tf_op jit(solution)/shard_map/ppermute | solution.py:541
  408.9 17.8 %collective-permute-start.24 = (f32[4,1,24,1152]{3,2,0,1:T(8,128)}, f32[4,1,24,1152]{3,2,0,1:T(8,128)S(1)}, u32[]{:S(2)}, u32[]{:S(2)}) collective-permute-start(f32[4,1,24,1152]{3,2,0,1:T(8,128)} %bitcast.119), channel_id=1, source_target_pairs={{0,2},{1,3},{2,0},{3,1},{4,6},{5,7},{6,4},{7,5},{8,10},{9,11},{10,... | collective-permute-start | bytes 1327112 | tf_op jit(solution)/shard_map/ppermute | solution.py:541
  409.4 9.0 %collective-permute-start.20 = (f32[48,768]{1,0:T(8,128)S(1)}, f32[48,768]{1,0:T(8,128)S(1)}, u32[]{:S(2)}, u32[]{:S(2)}) collective-permute-start(f32[48,768]{1,0:T(8,128)S(1)} %add.16), channel_id=1, source_target_pairs={{0,4},{1,5},{2,6},{3,7},{4,0},{5,1},{6,2},{7,3},{8,12},{9,13},{10,... | collective-permute-start | bytes 442376 | tf_op jit(solution)/shard_map/ppermute | solution.py:541
  409.9 11.9 %collective-permute-start.30 = (f32[24,1536]{1,0:T(8,128)S(1)}, f32[24,1536]{1,0:T(8,128)S(1)}, u32[]{:S(2)}, u32[]{:S(2)}) collective-permute-start(f32[24,1536]{1,0:T(8,128)S(1)} %copy-done.22), channel_id=1, source_target_pairs={{0,8},{1,9},{2,10},{3,11},{4,12},{5,13},{6,14},{7,15},{8,0},{9,1},... | collective-permute-start | bytes 442376 | tf_op jit(solution)/shard_map/ppermute | solution.py:575
  413.9 10.5 %collective-permute-start.31 = (f32[24,1536]{1,0:T(8,128)S(1)}, f32[24,1536]{1,0:T(8,128)S(1)}, u32[]{:S(2)}, u32[]{:S(2)}) collective-permute-start(f32[24,1536]{1,0:T(8,128)S(1)} %copy-done.21), channel_id=1, source_target_pairs={{0,16},{1,17},{2,18},{3,19},{4,20},{5,21},{6,22},{7,23},{8,24},{9,... | collective-permute-start | bytes 442376 | tf_op jit(solution)/shard_map/ppermute | solution.py:575
  418.4 14.7 %collective-permute-start.32 = (f32[24,1536]{1,0:T(8,128)S(1)}, f32[24,1536]{1,0:T(8,128)S(1)}, u32[]{:S(2)}, u32[]{:S(2)}) collective-permute-start(f32[24,1536]{1,0:T(8,128)S(1)} %copy-done.20), channel_id=1, source_target_pairs={{0,24},{1,25},{2,26},{3,27},{4,28},{5,29},{6,30},{7,31},{8,16},{9,... | collective-permute-start | bytes 442376 | tf_op jit(solution)/shard_map/ppermute | solution.py:575
  421.8 43.0 %copy-start.3 = (f32[24,1536]{1,0:T(8,128)}, f32[24,1536]{1,0:T(8,128)S(1)}, u32[]{:S(2)}) copy-start(f32[24,1536]{1,0:T(8,128)S(1)} %collective-permute-done.30.refs_13_) | copy-start | bytes 442372
  421.9 11.4 %collective-permute-start.23 = (f32[48,768]{1,0:T(8,128)S(1)}, f32[48,768]{1,0:T(8,128)S(1)}, u32[]{:S(2)}, u32[]{:S(2)}) collective-permute-start(f32[48,768]{1,0:T(8,128)S(1)} %add.17), channel_id=1, source_target_pairs={{0,8},{1,9},{2,10},{3,11},{4,12},{5,13},{6,14},{7,15},{8,0},{9,1},... | collective-permute-start | bytes 442376 | tf_op jit(solution)/shard_map/ppermute | solution.py:541
  424.4 40.4 %copy-start.4 = (f32[24,1536]{1,0:T(8,128)}, f32[24,1536]{1,0:T(8,128)S(1)}, u32[]{:S(2)}) copy-start(f32[24,1536]{1,0:T(8,128)S(1)} %collective-permute-done.31.refs_14_) | copy-start | bytes 442372
  424.4 13.2 %collective-permute-start.27 = (f32[24,1536]{1,0:T(8,128)S(1)}, f32[24,1536]{1,0:T(8,128)S(1)}, u32[]{:S(2)}, u32[]{:S(2)}) collective-permute-start(f32[24,1536]{1,0:T(8,128)S(1)} %copy-done.19), channel_id=1, source_target_pairs={{0,8},{1,9},{2,10},{3,11},{4,12},{5,13},{6,14},{7,15},{8,0},{9,1},... | collective-permute-start | bytes 442376 | tf_op jit(solution)/shard_map/ppermute | solution.py:575
  424.6 13.4 %collective-permute-start.28 = (f32[24,1536]{1,0:T(8,128)S(1)}, f32[24,1536]{1,0:T(8,128)S(1)}, u32[]{:S(2)}, u32[]{:S(2)}) collective-permute-start(f32[24,1536]{1,0:T(8,128)S(1)} %copy-done.18), channel_id=1, source_target_pairs={{0,16},{1,17},{2,18},{3,19},{4,20},{5,21},{6,22},{7,23},{8,24},{9,... | collective-permute-start | bytes 442376 | tf_op jit(solution)/shard_map/ppermute | solution.py:575
  426.7 14.3 %collective-permute-start.29 = (f32[24,1536]{1,0:T(8,128)S(1)}, f32[24,1536]{1,0:T(8,128)S(1)}, u32[]{:S(2)}, u32[]{:S(2)}) collective-permute-start(f32[24,1536]{1,0:T(8,128)S(1)} %copy-done.17), channel_id=1, source_target_pairs={{0,24},{1,25},{2,26},{3,27},{4,28},{5,29},{6,30},{7,31},{8,16},{9,... | collective-permute-start | bytes 442376 | tf_op jit(solution)/shard_map/ppermute | solution.py:575
  431.1 22.4 %copy-start.23 = (f32[24,1152]{1,0:T(8,128)S(1)}, f32[24,1152]{1,0:T(8,128)}, u32[]{:S(2)}) copy-start(f32[24,1152]{1,0:T(8,128)} %get-tuple-element.383) | copy-start | bytes 331780
  433.2 31.7 %copy-start.5 = (f32[24,1536]{1,0:T(8,128)}, f32[24,1536]{1,0:T(8,128)S(1)}, u32[]{:S(2)}) copy-start(f32[24,1536]{1,0:T(8,128)S(1)} %collective-permute-done.32.refs_15_) | copy-start | bytes 442372
  433.2 18.5 %collective-permute-start.36 = (f32[24,1152]{1,0:T(8,128)}, f32[24,1152]{1,0:T(8,128)S(1)}, u32[]{:S(2)}, u32[]{:S(2)}) collective-permute-start(f32[24,1152]{1,0:T(8,128)} %get-tuple-element.384), channel_id=1, source_target_pairs={{0,8},{1,9},{2,10},{3,11},{4,12},{5,13},{6,14},{7,15},{8,0},{9,1},... | collective-permute-start | bytes 331784 | tf_op jit(solution)/shard_map/ppermute | solution.py:575
  433.2 20.2 %collective-permute-start.37 = (f32[24,1152]{1,0:T(8,128)}, f32[24,1152]{1,0:T(8,128)S(1)}, u32[]{:S(2)}, u32[]{:S(2)}) collective-permute-start(f32[24,1152]{1,0:T(8,128)} %get-tuple-element.385), channel_id=1, source_target_pairs={{0,16},{1,17},{2,18},{3,19},{4,20},{5,21},{6,22},{7,23},{8,24},{9,... | collective-permute-start | bytes 331784 | tf_op jit(solution)/shard_map/ppermute | solution.py:575
  437.6 27.2 %copy-start.6 = (f32[24,1536]{1,0:T(8,128)}, f32[24,1536]{1,0:T(8,128)S(1)}, u32[]{:S(2)}) copy-start(f32[24,1536]{1,0:T(8,128)S(1)} %collective-permute-done.27.refs_9_) | copy-start | bytes 442372
  437.6 31.8 %collective-permute-start.26 = (f32[48,768]{1,0:T(8,128)S(1)}, f32[48,768]{1,0:T(8,128)S(1)}, u32[]{:S(2)}, u32[]{:S(2)}) collective-permute-start(f32[48,768]{1,0:T(8,128)S(1)} %add.18), channel_id=1, source_target_pairs={{0,16},{1,17},{2,18},{3,19},{4,20},{5,21},{6,22},{7,23},{8,24},{9,... | collective-permute-start | bytes 442376 | tf_op jit(solution)/shard_map/ppermute | solution.py:541
  438.0 26.9 %copy-start.7 = (f32[24,1536]{1,0:T(8,128)}, f32[24,1536]{1,0:T(8,128)S(1)}, u32[]{:S(2)}) copy-start(f32[24,1536]{1,0:T(8,128)S(1)} %collective-permute-done.28.refs_10_) | copy-start | bytes 442372
  438.0 19.8 %collective-permute-start.38 = (f32[24,1152]{1,0:T(8,128)}, f32[24,1152]{1,0:T(8,128)S(1)}, u32[]{:S(2)}, u32[]{:S(2)}) collective-permute-start(f32[24,1152]{1,0:T(8,128)} %get-tuple-element.386), channel_id=1, source_target_pairs={{0,24},{1,25},{2,26},{3,27},{4,28},{5,29},{6,30},{7,31},{8,16},{9,... | collective-permute-start | bytes 331784 | tf_op jit(solution)/shard_map/ppermute | solution.py:575
  441.0 23.9 %copy-start.8 = (f32[24,1536]{1,0:T(8,128)}, f32[24,1536]{1,0:T(8,128)S(1)}, u32[]{:S(2)}) copy-start(f32[24,1536]{1,0:T(8,128)S(1)} %collective-permute-done.29.refs_11_) | copy-start | bytes 442372
  441.0 16.8 %collective-permute-start.33 = (f32[24,1152]{1,0:T(8,128)S(1)}, f32[24,1152]{1,0:T(8,128)S(1)}, u32[]{:S(2)}, u32[]{:S(2)}) collective-permute-start(f32[24,1152]{1,0:T(8,128)S(1)} %copy-done.25), channel_id=1, source_target_pairs={{0,8},{1,9},{2,10},{3,11},{4,12},{5,13},{6,14},{7,15},{8,0},{9,1},... | collective-permute-start | bytes 331784 | tf_op jit(solution)/shard_map/ppermute | solution.py:575
  451.7 13.2 %collective-permute-start.34 = (f32[24,1152]{1,0:T(8,128)S(1)}, f32[24,1152]{1,0:T(8,128)S(1)}, u32[]{:S(2)}, u32[]{:S(2)}) collective-permute-start(f32[24,1152]{1,0:T(8,128)S(1)} %copy-done.24), channel_id=1, source_target_pairs={{0,16},{1,17},{2,18},{3,19},{4,20},{5,21},{6,22},{7,23},{8,24},{9,... | collective-permute-start | bytes 331784 | tf_op jit(solution)/shard_map/ppermute | solution.py:575
  453.5 11.3 %collective-permute-start.35 = (f32[24,1152]{1,0:T(8,128)S(1)}, f32[24,1152]{1,0:T(8,128)S(1)}, u32[]{:S(2)}, u32[]{:S(2)}) collective-permute-start(f32[24,1152]{1,0:T(8,128)S(1)} %copy-done.23), channel_id=1, source_target_pairs={{0,24},{1,25},{2,26},{3,27},{4,28},{5,29},{6,30},{7,31},{8,16},{9,... | collective-permute-start | bytes 331784 | tf_op jit(solution)/shard_map/ppermute | solution.py:575
  (18 other events, 178.5 us)
where the time goes:
time: 482 us; the launch traced here: 473 us
  Pallas kernels  362 us (75%)
  starting transfers between devices  69.4 us (14%)
  waiting for transfers between devices  34.1 us (7%)
    pallas_call x3, Pallas kernels, attn_bwd(): pl.pallas_call(functools.partial(bwd_kernel, causal, p0, before is not No...  81.7 us
    pallas_call x1, Pallas kernels, mid(): pl.pallas_call(functools.partial(mid_kernel, n), grid=(S // T,), in_specs...  57 us
    pallas_call x12, Pallas kernels, halve(): pl.pallas_call(halve_kernel, grid_spec=gs, out_shape=[sh, sh], compiler_p...  53.8 us
    pallas_call x2, Pallas kernels, attn_fwd(): pl.pallas_call(functools.partial(fwd_kernel, causal), grid_spec=grid_spec...  49.7 us
    ppermute x18, starting transfers between devices, last_step(): lax.ppermute(s, 'dp', [(j, j ^ m + 1 << zs[0]) for j in range(n)])  44.1 us
    pallas_call x3, Pallas kernels, wgrad_cols(): pl.pallas_call(functools.partial(wcol_kernel, plan), grid=(at,), in_specs...  35.3 us
    ppermute x21, waiting for transfers between devices, swap(): return lax.ppermute(x, 'dp', [(j, j ^ 1 << bit) for j in range(n)])  24.4 us
    ppermute x21, starting transfers between devices, swap(): return lax.ppermute(x, 'dp', [(j, j ^ 1 << bit) for j in range(n)])  18 us
  transfers between devices with their start and end apart: 40, of which 7 were waited for; matrix products, arithmetic and copies ran while one was open for 0% of the time, Pallas kernels for 61%

commit v1 on v0

--- a/solution.py
+++ b/solution.py
@@ -57,29 +57,38 @@
             qq=lax.broadcasted_iota(jnp.int32,(TILE,512),1)
             t_scr[h]=jnp.where(qq>=kk,t,NEG)
     nq=S//TILE; nk=M//TILE
-    for i in range(nq):
+    def soft(i,h):
+        b=i%2
         qs=slice(i*TILE,(i+1)*TILE)
+        tiles=range(i+1) if causal else range(nk)
+        m=None
+        for j in tiles:
+            s=nt(km[h,j*TILE:(j+1)*TILE],qm[h,qs])
+            if causal and j==i: s=s+t_scr[h,:,0:256]
+            if causal and j==i-1: s=s+t_scr[h,:,256:512]
+            s_scr[b,h,j*TILE:(j+1)*TILE]=s
+            mj=jnp.max(s,axis=0,keepdims=True)
+            m=mj if m is None else jnp.maximum(m,mj)
+        m2=m*LOG2E
+        for j in tiles:
+            p_scr[b,h,j*TILE:(j+1)*TILE]=jnp.exp2(s_scr[b,h,j*TILE:(j+1)*TILE]*LOG2E-m2).astype(BF)
+        return m2
+    def mix(i,ms):
+        b=i%2
+        qs=slice(i*TILE,(i+1)*TILE)
+        n=(i+1 if causal else nk)*TILE
         accs=[]
         for h in range(2):
-            tiles=range(i+1) if causal else range(nk)
-            m=None
-            for j in tiles:
-                s=nt(km[h,j*TILE:(j+1)*TILE],qm[h,qs])
-                if causal and j==i: s=s+t_scr[h,:,0:256]
-                if causal and j==i-1: s=s+t_scr[h,:,256:512]
-                s_scr[h,j*TILE:(j+1)*TILE]=s
-                mj=jnp.max(s,axis=0,keepdims=True)
-                m=mj if m is None else jnp.maximum(m,mj)
-            m2=m*LOG2E
-            n=len(tiles)*TILE
-            for j in tiles:
-                p_scr[h,j*TILE:(j+1)*TILE]=jnp.exp2(s_scr[h,j*TILE:(j+1)*TILE]*LOG2E-m2).astype(BF)
-            acc=nn(vt[h,:,0:n],p_scr[h,0:n])
+            acc=nn(vt[h,:,0:n],p_scr[b,h,0:n])
             l=acc[64:65]
-            lse_ref[0,h:h+1,qs]=m2+jnp.log2(l)
+            lse_ref[0,h:h+1,qs]=ms[h]+jnp.log2(l)
             accs.append(acc[0:64]*((hs_ref[2*pl.program_id(0)+h] if causal else 1.0)/l))
-        ot=jnp.concatenate(accs,axis=0)
-        o_ref[qs]=ot.T.astype(BF)
+        o_ref[qs]=jnp.concatenate(accs,axis=0).T.astype(BF)
+    ms=None
+    for i in range(nq+1):
+        new=[soft(i,h) for h in range(2)] if i<nq else None
+        if i>0: mix(i-1,ms)
+        ms=new
 
 def attn_fwd(causal, limit, hs, bias, q, k, v):
     S,D=q.shape; M=k.shape[0]
@@ -94,7 +103,7 @@
         out_specs=[pl.BlockSpec((S,128),lambda p,*_:(0,p)),
                    pl.BlockSpec((1,2,S),lambda p,*_:(p,0,0))],
         scratch_shapes=[pltpu.VMEM((2,M,128),BF),pltpu.VMEM((2,S,128),BF),pltpu.VMEM((2,80,M),BF),
-                        pltpu.VMEM((2,M,TILE),F32),pltpu.VMEM((2,M,TILE),BF),pltpu.VMEM((2,TILE,512),F32)])
+                        pltpu.VMEM((2,2,M,TILE),F32),pltpu.VMEM((2,2,M,TILE),BF),pltpu.VMEM((2,TILE,512),F32)])
     return pl.pallas_call(functools.partial(fwd_kernel,causal),grid_spec=grid_spec,
         out_shape=(jax.ShapeDtypeStruct((S,D),BF),jax.ShapeDtypeStruct((pairs,2,S),F32)),
         compiler_params=params(1),name="attn_fwd",
@@ -136,37 +145,37 @@
     if causal:
         d_scr[...]=jnp.zeros_like(d_scr); far[...]=jnp.zeros_like(far)
     gqt[...]=jnp.zeros_like(gqt)
-    def block(j):
+    def scores(j,h):
+        b=j%2
         js=slice(j*TILE,(j+1)*TILE)
-        i0=j if causal else 0
+        for i in range(j if causal else 0,nq):
+            qs=slice(i*TILE,(i+1)*TILE)
+            s=nt(km[h,js],qm[h,qs])*LOG2E
+            if causal and i-j<2:
+                s=s+t_scr[h,:,(i-j)*TILE:(i-j+1)*TILE]
+            p=jnp.exp2(s-lse_ref[0,h:h+1,qs])
+            gs=p*(nt(vm[h,js],go_ref[qs])-dl[h:h+1,qs])
+            p_scr[b,h,:,qs]=p.astype(BF)
+            gs_scr[b,h,:,qs]=gs.astype(BF)
+            if causal:
+                if i-j<2:
+                    d_scr[h,:,(i-j)*TILE:(i-j+1)*TILE]+=gs
+                else:
+                    far[h]+=jnp.sum(gs.reshape(TILE//8,8,TILE),axis=0)
+    def products(j,h):
+        b=j%2
+        js=slice(j*TILE,(j+1)*TILE)
+        a=j*TILE if causal else 0
+        if h==0:
+            gv_ref[js]=(nn(p_scr[b,0,:,a:],gom[0,a:])+nn(p_scr[b,1,:,a:],gom[1,a:])).astype(BF)
+            gqt[0:64,a:]+=nn(kt[0:64,js],gs_scr[b,0,:,a:])
+        else:
+            gk_ref[js]=(nn(gs_scr[b,0,:,a:],q0[0,a:])+nn(gs_scr[b,1,:,a:],q0[1,a:])).astype(BF)
+            gqt[64:128,a:]+=nn(kt[64:128,js],gs_scr[b,1,:,a:])
+    for j in range(nk+1):
         for h in range(2):
-            for i in range(i0,nq):
-                qs=slice(i*TILE,(i+1)*TILE)
-                s=nt(km[h,js],qm[h,qs])*LOG2E
-                if causal and i-j<2:
-                    s=s+t_scr[h,:,(i-j)*TILE:(i-j+1)*TILE]
-                p=jnp.exp2(s-lse_ref[0,h:h+1,qs])
-                gs=p*(nt(vm[h,js],go_ref[qs])-dl[h:h+1,qs])
-                p_scr[h,:,qs]=p.astype(BF)
-                gs_scr[h,:,qs]=gs.astype(BF)
-                if causal:
-                    if i-j<2:
-                        d_scr[h,:,(i-j)*TILE:(i-j+1)*TILE]+=gs
-                    else:
-                        far[h]+=jnp.sum(gs.reshape(TILE//8,8,TILE),axis=0)
-            gqt[h*64:(h+1)*64,i0*TILE:]+=nn(kt[h*64:(h+1)*64,js],gs_scr[h,:,i0*TILE:])
-        gv_ref[js]=(nn(p_scr[0,:,i0*TILE:],gom[0,i0*TILE:])+nn(p_scr[1,:,i0*TILE:],gom[1,i0*TILE:])).astype(BF)
-        gk_ref[js]=(nn(gs_scr[0,:,i0*TILE:],q0[0,i0*TILE:])+nn(gs_scr[1,:,i0*TILE:],q0[1,i0*TILE:])).astype(BF)
-    for j in range(nk):
-        if causal:
-            block(j)
-        else:
-            @pl.when(j*TILE<limit)
-            def _(): block(j)
-            @pl.when(j*TILE>=limit)
-            def _():
-                gv_ref[j*TILE:(j+1)*TILE]=jnp.zeros((TILE,128),BF)
-                gk_ref[j*TILE:(j+1)*TILE]=jnp.zeros((TILE,128),BF)
+            if j<nk: scores(j,h)
+            if j>0: products(j-1,h)
     gq_ref[...]=gqt[...].T.astype(BF)
     if causal:
         for h in range(2):
@@ -188,7 +197,7 @@
     outs=[col,colm,colm,pl.BlockSpec((1,2,128),lambda p,*_:(p+p0,0,0))]
     shapes=[jax.ShapeDtypeStruct((S,D),BF),jax.ShapeDtypeStruct((M,D),BF),jax.ShapeDtypeStruct((M,D),BF),jax.ShapeDtypeStruct((pairs,2,128),F32)]
     scr=[pltpu.VMEM((2,M,128),BF),pltpu.VMEM((2,S,128),BF),pltpu.VMEM((2,S,128),BF),pltpu.VMEM((2,M,128),BF),pltpu.VMEM((2,S,128),BF),
-         pltpu.VMEM((128,M),BF),pltpu.VMEM((2,TILE,S),BF),pltpu.VMEM((2,TILE,S),BF),pltpu.VMEM((128,S),F32),pltpu.VMEM((8,S),F32)]
+         pltpu.VMEM((128,M),BF),pltpu.VMEM((2,2,TILE,S),BF),pltpu.VMEM((2,2,TILE,S),BF),pltpu.VMEM((128,S),F32),pltpu.VMEM((8,S),F32)]
     if causal:
         outs.append(pl.BlockSpec((1,2,256),lambda p,*_:(p+p0,0,0))); shapes.append(jax.ShapeDtypeStruct((pairs,2,256),F32))
         scr+=[pltpu.VMEM((2,TILE,512),F32),pltpu.VMEM((2,TILE,512),F32),pltpu.VMEM((2,8,TILE),F32)]
@@ -309,7 +318,6 @@
     for c in range(0,FF,CH):
         cs=slice(c,c+CH)
         n=(ge[:,cs]-mean)*inv
-        ge[:,cs]=n
         u_o[:,cs]=(n*mg_v[:,cs]+mb_v[:,cs]).astype(BF)
         gu=nt(g3b,wout[cs,:])
         en=gu*n
@@ -323,9 +331,10 @@
     m1=jnp.sum(s1,axis=1,keepdims=True)*(1.0/FF); m2=jnp.sum(s2,axis=1,keepdims=True)*(1.0/FF)
     out=x2+(nn(u_o[...],wout[...])+vec(bo))
     lo_o[...]=jnp.where(valid,out,0.0).astype(BF)
+    slope=inv*m2; level=m1-mean*slope
     for c in range(0,FF,CH):
         cs=slice(c,c+CH)
-        gf=((gus[:,cs]-m1-ge[:,cs]*m2)*inv*dg[:,cs]).astype(BF)
+        gf=((gus[:,cs]-level-ge[:,cs]*slope)*inv*dg[:,cs]).astype(BF)
         gf_o[:,cs]=gf
         v3_o[2:3,cs]+=col_sum(gf.astype(F32))
     gh=nt(gf_o[...],wi[...])
@@ -386,74 +395,67 @@
         out_shape=[sd((S,D),F32)]+[sd((S,D),BF)]*4+[sd((8,D),F32)],
         compiler_params=params(1),name="cross_back",cost_estimate=cost(4*S*D*D,4*D*D+28*S*D))(hs,gq,x1,gx2,n,inv,gv,cwq,wo,cng,cnb,spg)
 
-def self_norm_kernel(x_ref,gq_ref,gv_ref,g_ref,b_ref,h_o,gqs_o,v_o):
-    @pl.when(pl.program_id(0)==0)
-    def _(): v_o[...]=jnp.zeros_like(v_o)
-    n,_=norm_rows(x_ref[...].astype(F32))
-    h_o[...]=(n*vec(g_ref)+vec(b_ref)).astype(BF)
+PLACE=(15,16,13,14,12,10,11,6,7,8,9,5,3,4,0,1,2)
+WIDE_ROW=17; BUCKET_LANE=32; HEAD_LANE=64
+def tail_kernel(n,core_ref,fac_ref,hs_ref,x_ref,gx1_ref,gq_ref,gk_ref,gv_ref,wq,wk,wv,g_ref,b_ref,va,vb,vf,gb,ds,
+                gt_o,h_o,gqs_o,keep_o,send_o,v_s,f_s,p_s,t_s):
+    D=x_ref.shape[1]; H=hs_ref.shape[0]; FF=vf.shape[1]
+    step=pl.program_id(0)
+    @pl.when(step==0)
+    def _():
+        v_s[...]=jnp.zeros_like(v_s); f_s[...]=jnp.zeros_like(f_s); p_s[...]=jnp.zeros_like(p_s)
+        v_s[0:6,0:D]=va[0:6]
+        v_s[6:13,0:D]=vb[0:7]
+        f_s[1:4,0:FF]=vf[0:3]
+        for h in range(H): p_s[h:h+1]=gb[h//2,h%2:h%2+1,:]
+    n_x,inv=norm_rows(x_ref[...].astype(F32))
+    h_o[...]=(n_x*vec(g_ref)+vec(b_ref)).astype(BF)
     gq=gq_ref[...]*jnp.asarray(0.125,BF)
     gqs_o[...]=gq
-    v_o[0:1]+=col_sum(gq.astype(F32)); v_o[1:2]+=col_sum(gv_ref[...].astype(F32))
-def self_norm(x,gq,gv,g,b,T=256):
-    S,D=x.shape
-    r=rows_of(T,D); u=whole((D,)); sd=jax.ShapeDtypeStruct
-    return pl.pallas_call(self_norm_kernel,grid=(S//T,),in_specs=[r,r,r,u,u],out_specs=[r,r,pl.BlockSpec((8,D),lambda *_:(0,0))],
-        out_shape=[sd((S,D),BF)]*2+[sd((8,D),F32)],compiler_params=params(1),name="self_norm",cost_estimate=cost(S*D*20,S*D*10))(x,gq,gv,g,b)
-
-def tail_kernel(fac_ref,hs_ref,x_ref,gx1_ref,gq_ref,gk_ref,gv_ref,wq,wk,wv,g_ref,va,vb,vc,vf,gb,ds,gt_o,v_o):
-    D=x_ref.shape[1]; H=hs_ref.shape[0]
-    fac=fac_ref[0:1,0:1]
-    @pl.when(pl.program_id(0)==0)
+    gh=nt(gq,wq[...])+nt(gk_ref[...],wk[...])+nt(gv_ref[...],wv[...])
+    v_s[13:14,0:D]+=col_sum(gq.astype(F32)); v_s[14:15,0:D]+=col_sum(gv_ref[...].astype(F32))
+    v_s[15:16,0:D]+=col_sum(gh*n_x); v_s[16:17,0:D]+=col_sum(gh)
+    gt_o[...]=gx1_ref[...]+norm_back(gh,n_x,inv,vec(g_ref))
+    @pl.when(step==pl.num_programs(0)-1)
     def _():
-        v_o[...]=jnp.zeros_like(v_o)
-        v_o[0:8]=va[...]*fac
-        v_o[8:16]=vb[...]*fac
-        v_o[16:18]=vc[0:2]*fac
-        for k in range(3):
-            for c in range(vf.shape[1]//D):
-                v_o[24+4*k+c:25+4*k+c]=vf[k:k+1,c*D:(c+1)*D]*fac
+        fac=fac_ref[0:1,0:1]
+        w=D//n; f=FF//n; b=256//n
+        row=lax.broadcasted_iota(jnp.int32,(24,128),0); lane=lax.broadcasted_iota(jnp.int32,(24,128),1)
+        heads=jnp.zeros((24,128),F32)
         for h in range(H):
-            v_o[36+h:37+h,0:256]=gb[h//2,h%2:h%2+1,:]*fac
-            v_o[36+h:37+h,256:384]=ds[h//2,h%2:h%2+1,:]*fac*(1.0/jnp.full((1,1),hs_ref[h],F32))
-    n,inv=norm_rows(x_ref[...].astype(F32))
-    gh=nt(gq_ref[...],wq[...])+nt(gk_ref[...],wk[...])+nt(gv_ref[...],wv[...])
-    v_o[18:19]+=col_sum(gh*n)*fac; v_o[19:20]+=col_sum(gh)*fac
-    gt_o[...]=gx1_ref[...]+norm_back(gh,n,inv,vec(g_ref))
-def tail(fac,hs,x,gx1,gq,gk,gv,wq,wk,wv,g,va,vb,vc,vf,gb,ds,T=256):
-    S,D=x.shape
+            heads=jnp.where((row==h)&(lane==HEAD_LANE),ds[h//2,h%2:h%2+1,:]*(1.0/jnp.full((1,1),hs_ref[h],F32)),heads)
+        def window(ref,rows,at):
+            lo=at//128*128
+            v=ref[0:rows,lo:lo+256]
+            return v if at==lo else pltpu.roll(v,256-(at-lo),1)
+        for dev in range(n):
+            t=jnp.where(lane<w,window(v_s,24,w*dev)[:,:128],heads)
+            p=pltpu.roll(p_s[...],(256-b*dev+BUCKET_LANE)%256,1)[:,:128]
+            p=jnp.where((lane[:16]>=BUCKET_LANE)&(lane[:16]<BUCKET_LANE+b),p,t[0:16])
+            u=t[16:24]+jnp.where((lane[:8]<f)&(row[:8]>0)&(row[:8]<4),window(f_s,8,f*dev)[:,:128],0.0)
+            t_s[dev,0:16]=p*fac
+            t_s[dev,16:24]=u*fac
+        core=core_ref[0]
+        for k in range(n//2):
+            keep_o[k]=t_s[2*k+core]
+            send_o[k]=t_s[2*k+1-core]
+def tail(n,core,fac,hs,x,gx1,gq,gk,gv,wq,wk,wv,g,b,va,vb,vf,gb,ds,T=256):
+    S,D=x.shape; FF=vf.shape[1]
     r=rows_of(T,D); w=whole((D,D)); u=whole((D,)); sd=jax.ShapeDtypeStruct
-    return pl.pallas_call(tail_kernel,grid=(S//T,),in_specs=[whole((8,128)),SMEM]+[r]*5+[w]*3+[u]+[whole(v.shape) for v in (va,vb,vc,vf,gb,ds)],
-        out_specs=[r,pl.BlockSpec((48,D),lambda *_:(0,0))],
-        out_shape=[sd((S,D),F32)]+[sd((48,D),F32)],compiler_params=params(1),name="tail",cost_estimate=cost(10*S*D*D,10*D*D+S*D*24))(fac,hs,x,gx1,gq,gk,gv,wq,wk,wv,g,va,vb,vc,vf,gb,ds)
-
+    tile=pl.BlockSpec((n//2,24,128),lambda *_:(0,0,0))
+    return pl.pallas_call(functools.partial(tail_kernel,n),grid=(S//T,),
+        in_specs=[SMEM,whole((8,128)),SMEM]+[r]*5+[w]*3+[u]*2+[whole(v.shape) for v in (va,vb,vf,gb,ds)],
+        out_specs=[r,r,r,tile,tile],
+        out_shape=[sd((S,D),F32),sd((S,D),BF),sd((S,D),BF),sd((n//2,24,128),F32),sd((n//2,24,128),F32)],
+        scratch_shapes=[pltpu.VMEM((24,D+128),F32),pltpu.VMEM((8,FF+128),F32),pltpu.VMEM((16,256),F32),pltpu.VMEM((n,24,128),F32)],
+        compiler_params=params(1),name="tail",cost_estimate=cost(6*S*D*D,6*D*D+S*D*18))(core,fac,hs,x,gx1,gq,gk,gv,wq,wk,wv,g,b,va,vb,vf,gb,ds)
 def memory_kernel(k_ref,v_ref,ck,cv,o):
     o[...]=nt(k_ref[...],ck[...])+nt(v_ref[...],cv[...])
 def memory_grad(gk,gv,ck,cv,T=256):
     S,D=gk.shape
     r=rows_of(T,D); w=whole((D,D))
     return pl.pallas_call(memory_kernel,grid=(S//T,),in_specs=[r,r,w,w],out_specs=r,out_shape=jax.ShapeDtypeStruct((S,D),F32),
-        compiler_params=params(1),name="memory",cost_estimate=cost(4*S*D*D,4*D*D+S*D*8))(gk,gv,ck,cv)
-
-ROWS=(18,19,16,17,14,12,13,8,9,10,11,5,3,4,0,1,2)
-def pick_kernel(n,idx_ref,v,*outs):
-    D=v.shape[1]; w=D//n; idx=idx_ref[0]
-    x=pltpu.roll(v[0:24],lax.rem(D-w*idx,D),1)
-    for r,o in zip(ROWS,outs): o[...]=x[r:r+1,:w].reshape(w)
-    each=n//4; wide=4*D//n
-    shift=lax.rem(D-wide*lax.rem(idx,each),D)
-    for k in range(3):
-        y=pltpu.roll(v[pl.ds(24+4*k+idx//each,1),:],shift,1)
-        outs[17+k][...]=y[:,:wide].reshape(wide)
-    H=outs[20].shape[0]; b=256//n
-    z=pltpu.roll(v[36:36+H,0:256],lax.rem(256-b*idx,256),1)
-    outs[20][...]=z[:,:b]
-    eye=lax.broadcasted_iota(jnp.int32,(H,128),0)==lax.broadcasted_iota(jnp.int32,(H,128),1)
-    outs[21][...]=col_sum(jnp.where(eye,v[36:36+H,256:384],0.0))[:,:H].reshape(H)
-def pick(n,idx,v,H):
-    D=v.shape[1]; sd=jax.ShapeDtypeStruct
-    shapes=[sd((D//n,),F32)]*17+[sd((4*D//n,),F32)]*3+[sd((H,256//n),F32),sd((H,),F32)]
-    return pl.pallas_call(functools.partial(pick_kernel,n),in_specs=[SMEM,pl.BlockSpec(v.shape)],out_shape=shapes,
-        compiler_params=params(0),name="pick")(idx,v)
+        compiler_params=params(1),name="memory",cost_estimate=cost(1000,1000))(gk,gv,ck,cv)
 
 def part_rows(scr,core,keep_o,send_o):
     groups,r=keep_o.shape[:2]
@@ -483,7 +485,7 @@
         @pl.when((step>=first)&(step<last))
         def _(): scr[...]=tn(ins[l][...],ins[r][...])*fac_ref[0:1,0:1]
     part_rows(scr,core_ref[0],keep_o,send_o)
-def wgrad_cols(core,fac,pairs,n,B=768):
+def wgrad_cols(core,fac,pairs,n,B=768,weight=1.0):
     ins=[]; specs=[]; plan=[]; at=0; seen={}
     S,M=pairs[0][0].shape
     for lhs,rhs in pairs:
@@ -498,43 +500,71 @@
     o=pl.BlockSpec((n//2,r,B),lambda i:(0,0,i)); sh=jax.ShapeDtypeStruct((n//2,r,N),F32)
     return pl.pallas_call(functools.partial(wcol_kernel,plan),grid=(at,),in_specs=[SMEM,whole((8,128))]+specs,
         out_specs=[o,o],scratch_shapes=[pltpu.VMEM((M,B),F32)],out_shape=[sh,sh],compiler_params=params(1),name="wgrad",
-        cost_estimate=cost(4*S*M*N,2*S*M*len(ins)+4*M*N))(core,fac,*ins)
-
-def halve_kernel(bit_ref,km,ko,gm,go,keep_o,send_o):
-    send_o[...]=ko[:,0]+go[:,0]
-    keep_o[...]=km[:,0]+gm[:,0]
-def halve(bit,keep,got,part=0,parts=1):
-    A,_,B,r,C=keep.shape
-    C=C//parts
-    K=max(1,A//4)
-    mine=pl.BlockSpec((K,1,B,r,C),lambda i,b:(i,b[0],0,0,part)); other=pl.BlockSpec((K,1,B,r,C),lambda i,b:(i,1-b[0],0,0,part))
-    o=pl.BlockSpec((K,B,r,C),lambda i,b:(i,0,0,0)); sh=jax.ShapeDtypeStruct((A,B,r,C),F32)
-    gs=pltpu.PrefetchScalarGridSpec(num_scalar_prefetch=1,grid=(A//K,),in_specs=[mine,other,mine,other],out_specs=[o,o])
-    return pl.pallas_call(halve_kernel,grid_spec=gs,out_shape=[sh,sh],compiler_params=params(1),name="halve",
-        cost_estimate=cost(1000,1000))(bit,keep,keep,got,got)
-
-def deal_kernel(z_ref,k0,k1,k2,k3,g0,g1,g2,g3,o0,o1,o2,o3):
-    for k,g,o in ((k0,g0,o0),(k1,g1,o1),(k2,g2,o2),(k3,g3,o3)):
-        o[...]=k[0]+g[0]
-def deal(z,keep,got):
-    _,r,C=keep.shape
-    spec=lambda m: pl.BlockSpec((1,r,C),lambda i,z,m=m:(z[0]^m,0,0))
+        cost_estimate=cost(4*S*M*N*weight,(2*S*M*len(ins)+4*M*N)*weight))(core,fac,*ins)
+
+def halve_kernel(count,bit_ref,*refs):
+    for c in range(count):
+        km,ko,gm,go=refs[4*c:4*c+4]
+        keep_o,send_o=refs[4*count+2*c:4*count+2*c+2]
+        send_o[...]=ko[:,0]+go[:,0]
+        keep_o[...]=km[:,0]+gm[:,0]
+def halve(bits,chains):
+    specs=[];ins=[];outs=[];shapes=[]
+    size=sum(4*keep.size//parts for keep,got,part,parts in chains)
+    steps=min([4 if size>8e6 else 2]+[keep.shape[0] for keep,*_ in chains])
+    for c,(keep,got,part,parts) in enumerate(chains):
+        A,_,B,r,C=keep.shape
+        C=C//parts; K=A//steps
+        for flip in (False,True,False,True):
+            specs.append(pl.BlockSpec((K,1,B,r,C),functools.partial(lambda c,flip,part,i,b:(i,1-b[c] if flip else b[c],0,0,part),c,flip,part)))
+        ins+=[keep,keep,got,got]
+        outs+=[pl.BlockSpec((K,B,r,C),lambda i,b:(i,0,0,0))]*2
+        shapes+=[jax.ShapeDtypeStruct((A,B,r,C),F32)]*2
+    gs=pltpu.PrefetchScalarGridSpec(num_scalar_prefetch=1,grid=(steps,),in_specs=specs,out_specs=outs)
+    return pl.pallas_call(functools.partial(halve_kernel,len(chains)),grid_spec=gs,out_shape=shapes,compiler_params=params(1),name="halve",
+        cost_estimate=cost(1000,1000))(bits,*ins)
+
+def deal_kernel(count,z_ref,*refs):
+    outs=refs[8*count:]
+    for m,o in enumerate(outs):
+        at=0
+        for c in range(count):
+            k,g=refs[8*c+m],refs[8*c+4+m]
+            o[:,at:at+k.shape[-1]]=k[0]+g[0]
+            at+=k.shape[-1]
+def deal(z,chains):
+    r=chains[0][0].shape[1]; C=sum(k.shape[2] for k,_ in chains)
+    specs=[];ins=[]
+    for k,g in chains:
+        specs+=[pl.BlockSpec((1,r,k.shape[2]),lambda i,z,m=m:(z[0]^m,0,0)) for m in range(4)]*2
+        ins+=[k]*4+[g]*4
     o=pl.BlockSpec((r,C),lambda i,z:(0,0)); sh=jax.ShapeDtypeStruct((r,C),F32)
-    gs=pltpu.PrefetchScalarGridSpec(num_scalar_prefetch=1,grid=(1,),in_specs=[spec(m) for m in range(4)]*2,out_specs=[o]*4)
-    return pl.pallas_call(deal_kernel,grid_spec=gs,out_shape=[sh]*4,compiler_params=params(1),name="deal",
-        cost_estimate=cost(1000,1000))(z,*([keep]*4),*([got]*4))
-
-def finish_kernel(plan,*refs):
-    ins=refs[:-len(plan)]; outs=refs[-len(plan):]
-    for o,pieces in zip(outs,plan):
-        at=0
-        for c,lo,hi in pieces:
-            o[:,at:at+hi-lo]=(ins[4*c][:,lo:hi]+ins[4*c+1][:,lo:hi])+(ins[4*c+2][:,lo:hi]+ins[4*c+3][:,lo:hi])
-            at+=hi-lo
-def finish(chains,plan):
-    ins=[v for c in chains for v in c.last]
-    shapes=[jax.ShapeDtypeStruct((ins[4*p[0][0]].shape[0],sum(hi-lo for _,lo,hi in p)),F32) for p in plan]
-    return pl.pallas_call(functools.partial(finish_kernel,plan),in_specs=[pl.BlockSpec(v.shape) for v in ins],out_shape=shapes,
+    gs=pltpu.PrefetchScalarGridSpec(num_scalar_prefetch=1,grid=(1,),in_specs=specs,out_specs=[o]*4)
+    return pl.pallas_call(functools.partial(deal_kernel,len(chains)),grid_spec=gs,out_shape=[sh]*4,compiler_params=params(1),name="deal",
+        cost_estimate=cost(1000,1000))(z,*ins)
+
+def finish_kernel(n,plan,tile,*refs):
+    count=len(plan)+22
+    ins=refs[:-count]; outs=refs[-count:]
+    total=lambda c,lo,hi: (ins[4*c][:,lo:hi]+ins[4*c+1][:,lo:hi])+(ins[4*c+2][:,lo:hi]+ins[4*c+3][:,lo:hi])
+    for o,(c,lo,hi) in zip(outs,plan):
+        o[...]=total(c,lo,hi)
+    t=total(*tile)
+    outs=outs[len(plan):]
+    for r,o in zip(PLACE,outs): o[...]=t[r:r+1,:o.shape[0]].reshape(o.shape[0])
+    for k in range(3):
+        o=outs[17+k]
+        o[...]=t[WIDE_ROW+k:WIDE_ROW+k+1,:o.shape[0]].reshape(o.shape[0])
+    H,b=outs[20].shape
+    outs[20][...]=pltpu.roll(t,128-BUCKET_LANE,1)[:H,:b]
+    x=pltpu.roll(t,128-HEAD_LANE,1)[0:16,0:1]
+    eye=lax.broadcasted_iota(jnp.int32,(16,128),0)==lax.broadcasted_iota(jnp.int32,(16,128),1)
+    outs[21][...]=col_sum(jnp.where(eye,x,0.0))[:,:H].reshape(H)
+def finish(n,groups,plan,tile,D,FF,H):
+    ins=[v for g in groups for v in g]
+    sd=jax.ShapeDtypeStruct
+    shapes=[sd((ins[4*c].shape[0],hi-lo),F32) for c,lo,hi in plan]+[sd((D//n,),F32)]*17+[sd((FF//n,),F32)]*3+[sd((H,256//n),F32),sd((H,),F32)]
+    return pl.pallas_call(functools.partial(finish_kernel,n,plan,tile),in_specs=[pl.BlockSpec(v.shape) for v in ins],out_shape=shapes,
         compiler_params=params(0),name="finish",cost_estimate=cost(1000,1000))(*ins)
 
 def swap(x,n,bit):
@@ -542,38 +572,41 @@
 def after(token,*vals):
     return lax.optimization_barrier(tuple(vals)+tuple(token))[:len(vals)]
 class Halving:
-    def __init__(self,n,index,keep,send,order):
-        self.n,self.index,self.order=n,index,list(order)
+    def __init__(self,n,keep,send,order):
+        self.n,self.order=n,list(order)
         self.live=list(range(n.bit_length()-2,0,-1))
         self.keep=keep; self.got=swap(send,n,0); self.part=(0,1)
     def split(self,orders):
         chains=[]
         for k,order in enumerate(orders):
             h=object.__new__(Halving)
-            h.n,h.index,h.order,h.live=self.n,self.index,list(order),list(self.live)
+            h.n,h.order,h.live=self.n,list(order),list(self.live)
             h.keep,h.got,h.part=self.keep,self.got,(k,len(orders))
             chains.append(h)
         return chains
-    def step(self,token):
-        keep,got=after(token,self.keep,self.got)
-        b=self.order.pop(0)
-        axis=self.live.index(b)
-        self.live.remove(b)
-        shape=(2**axis,2,2**(len(self.live)-axis))+keep.shape[-2:]
-        bit=((self.index>>b)&1).reshape(1).astype(jnp.int32)
-        self.keep,send=halve(bit,keep.reshape(shape),got.reshape(shape),*self.part)
-        self.part=(0,1)
-        self.got=swap(send,self.n,b)
-        return send
-
-    def last_step(self,token,zs):
-        keep,got=after(token,self.keep,self.got)
-        z=((self.index>>zs[0])&3).reshape(1).astype(jnp.int32)
-        shape=(4,)+keep.shape[-2:]
-        own,*sends=deal(z,keep.reshape(shape),got.reshape(shape))
-        n=self.n
-        self.last=[own]+[lax.ppermute(s,"dp",[(j,j^((m+1)<<zs[0])) for j in range(n)]) for m,s in enumerate(sends)]
-        return own
+def step(token,index,*chains):
+    bits=[];work=[]
+    flat=after(token,*[v for c in chains for v in (c.keep,c.got)])
+    for k,c in enumerate(chains):
+        b=c.order.pop(0)
+        axis=c.live.index(b)
+        c.live.remove(b)
+        keep,got=flat[2*k:2*k+2]
+        shape=(2**axis,2,2**(len(c.live)-axis))+keep.shape[-2:]
+        bits.append((b,(index>>b)&1))
+        work.append((keep.reshape(shape),got.reshape(shape))+c.part)
+    outs=halve(jnp.stack([v for _,v in bits]).astype(jnp.int32),work)
+    for k,c in enumerate(chains):
+        c.keep,c.part=outs[2*k],(0,1)
+        c.got=swap(outs[2*k+1],c.n,bits[k][0])
+    return [outs[2*k+1] for k in range(len(chains))]
+def last_step(token,index,zs,*chains):
+    flat=after(token,*[v for c in chains for v in (c.keep,c.got)])
+    z=((index>>zs[0])&3).reshape(1).astype(jnp.int32)
+    cut=lambda v: v.reshape((4,)+v.shape[-2:])
+    own,*sends=deal(z,[(cut(flat[2*k]),cut(flat[2*k+1])) for k in range(len(chains))])
+    n=chains[0].n
+    return [own]+[lax.ppermute(s,"dp",[(j,j^((m+1)<<zs[0])) for j in range(n)]) for m,s in enumerate(sends)]
 
 def shards(n,tokens,memory,out_grad,dec_len,mem_len,group_bounds,
            self_norm_gain,self_norm_bias,self_query,self_query_bias,self_key,self_value,self_value_bias,self_output,self_output_bias,
@@ -596,77 +629,57 @@
     a2,lse2=attn_fwd(False,mem_len,head_scale,position_bias,q2,k2,v2)
     lo,gx2,go2,u,gf,h3,g3,gb2,va,vf,fac=mid(n,dec_len,group_bounds,idx,all_dec,a2,x1,og,cross_output,feed_inner,feed_outer,cross_output_bias,cross_post_gain,cross_post_bias,feed_norm_gain,feed_norm_bias,feed_inner_bias,feed_mid_gain,feed_mid_bias,feed_outer_bias)
     keep,send=wgrad_cols(core,fac,[(h3,gf),(a2,gb2)],n)
-    fi=Halving(n,index,keep,send,order_b)
+    fi=Halving(n,keep,send,order_b)
     u,=after([send],u)
     keep,send=wgrad_rows(core,fac,u,g3,n)
-    fo=Halving(n,index,keep,send,order_a)
-    t=[fi.step([send])]
-    t=[fo.step(t)]
+    fo=Halving(n,keep,send,order_a)
+    t=step([send],index,fi)
+    t=step(t,index,fo)
     go2,=after(t,go2)
-    back=attn_bwd(False,mem_len,head_scale,position_bias,q2,k2,v2,go2,a2,lse2,0,pairs)
-    gq2,gk2,gv2,_=back
+    gq2,gk2,gv2,_=attn_bwd(False,mem_len,head_scale,position_bias,q2,k2,v2,go2,a2,lse2,0,pairs)
     gx1,go1,h2,gqs2,gb1,vb=cross_back(head_scale,gq2,x1,gx2,nb1,ib1,gv2,cross_query,self_output,cross_norm_gain,cross_norm_bias,self_post_gain)
-    t=[fo.step([vb])]
+    t=step([vb],index,fo)
     h2,=after(t,h2)
     keep,send=wgrad_cols(core,fac,[(h2,gqs2),(m,gv2),(m,gk2),(a1,gb1)],n)
-    g2=Halving(n,index,keep,send,[])
-    t=[fi.step([send])]
+    g2=Halving(n,keep,send,[])
+    t=step([send],index,fi)
     go1,=after(t,go1)
     half=pairs//2
     back=attn_bwd(True,dec_len,head_scale,position_bias,q1,k1,v1,go1,a1,lse1,0,half)
-    while fo.order: t=[fo.step([back[3]])]
-    t=[fo.last_step([back[3]],zs)]
+    t=[back[3]]
+    while fo.order: t=step(t,index,fo)
+    r_fo=last_step(t,index,zs,fo)
     ga,gb_=g2.split([order_a,order_b])
-    t=[ga.step(t)]
-    t=[gb_.step(t)]
+    t=step([r_fo[0]],index,ga,gb_)
     go1,=after(t,go1)
     gq1,gk1,gv1,ds,gb=attn_bwd(True,dec_len,head_scale,position_bias,q1,k1,v1,go1,a1,lse1,half,pairs-half,back)
-    h1,gqs1,vc=self_norm(x,gq1,gv1,self_norm_gain,self_norm_bias)
-    while fi.order: t=[fi.step([vc])]
-    t=[fi.last_step([vc],zs)]
-    h1,=after(t+fo.last[1:]+[ga.got,gb_.got],h1)
-    t=[ga.step([vc,h1])]
-    t=[gb_.step(t)]
-    h1,=after(t,h1)
+    t=[ds]
+    while fi.order: t=step(t,index,fi)
+    r_fi=last_step(t,index,zs,fi)
+    gx1,=after([r_fi[0]],gx1)
+    gt,h1,gqs1,keep,send=tail(n,core,fac,head_scale,x,gx1,gq1,gk1,gv1,self_query,self_key,self_value,self_norm_gain,self_norm_bias,va,vb,vf,gb,ds)
+    sv=Halving(n,keep,send,order_a)
+    h1,=after([send]+r_fo[1:],h1)
     keep,send=wgrad_cols(core,fac,[(h1,gqs1),(h1,gv1),(h1,gk1)],n)
-    g3_=Halving(n,index,keep,send,[])
-    gx1,=after([send],gx1)
-    gt,packed=tail(fac,head_scale,x,gx1,gqs1,gk1,gv1,self_query,self_key,self_value,self_norm_gain,va,vb,vc,vf,gb,ds)
+    g3_=Halving(n,keep,send,[])
+    t=[send]
+    while ga.order: t=step(t,index,ga,gb_)
+    gk2,=after(t+r_fi[1:],gk2)
+    gm=memory_grad(gk2,gv2,cross_key,cross_value)
     sa,sb=g3_.split([order_a,order_b])
-    t=[sa.step([packed])]
-    t=[sb.step(t)]
-    gk2,=after(t+fi.last[1:],gk2)
-    bit=0
-    other=swap(packed,n,bit)
-    gm=memory_grad(gk2,gv2,cross_key,cross_value)
-    t=[gm]
-    def add_up(t,packed,other,bit):
-        packed,other=after(t,packed,other)
-        packed=packed+other
-        bit+=1
-        if (1<<bit)<n: other=swap(packed,n,bit)
-        return packed,other,bit
-    packed,other,bit=add_up(t,packed,other,bit)
-    t=[packed]
-    for c in (ga,gb_):
-        while c.order: t=[c.step(t)]
-        t=[c.last_step(t,zs)]
-    packed,other,bit=add_up(t,packed,other,bit)
-    t=[packed]
-    while sa.order or sb.order:
-        for c in (sa,sb): t=[c.step(t)]
-        if (1<<bit)<n:
-            packed,other,bit=add_up(t,packed,other,bit)
-            t=[packed]
-    for c in (sa,sb): t=[c.last_step(t,zs)]
-    while (1<<bit)<n:
-        packed,other,bit=add_up(t,packed,other,bit)
-        t=[packed]
-    small=pick(n,idx,packed,H)
-    FF=feed_inner.shape[1]; M=D+D//2
-    g_fo,g_fi,g_co,g_cq,g_cv,g_ck,g_so,g_sq,g_sv,g_sk=finish([fo,fi,ga,gb_,sa,sb],[
-        [(0,0,D)],[(1,0,FF)],[(1,FF,FF+D)],[(2,0,D)],[(2,D,2*D)],[(3,0,D)],[(3,D,2*D)],
-        [(4,0,D)],[(4,D,M),(5,0,D//2)],[(5,D//2,M)]])
+    t=step([gm,ga.got,gb_.got],index,sa,sb,sv)
+    r_g2=last_step(t,index,zs,ga,gb_)
+    t=r_g2
+    while sa.order: t=step(t,index,sa,sb,sv)
+    FF=feed_inner.shape[1]
+    if sv.keep.shape[-2]==sa.keep.shape[-2]:
+        groups=[last_step(t,index,zs,sa,sb,sv)]
+        tile=(3,3*D,3*D+128)
+    else:
+        groups=[last_step(t,index,zs,sa,sb),last_step(t,index,zs,sv)]
+        tile=(4,0,128)
+    g_fo,g_fi,g_co,g_cq,g_cv,g_ck,g_so,g_sq,g_sv,g_sk,*small=finish(n,[r_fo,r_fi,r_g2]+groups,[
+        (0,0,D),(1,0,FF),(1,FF,FF+D),(2,0,D),(2,D,2*D),(2,2*D,3*D),(2,3*D,4*D),(3,0,D),(3,D,2*D),(3,2*D,3*D)],tile,D,FF,H)
     (sng,snb,sqb,svb,sob,spg,spb,cng,cnb,cqb,cvb,cob,cpg,cpb,fng,fnb,fob,fmg,fmb,fib,gpos,ghs)=small
     fo_b=fob
     return (lo[None],gt[None],gm[None],

time: 482 us -> 482 us (level)
  waiting for transfers between devices: 34.1 us -> 96.1 us
  Pallas kernels: 362 us -> 312 us
  starting transfers between devices: 69.4 us -> 54.9 us
  local copies, waits for them, and re-layouts: 3.3 us -> 8.2 us
    ppermute x18 -> x12, waiting for transfers between devices: 9.73 us -> 48.7 us  [last_step(): lax.ppermute(s, 'dp', [(j, j ^ m + 1 << zs[0]) for j in range(n)])]
    ppermute x21 -> x19, waiting for transfers between devices: 24.4 us -> 47.3 us  [swap(): return lax.ppermute(x, 'dp', [(j, j ^ 1 << bit) for j in range(n)])]
    pallas_call x22 -> x14, Pallas kernels: 88.3 us -> 67.1 us  [the longest x8 41.2 us: halve(): pl.pallas_call(functools.partial(halve_kernel, len(chains)), grid_spec=gs...]
    pallas_call x2, Pallas kernels: 49.7 us -> 35.1 us  [attn_fwd(): pl.pallas_call(functools.partial(fwd_kernel, causal), grid_spec=grid_spec...]
    pallas_call x3, Pallas kernels: 81.7 us -> 67.1 us  [attn_bwd(): pl.pallas_call(functools.partial(bwd_kernel, causal, p0, before is not No...]
    ppermute x18 -> x12, starting transfers between devices: 44.1 us -> 31 us  [last_step(): lax.ppermute(s, 'dp', [(j, j ^ m + 1 << zs[0]) for j in range(n)])]
    unnamed x53 -> x51, local copies, waits for them, and re-layouts: 2.64 us -> 7.54 us
    ppermute x21 -> x19, starting transfers between devices: 18 us -> 16.5 us  [swap(): return lax.ppermute(x, 'dp', [(j, j ^ 1 << bit) for j in range(n)])]
  transfers between devices with their start and end apart: 40 -> 32, of which waited for: 7 -> 9; matrix products, arithmetic and copies ran while one was open for 0% -> 0% of each run, Pallas kernels for 61% -> 46%
where the time goes in v1:
time: 482 us; the launch traced here: 475 us
  Pallas kernels  312 us (65%)
  waiting for transfers between devices  96.1 us (20%)
  starting transfers between devices  54.9 us (11%)
  local copies, waits for them, and re-layouts  8.2 us (2%)
    pallas_call x3, Pallas kernels, attn_bwd(): pl.pallas_call(functools.partial(bwd_kernel, causal, p0, before is not No...  67.1 us
    pallas_call x1, Pallas kernels, mid(): pl.pallas_call(functools.partial(mid_kernel, n), grid=(S // T,), in_specs...  56.7 us
    ppermute x12, waiting for transfers between devices, last_step(): lax.ppermute(s, 'dp', [(j, j ^ m + 1 << zs[0]) for j in range(n)])  48.7 us
    ppermute x19, waiting for transfers between devices, swap(): return lax.ppermute(x, 'dp', [(j, j ^ 1 << bit) for j in range(n)])  47.3 us
    pallas_call x8, Pallas kernels, halve(): pl.pallas_call(functools.partial(halve_kernel, len(chains)), grid_spec=gs...  41.2 us
    pallas_call x2, Pallas kernels, attn_fwd(): pl.pallas_call(functools.partial(fwd_kernel, causal), grid_spec=grid_spec...  35.1 us
    pallas_call x3, Pallas kernels, wgrad_cols(): pl.pallas_call(functools.partial(wcol_kernel, plan), grid=(at,), in_specs...  34.9 us
    ppermute x12, starting transfers between devices, last_step(): lax.ppermute(s, 'dp', [(j, j ^ m + 1 << zs[0]) for j in range(n)])  31 us
  transfers between devices with their start and end apart: 32, of which 9 were waited for; matrix products, arithmetic and copies ran while one was open for 0% of the time, Pallas kernels for 46%

profile of v1, /device:TPU:0, one launch (start us, length us, event | category | flops | bytes accessed | tf_op | source)
XLA Modules:
  0.0 474.6 jit_solution(14388649712964995950)
XLA Ops:
  2.0 7.4 %all-to-all-start = ((f32[32,8,128]{2,1,0:T(8,128)}), f32[32,8,128]{2,1,0:T(8,128)}, u32[]{:S(2)}, u32[]{:S(2)}) async-start(f32[32,8,128]{2,1,0:T(8,128)} %broadcast_in_dim.17), calls=%async_computation | async-start | bytes 262144 | tf_op jit(solution)/shard_map/all_to_all | solution.py:625
  10.1 11.9 %pre.1 = (bf16[1024,768]{1,0:T(8,128)(2,1)}, bf16[1024,768]{1,0:T(8,128)(2,1)}, bf16[1024,768]{1,0:T(8,128)(2,1)}, bf16[1024,768]{1,0:T(8,128)(2,1)}, bf16[1024,768]{1,0:T(8,128)(2,1)}) custom-call(bf16[1024,768]{1,0:T(8,128)(2,1)} %bitcast.156, bf16[1024,768]{1,0:T(8,128)(2,1)} %bitcast.154, f32[768]{0:T(1024)} %g_ref.3, f32[768]{0:T(1024)} %b_ref.3, ...), custom_call_target="tpu_custom_call" | custom-call | flops 1207959552000 | bytes 3381657600 | tf_op jit(solution)/shard_map/pre/pallas_call | solution.py:246
  22.0 15.7 %attn_fwd.2 = (bf16[1024,768]{1,0:T(8,128)(2,1)}, f32[6,2,1024]{2,1,0:T(2,128)}) custom-call(s32[1]{0:T(128)S(6)} %copy.91.limit_ref.dec_ref, f32[12]{0:T(128)} %hs_ref.13, f32[12,256]{1,0:T(8,128)} %bias_ref.9, bf16[1024,768]{1,0:T(8,128)(2,1)} %get-tuple-element.217.q_ref, bf16[1024,768]{1,0:T(8,128)(2,1)} %get-tuple-element.218.k_ref, ...), custom_call_target="tpu_custom_call" | custom-call | flops 644245094400 | bytes 1258291200 | tf_op jit(solution)/shard_map/attn_fwd/pallas_call | solution.py:107
  37.7 9.4 %post.1 = (f32[1024,768]{1,0:T(8,128)}, bf16[1024,768]{1,0:T(8,128)(2,1)}, bf16[1024,768]{1,0:T(8,128)(2,1)}, f32[1024,1]{1,0:T(8,128)}) custom-call(bf16[1024,768]{1,0:T(8,128)(2,1)} %get-tuple-element.220.a_ref.refs_5_, bf16[1024,768]{1,0:T(8,128)(2,1)} %bitcast.157, bf16[768,768]{1,0:T(8,128)(2,1)} %wo.3, f32[768]{0:T(1024)} %bo.2, f32[768]{0:T(1024)} %spg.1, ...), custom_call_target="tpu_custom_call" | custom-call | flops 483183820800 | bytes 2359296000 | tf_op jit(solution)/shard_map/post/pallas_call | solution.py:262
  47.1 19.4 %attn_fwd.3 = (bf16[1024,768]{1,0:T(8,128)(2,1)}, f32[6,2,1024]{2,1,0:T(2,128)}) custom-call(s32[1]{0:T(128)S(6)} %copy.92.limit_ref, f32[12]{0:T(128)} %hs_ref.13, f32[12,256]{1,0:T(8,128)} %bias_ref.9, bf16[1024,768]{1,0:T(8,128)(2,1)} %get-tuple-element.221.q_ref, bf16[1024,768]{1,0:T(8,128)(2,1)} %get-tuple-element.222.k_ref, ...), custom_call_target="tpu_custom_call" | custom-call | flops 1288490188800 | bytes 1258291200 | tf_op jit(solution)/shard_map/attn_fwd/pallas_call | solution.py:107
  66.5 56.7 %mid.1 = (bf16[1024,768]{1,0:T(8,128)(2,1)}, f32[1024,768]{1,0:T(8,128)}, bf16[1024,768]{1,0:T(8,128)(2,1)}, bf16[1024,3072]{1,0:T(8,128)(2,1)}, bf16[1024,3072]...) custom-call(s32[1]{0:T(128)S(6)} %copy.91.limit_ref.dec_ref, ...), custom_call_target="tpu_custom_call" | custom-call | flops 4348654387200 | bytes 7785676800 | tf_op jit(solution)/shard_map/mid/pallas_call | solution.py:356
  123.3 13.4 %wgrad.4 = (f32[16,24,3840]{2,1,0:T(8,128)}, f32[16,24,3840]{2,1,0:T(8,128)}) custom-call(s32[1]{0:T(128)S(6)} %and.9.core_ref, f32[8,128]{1,0:T(8,128)} %get-tuple-element.227.fac_ref, bf16[1024,768]{1,0:T(8,128)(2,1)} %get-tuple-element.230.refs_0_, bf16[1024,3072]{1,0:T(8,128)(2,1)} %get-tuple-element.231.refs_1_, ...), custom_call_target="tpu_custom_call" | custom-call | flops 2415919104000 | bytes 3617587200 | tf_op jit(solution)/shard_map/wgrad/pallas_call | solution.py:501
  136.8 10.4 %wgrad.5 = (f32[16,96,768]{2,1,0:T(8,128)}, f32[16,96,768]{2,1,0:T(8,128)}) custom-call(s32[1]{0:T(128)S(6)} %and.9.core_ref, f32[8,128]{1,0:T(8,128)} %get-tuple-element.227.fac_ref, bf16[1024,3072]{1,0:T(8,128)(2,1)} %get-tuple-element.234.l_ref, bf16[1024,768]{1,0:T(8,128)(2,1)} %get-tuple-element.235.r_ref), custom_call_target="tpu_custom_call" | custom-call | flops 1932735283200 | bytes 3460300800 | tf_op jit(solution)/shard_map/wgrad/pallas_call | solution.py:477
  148.2 7.5 %halve.8 = (f32[4,2,24,3840]{3,2,1,0:T(8,128)}, f32[4,2,24,3840]{3,2,1,0:T(8,128)}) custom-call(s32[1]{0:T(128)} %bitcast.7.bit_ref, f32[4,2,2,24,3840]{4,3,2,1,0:T(8,128)} %bitcast.76, f32[4,2,2,24,3840]{4,3,2,1,0:T(8,128)} %bitcast.77, f32[4,2,2,24,3840]{4,3,2,1,0:T(8,128)} %bitcast.9.refs_2_.refs_3_, f32[4,2,2,24,3840]{4,3,2,1,0:T(8,128)} %bitcast.9.refs_2_.refs_3_), custom_call_target="tpu_custom_call" | custom-call | flops 200000 | bytes 200000 | tf_op jit(solution)/shard_map/halve/pallas_call | solution.py:524
  155.7 1.7 collective-permute-start.2
  157.4 5.9 %halve.9 = (f32[8,1,96,768]{3,2,1,0:T(8,128)}, f32[8,1,96,768]{3,2,1,0:T(8,128)}) custom-call(s32[1]{0:T(128)} %bitcast.6.bit_ref, f32[8,2,1,96,768]{4,3,2,1,0:T(8,128)} %bitcast.82, f32[8,2,1,96,768]{4,3,2,1,0:T(8,128)} %bitcast.83, f32[8,2,1,96,768]{4,3,2,1,0:T(8,128)} %bitcast.11.refs_2_.refs_3_, f32[8,2,1,96,768]{4,3,2,1,0:T(8,128)} %bitcast.11.refs_2_.refs_3_), custom_call_target="tpu_custom_call" | custom-call | flops 200000 | bytes 200000 | tf_op jit(solution)/shard_map/halve/pallas_call | solution.py:524
  164.7 37.1 %attn_bwd.3 = (bf16[1024,768]{1,0:T(8,128)(2,1)}, bf16[1024,768]{1,0:T(8,128)(2,1)}, bf16[1024,768]{1,0:T(8,128)(2,1)}, f32[6,2,128]{2,1,0:T(2,128)}) custom-call(s32[1]{0:T(128)S(6)} %copy.92.limit_ref, f32[12]{0:T(128)} %hs_ref.13, f32[12,256]{1,0:T(8,128)} %bias_ref.9, bf16[1024,768]{1,0:T(8,128)(2,1)} %get-tuple-element.221.q_ref, ...), custom_call_target="tpu_custom_call" | custom-call | flops 3221225472000 | bytes 2516582400 | tf_op jit(solution)/shard_map/attn_bwd/pallas_call | solution.py:210
  201.8 12.1 %cross_back.1 = (f32[1024,768]{1,0:T(8,128)}, bf16[1024,768]{1,0:T(8,128)(2,1)}, bf16[1024,768]{1,0:T(8,128)(2,1)}, bf16[1024,768]{1,0:T(8,128)(2,1)}, bf16[1024,768]{1,0:T(8,128)(2,1)}, /*index=5*/f32[8,768]{1,0:T(8,128)}) custom-call(f32[12]{0:T(128)} %hs_ref.13, bf16[1024,768]{1,0:T(8,128)(2,1)} %get-tuple-element.247.gq_ref, ...), custom_call_target="tpu_custom_call" | custom-call | flops 483183820800 | bytes 4875878400 | tf_op jit(solution)/shard_map/cross_back/pallas_call | solution.py:393
  213.9 2.6 collective-permute-done.3
  216.6 3.5 halve.10
  220.4 12.3 %wgrad.6 = (f32[16,24,3072]{2,1,0:T(8,128)}, f32[16,24,3072]{2,1,0:T(8,128)}) custom-call(s32[1]{0:T(128)S(6)} %and.9.core_ref, f32[8,128]{1,0:T(8,128)} %get-tuple-element.227.fac_ref, bf16[1024,768]{1,0:T(8,128)(2,1)} %get-tuple-element.260.refs_0_, bf16[1024,768]{1,0:T(8,128)(2,1)} %get-tuple-element.261.refs_1_, bf16[1024,768]{1,0:T(8,128)(2,1)} %bitcast.155, ...), custom_call_target="tpu_custom_call" | custom-call | flops 1932735283200 | bytes 4089446400 | tf_op jit(solution)/shard_map/wgrad/pallas_call | solution.py:501
  232.7 4.0 halve.11
  236.7 1.7 collective-permute-start.4
  238.4 15.0 %attn_bwd.4 = (bf16[1024,768]{1,0:T(8,128)(2,1)}, bf16[1024,768]{1,0:T(8,128)(2,1)}, bf16[1024,768]{1,0:T(8,128)(2,1)}, f32[6,2,128]{2,1,0:T(2,128)}, f32[6,2,256]{2,1,0:T(2,128)}) custom-call(s32[1]{0:T(128)S(6)} %copy.91.limit_ref.dec_ref, f32[12]{0:T(128)} %hs_ref.13, f32[12,256]{1,0:T(8,128)} %bias_ref.9, bf16[1024,768]{1,0:T(8,128)(2,1)} %get-tuple-element.217.q_ref, ...), custom_call_target="tpu_custom_call" | custom-call | flops 805306368000 | bytes 1258291200 | tf_op jit(solution)/shard_map/attn_bwd/pallas_call | solution.py:210
  253.5 2.6 deal.4
  256.1 2.4 collective-permute-start.10
  260.0 6.7 %halve.12 = (f32[8,1,24,1536]{3,2,1,0:T(8,128)}, f32[8,1,24,1536]{3,2,1,0:T(8,128)}, f32[4,2,24,1536]{3,2,1,0:T(8,128)}, f32[4,2,24,1536]{3,2,1,0:T(8,128)}) custom-call(s32[2]{0:T(128)} %get-tuple-element.434.bit_ref, f32[8,2,1,24,3072]{4,3,2,1,0:T(8,128)} %bitcast.60, f32[8,2,1,24,3072]{4,3,2,1,0:T(8,128)} %bitcast.61, ...), custom_call_target="tpu_custom_call" | custom-call | flops 200000 | bytes 200000 | tf_op jit(solution)/shard_map/halve/pallas_call | solution.py:524
  266.7 15.0 %attn_bwd.5 = (bf16[1024,768]{1,0:T(8,128)(2,1)}, bf16[1024,768]{1,0:T(8,128)(2,1)}, bf16[1024,768]{1,0:T(8,128)(2,1)}, f32[6,2,128]{2,1,0:T(2,128)}, f32[6,2,256]{2,1,0:T(2,128)}) custom-call(s32[1]{0:T(128)S(6)} %copy.91.limit_ref.dec_ref, f32[12]{0:T(128)} %hs_ref.13, ...), custom_call_target="tpu_custom_call", output_to_operand_aliasing={{0}: (9, {}), {1}: (10, {}), {2}: (11, {}), {3}: (12, {}), ... | custom-call | flops 805306368000 | bytes 1258291200 | tf_op jit(solution)/shard_map/attn_bwd/pallas_call | solution.py:210
  281.7 2.9 deal.5
  284.6 11.7 %tail.1 = (f32[1024,768]{1,0:T(8,128)}, bf16[1024,768]{1,0:T(8,128)(2,1)}, bf16[1024,768]{1,0:T(8,128)(2,1)}, f32[16,24,128]{2,1,0:T(8,128)}, f32[16,24,128]{2,1,0:T(8,128)}) custom-call(s32[1]{0:T(128)S(6)} %and.9.core_ref, f32[8,128]{1,0:T(8,128)} %get-tuple-element.227.fac_ref, f32[12]{0:T(128)} %hs_ref.13, bf16[1024,768]{1,0:T(8,128)(2,1)} %bitcast.158, ...), custom_call_target="tpu_custom_call" | custom-call | flops 724775731200 | bytes 3538944000 | tf_op jit(solution)/shard_map/tail/pallas_call | solution.py:446
  296.3 9.2 %wgrad.7 = (f32[16,24,2304]{2,1,0:T(8,128)}, f32[16,24,2304]{2,1,0:T(8,128)}) custom-call(s32[1]{0:T(128)S(6)} %and.9.core_ref, f32[8,128]{1,0:T(8,128)} %get-tuple-element.227.fac_ref, bf16[1024,768]{1,0:T(8,128)(2,1)} %get-tuple-element.308.refs_0_, bf16[1024,768]{1,0:T(8,128)(2,1)} %get-tuple-element.309.refs_1_, ...), custom_call_target="tpu_custom_call" | custom-call | flops 1449551462400 | bytes 2673868800 | tf_op jit(solution)/shard_map/wgrad/pallas_call | solution.py:501
  306.3 1.5 collective-permute-start.8
  307.8 1.9 collective-permute-start.12
  309.7 24.5 %collective-permute-done.7 = f32[8,1,24,1536]{3,2,1,0:T(8,128)S(1)} collective-permute-done((f32[8,1,24,1536]{3,2,1,0:T(8,128)}, f32[8,1,24,1536]{3,2,1,0:T(8,128)S(1)}, u32[]{:S(2)}, u32[]{:S(2)}) %collective-permute-start.7) | collective-permute-done | bytes 1179680 | tf_op jit(solution)/shard_map/ppermute | solution.py:571
  335.7 4.3 halve.13
  340.0 1.6 collective-permute-start.15
  342.7 2.9 collective-permute-start.13
  347.0 23.1 %collective-permute-done.13.refs_6_ = f32[24,3840]{1,0:T(8,128)S(1)} collective-permute-done((f32[24,3840]{1,0:T(8,128)S(1)}, f32[24,3840]{1,0:T(8,128)S(1)}, u32[]{:S(2)}, u32[]{:S(2)}) %collective-permute-start.13) | collective-permute-done | bytes 368672 | tf_op jit(solution)/shard_map/ppermute | solution.py:609
  370.8 6.8 %memory.1 = f32[1024,768]{1,0:T(8,128)} custom-call(bf16[1024,768]{1,0:T(8,128)(2,1)} %get-tuple-element.320.refs_4_.k_ref, bf16[1024,768]{1,0:T(8,128)(2,1)} %get-tuple-element.251.gv_ref.refs_3_.v_ref, bf16[768,768]{1,0:T(8,128)(2,1)} %ck.3, bf16[768,768]{1,0:T(8,128)(2,1)} %cv.3), custom_call_target="tpu_custom_call" | custom-call | flops 200000 | bytes 200000 | tf_op jit(solution)/shard_map/memory/pallas_call | solution.py:457
  377.7 1.8 copy-done.9
  379.6 5.4 %halve.14 = (f32[8,1,24,1152]{3,2,1,0:T(8,128)}, f32[8,1,24,1152]{3,2,1,0:T(8,128)}, f32[4,2,24,1152]{3,2,1,0:T(8,128)}, f32[4,2,24,1152]{3,2,1,0:T(8,128)}, f32...) custom-call(s32[3]{0:T(128)} %get-tuple-element.436.bit_ref, f32[8,2,1,24,2304]{4,3,2,1,0:T(8,128)} %bitcast.64, ...), custom_call_target="tpu_custom_call" | custom-call | flops 200000 | bytes 200000 | tf_op jit(solution)/shard_map/halve/pallas_call | solution.py:524
  387.7 2.7 deal.6
  390.4 6.5 %collective-permute-start.19 = (f32[24,3072]{1,0:T(8,128)}, f32[24,3072]{1,0:T(8,128)S(1)}, u32[]{:S(2)}, u32[]{:S(2)}) collective-permute-start(f32[24,3072]{1,0:T(8,128)} %get-tuple-element.339), channel_id=1, source_target_pairs={{0,8},{1,9},{2,10},{3,11},{4,12},{5,13},{6,14},{7,15},{8,0},{9,1},... | collective-permute-start | bytes 884744 | tf_op jit(solution)/shard_map/ppermute | solution.py:609
  398.2 11.2 %collective-permute-done.24 = f32[8,1,24,128]{3,2,1,0:T(8,128)S(1)} collective-permute-done((f32[8,1,24,128]{3,2,1,0:T(8,128)}, f32[8,1,24,128]{3,2,1,0:T(8,128)S(1)}, u32[]{:S(2)}, u32[]{:S(2)}) %collective-permute-start.24) | collective-permute-done | bytes 98336 | tf_op jit(solution)/shard_map/ppermute | solution.py:571
  409.4 2.4 collective-permute-start.21
  411.8 8.3 %collective-permute-done.21.refs_11_ = f32[24,3072]{1,0:T(8,128)S(1)} collective-permute-done((f32[24,3072]{1,0:T(8,128)}, f32[24,3072]{1,0:T(8,128)S(1)}, u32[]{:S(2)}, u32[]{:S(2)}) %collective-permute-start.21) | collective-permute-done | bytes 294944 | tf_op jit(solution)/shard_map/ppermute | solution.py:609
  421.4 3.9 halve.15
  428.6 8.8 %collective-permute-done.27 = f32[4,1,24,128]{3,2,0,1:T(8,128)S(1)} collective-permute-done((f32[4,1,24,128]{3,2,0,1:T(8,128)}, f32[4,1,24,128]{3,2,0,1:T(8,128)S(1)}, u32[]{:S(2)}, u32[]{:S(2)}) %collective-permute-start.27) | collective-permute-done | bytes 49184 | tf_op jit(solution)/shard_map/ppermute | solution.py:571
  438.4 2.5 deal.7
  440.9 8.1 %collective-permute-start.28 = (f32[24,2432]{1,0:T(8,128)}, f32[24,2432]{1,0:T(8,128)S(1)}, u32[]{:S(2)}, u32[]{:S(2)}) collective-permute-start(f32[24,2432]{1,0:T(8,128)} %get-tuple-element.364), channel_id=1, source_target_pairs={{0,8},{1,9},{2,10},{3,11},{4,12},{5,13},{6,14},{7,15},{8,0},{9,1},... | collective-permute-start | bytes 700424 | tf_op jit(solution)/shard_map/ppermute | solution.py:609
  451.5 6.5 %collective-permute-done.28.refs_13_ = f32[24,2432]{1,0:T(8,128)S(1)} collective-permute-done((f32[24,2432]{1,0:T(8,128)}, f32[24,2432]{1,0:T(8,128)S(1)}, u32[]{:S(2)}, u32[]{:S(2)}) %collective-permute-start.28) | collective-permute-done | bytes 233504 | tf_op jit(solution)/shard_map/ppermute | solution.py:609
  458.0 10.8 %collective-permute-done.29.refs_14_ = f32[24,2432]{1,0:T(8,128)S(1)} collective-permute-done((f32[24,2432]{1,0:T(8,128)}, f32[24,2432]{1,0:T(8,128)S(1)}, u32[]{:S(2)}, u32[]{:S(2)}) %collective-permute-start.29) | collective-permute-done | bytes 233504 | tf_op jit(solution)/shard_map/ppermute | solution.py:609
  469.5 3.6 finish.1
  (98 shorter events, 24.6 us)
Async XLA Ops:
  2.0 64.5 %all-to-all-start = ((f32[32,8,128]{2,1,0:T(8,128)}), f32[32,8,128]{2,1,0:T(8,128)}, u32[]{:S(2)}, u32[]{:S(2)}) async-start(f32[32,8,128]{2,1,0:T(8,128)} %broadcast_in_dim.17), calls=%async_computation | async-start | bytes 262144 | tf_op jit(solution)/shard_map/all_to_all | solution.py:625
  136.7 11.5 %collective-permute-start.1 = (f32[16,24,3840]{2,1,0:T(8,128)}, f32[16,24,3840]{2,1,0:T(8,128)}, u32[]{:S(2)}, u32[]{:S(2)}) collective-permute-start(f32[16,24,3840]{2,1,0:T(8,128)} %get-tuple-element.233), channel_id=1, source_target_pairs={{0,1},{1,0},{2,3},{3,2},{4,5},{5,4},{6,7},{7,6},{8,9},{9,8},{10,11... | collective-permute-start | bytes 17694728 | tf_op jit(solution)/shard_map/ppermute | solution.py:571
  147.2 10.1 %collective-permute-start = (f32[16,96,768]{2,1,0:T(8,128)}, f32[16,96,768]{2,1,0:T(8,128)}, u32[]{:S(2)}, u32[]{:S(2)}) collective-permute-start(f32[16,96,768]{2,1,0:T(8,128)} %get-tuple-element.237), channel_id=1, source_target_pairs={{0,1},{1,0},{2,3},{3,2},{4,5},{5,4},{6,7},{7,6},{8,9},{9,8},{10,11... | collective-permute-start | bytes 14155784 | tf_op jit(solution)/shard_map/ppermute | solution.py:571
  155.7 77.1 %collective-permute-start.2 = (f32[4,2,24,3840]{3,2,1,0:T(8,128)}, f32[4,2,24,3840]{3,2,1,0:T(8,128)}, u32[]{:S(2)}, u32[]{:S(2)}) collective-permute-start(f32[4,2,24,3840]{3,2,1,0:T(8,128)} %get-tuple-element.241), channel_id=1, source_target_pairs={{0,4},{1,5},{2,6},{3,7},{4,0},{5,1},{6,2},{7,3},{8,12},{9,13},{10,... | collective-permute-start | bytes 8847368 | tf_op jit(solution)/shard_map/ppermute | solution.py:571
  163.3 53.3 %collective-permute-start.3 = (f32[8,1,96,768]{3,2,1,0:T(8,128)}, f32[8,1,96,768]{3,2,1,0:T(8,128)}, u32[]{:S(2)}, u32[]{:S(2)}) collective-permute-start(f32[8,1,96,768]{3,2,1,0:T(8,128)} %get-tuple-element.244), channel_id=1, source_target_pairs={{0,2},{1,3},{2,0},{3,1},{4,6},{5,7},{6,4},{7,5},{8,10},{9,11},{10,... | collective-permute-start | bytes 7077896 | tf_op jit(solution)/shard_map/ppermute | solution.py:571
  220.1 33.4 %collective-permute-start.6 = (f32[4,1,96,768]{3,2,0,1:T(8,128)}, f32[4,1,96,768]{3,2,0,1:T(8,128)}, u32[]{:S(2)}, u32[]{:S(2)}) collective-permute-start(f32[4,1,96,768]{3,2,0,1:T(8,128)} %bitcast.160), channel_id=1, source_target_pairs={{0,4},{1,5},{2,6},{3,7},{4,0},{5,1},{6,2},{7,3},{8,12},{9,13},{10,... | collective-permute-start | bytes 3538952 | tf_op jit(solution)/shard_map/ppermute | solution.py:571
  232.7 27.3 %collective-permute-start.5 = (f32[16,24,3072]{2,1,0:T(8,128)}, f32[16,24,3072]{2,1,0:T(8,128)}, u32[]{:S(2)}, u32[]{:S(2)}) collective-permute-start(f32[16,24,3072]{2,1,0:T(8,128)} %get-tuple-element.264), channel_id=1, source_target_pairs={{0,1},{1,0},{2,3},{3,2},{4,5},{5,4},{6,7},{7,6},{8,9},{9,8},{10,11... | collective-permute-start | bytes 14155784 | tf_op jit(solution)/shard_map/ppermute | solution.py:571
  236.7 45.0 %collective-permute-start.4 = (f32[4,1,24,3840]{3,2,0,1:T(8,128)}, f32[4,1,24,3840]{3,2,0,1:T(8,128)}, u32[]{:S(2)}, u32[]{:S(2)}) collective-permute-start(f32[4,1,24,3840]{3,2,0,1:T(8,128)} %bitcast.159), channel_id=1, source_target_pairs={{0,2},{1,3},{2,0},{3,1},{4,6},{5,7},{6,4},{7,5},{8,10},{9,11},{10,... | collective-permute-start | bytes 4423688 | tf_op jit(solution)/shard_map/ppermute | solution.py:571
  256.1 40.2 %collective-permute-start.10 = (f32[96,768]{1,0:T(8,128)}, f32[96,768]{1,0:T(8,128)}, u32[]{:S(2)}, u32[]{:S(2)}) collective-permute-start(f32[96,768]{1,0:T(8,128)} %get-tuple-element.306), channel_id=1, source_target_pairs={{0,16},{1,17},{2,18},{3,19},{4,20},{5,21},{6,22},{7,23},{8,24},{9,... | collective-permute-start | bytes 884744 | tf_op jit(solution)/shard_map/ppermute | solution.py:609
  258.5 37.8 %collective-permute-start.11 = (f32[96,768]{1,0:T(8,128)}, f32[96,768]{1,0:T(8,128)}, u32[]{:S(2)}, u32[]{:S(2)}) collective-permute-start(f32[96,768]{1,0:T(8,128)} %get-tuple-element.307), channel_id=1, source_target_pairs={{0,24},{1,25},{2,26},{3,27},{4,28},{5,29},{6,30},{7,31},{8,16},{9,... | collective-permute-start | bytes 884744 | tf_op jit(solution)/shard_map/ppermute | solution.py:609
  259.9 36.4 %collective-permute-start.9 = (f32[96,768]{1,0:T(8,128)}, f32[96,768]{1,0:T(8,128)}, u32[]{:S(2)}, u32[]{:S(2)}) collective-permute-start(f32[96,768]{1,0:T(8,128)} %get-tuple-element.305), channel_id=1, source_target_pairs={{0,8},{1,9},{2,10},{3,11},{4,12},{5,13},{6,14},{7,15},{8,0},{9,1},... | collective-permute-start | bytes 884744 | tf_op jit(solution)/shard_map/ppermute | solution.py:609
  296.3 10.0 %copy-start.21 = (f32[4,2,24,1536]{3,2,1,0:T(8,128)S(1)}, f32[4,2,24,1536]{3,2,1,0:T(8,128)}, u32[]{:S(2)}) copy-start(f32[4,2,24,1536]{3,2,1,0:T(8,128)} %get-tuple-element.283) | copy-start | bytes 3538948
  305.6 37.1 %copy-start.23 = (f32[24,3840]{1,0:T(8,128)S(1)}, f32[24,3840]{1,0:T(8,128)}, u32[]{:S(2)}) copy-start(f32[24,3840]{1,0:T(8,128)} %get-tuple-element.318) | copy-start | bytes 1105924
  305.6 40.0 %copy-start.22 = (f32[24,3840]{1,0:T(8,128)S(1)}, f32[24,3840]{1,0:T(8,128)}, u32[]{:S(2)}) copy-start(f32[24,3840]{1,0:T(8,128)} %get-tuple-element.319) | copy-start | bytes 1105924
  305.6 72.1 %collective-permute-start.17 = (f32[16,24,2304]{2,1,0:T(8,128)}, f32[16,24,2304]{2,1,0:T(8,128)S(1)}, u32[]{:S(2)}, u32[]{:S(2)}) collective-permute-start(f32[16,24,2304]{2,1,0:T(8,128)} %get-tuple-element.310), channel_id=1, source_target_pairs={{0,1},{1,0},{2,3},{3,2},{4,5},{5,4},{6,7},{7,6},{8,9},{9,8},{10,11... | collective-permute-start | bytes 10616840 | tf_op jit(solution)/shard_map/ppermute | solution.py:571
  305.7 28.6 %collective-permute-start.7 = (f32[8,1,24,1536]{3,2,1,0:T(8,128)}, f32[8,1,24,1536]{3,2,1,0:T(8,128)S(1)}, u32[]{:S(2)}, u32[]{:S(2)}) collective-permute-start(f32[8,1,24,1536]{3,2,1,0:T(8,128)} %get-tuple-element.282), channel_id=1, source_target_pairs={{0,2},{1,3},{2,0},{3,1},{4,6},{5,7},{6,4},{7,5},{8,10},{9,11},{10,... | collective-permute-start | bytes 3538952 | tf_op jit(solution)/shard_map/ppermute | solution.py:571
  306.3 28.0 %collective-permute-start.8 = (f32[4,2,24,1536]{3,2,1,0:T(8,128)S(1)}, f32[4,2,24,1536]{3,2,1,0:T(8,128)S(1)}, u32[]{:S(2)}, u32[]{:S(2)}) collective-permute-start(f32[4,2,24,1536]{3,2,1,0:T(8,128)S(1)} %copy-done.21), channel_id=1, source_target_pairs={{0,4},{1,5},{2,6},{3,7},{4,0},{5,1},{6,2},{7,3},{8,12},{9,13},{10,... | collective-permute-start | bytes 3538952 | tf_op jit(solution)/shard_map/ppermute | solution.py:571
  307.8 37.8 %collective-permute-start.12 = (f32[24,3840]{1,0:T(8,128)}, f32[24,3840]{1,0:T(8,128)S(1)}, u32[]{:S(2)}, u32[]{:S(2)}) collective-permute-start(f32[24,3840]{1,0:T(8,128)} %get-tuple-element.317), channel_id=1, source_target_pairs={{0,8},{1,9},{2,10},{3,11},{4,12},{5,13},{6,14},{7,15},{8,0},{9,1},... | collective-permute-start | bytes 1105928 | tf_op jit(solution)/shard_map/ppermute | solution.py:609
  334.3 35.9 %copy-start.24 = (f32[16,24,128]{2,1,0:T(8,128)S(1)}, f32[16,24,128]{2,1,0:T(8,128)}, u32[]{:S(2)}) copy-start(f32[16,24,128]{2,1,0:T(8,128)} %get-tuple-element.304) | copy-start | bytes 589828
  340.0 37.7 %collective-permute-start.15 = (f32[4,1,24,1536]{3,2,0,1:T(8,128)}, f32[4,1,24,1536]{3,2,0,1:T(8,128)S(1)}, u32[]{:S(2)}, u32[]{:S(2)}) collective-permute-start(f32[4,1,24,1536]{3,2,0,1:T(8,128)} %bitcast.162), channel_id=1, source_target_pairs={{0,4},{1,5},{2,6},{3,7},{4,0},{5,1},{6,2},{7,3},{8,12},{9,13},{10,... | collective-permute-start | bytes 1769480 | tf_op jit(solution)/shard_map/ppermute | solution.py:571
  341.5 36.2 %collective-permute-start.16 = (f32[4,1,24,1536]{3,2,0,1:T(8,128)}, f32[4,1,24,1536]{3,2,0,1:T(8,128)S(1)}, u32[]{:S(2)}, u32[]{:S(2)}) collective-permute-start(f32[4,1,24,1536]{3,2,0,1:T(8,128)} %bitcast.161), channel_id=1, source_target_pairs={{0,2},{1,3},{2,0},{3,1},{4,6},{5,7},{6,4},{7,5},{8,10},{9,11},{10,... | collective-permute-start | bytes 1769480 | tf_op jit(solution)/shard_map/ppermute | solution.py:571
  342.7 27.5 %collective-permute-start.13 = (f32[24,3840]{1,0:T(8,128)S(1)}, f32[24,3840]{1,0:T(8,128)S(1)}, u32[]{:S(2)}, u32[]{:S(2)}) collective-permute-start(f32[24,3840]{1,0:T(8,128)S(1)} %copy-done.23), channel_id=1, source_target_pairs={{0,16},{1,17},{2,18},{3,19},{4,20},{5,21},{6,22},{7,23},{8,24},{9,... | collective-permute-start | bytes 1105928 | tf_op jit(solution)/shard_map/ppermute | solution.py:609
  345.5 32.1 %copy-start.12 = (f32[24,3840]{1,0:T(8,128)}, f32[24,3840]{1,0:T(8,128)S(1)}, u32[]{:S(2)}) copy-start(f32[24,3840]{1,0:T(8,128)S(1)} %collective-permute-done.12.refs_5_) | copy-start | bytes 1105924
  345.5 25.3 %collective-permute-start.14 = (f32[24,3840]{1,0:T(8,128)S(1)}, f32[24,3840]{1,0:T(8,128)S(1)}, u32[]{:S(2)}, u32[]{:S(2)}) collective-permute-start(f32[24,3840]{1,0:T(8,128)S(1)} %copy-done.22), channel_id=1, source_target_pairs={{0,24},{1,25},{2,26},{3,27},{4,28},{5,29},{6,30},{7,31},{8,16},{9,... | collective-permute-start | bytes 1105928 | tf_op jit(solution)/shard_map/ppermute | solution.py:609
  370.2 7.5 %copy-start.13 = (f32[24,3840]{1,0:T(8,128)}, f32[24,3840]{1,0:T(8,128)S(1)}, u32[]{:S(2)}) copy-start(f32[24,3840]{1,0:T(8,128)S(1)} %collective-permute-done.13.refs_6_) | copy-start | bytes 1105924
  370.2 7.5 %collective-permute-start.18 = (f32[16,24,128]{2,1,0:T(8,128)S(1)}, f32[16,24,128]{2,1,0:T(8,128)S(1)}, u32[]{:S(2)}, u32[]{:S(2)}) collective-permute-start(f32[16,24,128]{2,1,0:T(8,128)S(1)} %copy-done.24), channel_id=1, source_target_pairs={{0,1},{1,0},{2,3},{3,2},{4,5},{5,4},{6,7},{7,6},{8,9},{9,8},{10,11... | collective-permute-start | bytes 589832 | tf_op jit(solution)/shard_map/ppermute | solution.py:571
  370.8 6.8 %copy-start.14 = (f32[24,3840]{1,0:T(8,128)}, f32[24,3840]{1,0:T(8,128)S(1)}, u32[]{:S(2)}) copy-start(f32[24,3840]{1,0:T(8,128)S(1)} %collective-permute-done.14.refs_7_) | copy-start | bytes 1105924
  377.7 1.8 copy-start.9
  377.7 7.3 %copy-start.1 = (f32[4,1,24,1536]{3,2,0,1:T(8,128)}, f32[4,1,24,1536]{3,2,0,1:T(8,128)S(1)}, u32[]{:S(2)}) copy-start(f32[4,1,24,1536]{3,2,0,1:T(8,128)S(1)} %collective-permute-done.15) | copy-start | bytes 1769476
  377.7 7.3 %copy-start.2 = (f32[4,1,24,1536]{3,2,0,1:T(8,128)}, f32[4,1,24,1536]{3,2,0,1:T(8,128)S(1)}, u32[]{:S(2)}) copy-start(f32[4,1,24,1536]{3,2,0,1:T(8,128)S(1)} %collective-permute-done.16) | copy-start | bytes 1769476
  377.7 1.8 copy-start
  385.0 35.1 %collective-permute-start.22 = (f32[8,1,24,1152]{3,2,1,0:T(8,128)}, f32[8,1,24,1152]{3,2,1,0:T(8,128)S(1)}, u32[]{:S(2)}, u32[]{:S(2)}) collective-permute-start(f32[8,1,24,1152]{3,2,1,0:T(8,128)} %get-tuple-element.331), channel_id=1, source_target_pairs={{0,2},{1,3},{2,0},{3,1},{4,6},{5,7},{6,4},{7,5},{8,10},{9,11},{10,... | collective-permute-start | bytes 2654216 | tf_op jit(solution)/shard_map/ppermute | solution.py:571
  386.3 33.8 %collective-permute-start.23 = (f32[4,2,24,1152]{3,2,1,0:T(8,128)}, f32[4,2,24,1152]{3,2,1,0:T(8,128)S(1)}, u32[]{:S(2)}, u32[]{:S(2)}) collective-permute-start(f32[4,2,24,1152]{3,2,1,0:T(8,128)} %get-tuple-element.332), channel_id=1, source_target_pairs={{0,4},{1,5},{2,6},{3,7},{4,0},{5,1},{6,2},{7,3},{8,12},{9,13},{10,... | collective-permute-start | bytes 2654216 | tf_op jit(solution)/shard_map/ppermute | solution.py:571
  386.8 22.6 %collective-permute-start.24 = (f32[8,1,24,128]{3,2,1,0:T(8,128)}, f32[8,1,24,128]{3,2,1,0:T(8,128)S(1)}, u32[]{:S(2)}, u32[]{:S(2)}) collective-permute-start(f32[8,1,24,128]{3,2,1,0:T(8,128)} %get-tuple-element.333), channel_id=1, source_target_pairs={{0,2},{1,3},{2,0},{3,1},{4,6},{5,7},{6,4},{7,5},{8,10},{9,11},{10,... | collective-permute-start | bytes 294920 | tf_op jit(solution)/shard_map/ppermute | solution.py:571
  390.4 21.4 %collective-permute-start.19 = (f32[24,3072]{1,0:T(8,128)}, f32[24,3072]{1,0:T(8,128)S(1)}, u32[]{:S(2)}, u32[]{:S(2)}) collective-permute-start(f32[24,3072]{1,0:T(8,128)} %get-tuple-element.339), channel_id=1, source_target_pairs={{0,8},{1,9},{2,10},{3,11},{4,12},{5,13},{6,14},{7,15},{8,0},{9,1},... | collective-permute-start | bytes 884744 | tf_op jit(solution)/shard_map/ppermute | solution.py:609
  396.9 14.9 %collective-permute-start.20 = (f32[24,3072]{1,0:T(8,128)}, f32[24,3072]{1,0:T(8,128)S(1)}, u32[]{:S(2)}, u32[]{:S(2)}) collective-permute-start(f32[24,3072]{1,0:T(8,128)} %get-tuple-element.340), channel_id=1, source_target_pairs={{0,16},{1,17},{2,18},{3,19},{4,20},{5,21},{6,22},{7,23},{8,24},{9,... | collective-permute-start | bytes 884744 | tf_op jit(solution)/shard_map/ppermute | solution.py:609
  409.4 10.7 %copy-start.11 = (f32[8,1,24,128]{3,2,1,0:T(8,128)}, f32[8,1,24,128]{3,2,1,0:T(8,128)S(1)}, u32[]{:S(2)}) copy-start(f32[8,1,24,128]{3,2,1,0:T(8,128)S(1)} %collective-permute-done.24) | copy-start | bytes 294916
  409.4 10.7 %collective-permute-start.21 = (f32[24,3072]{1,0:T(8,128)}, f32[24,3072]{1,0:T(8,128)S(1)}, u32[]{:S(2)}, u32[]{:S(2)}) collective-permute-start(f32[24,3072]{1,0:T(8,128)} %get-tuple-element.341), channel_id=1, source_target_pairs={{0,24},{1,25},{2,26},{3,27},{4,28},{5,29},{6,30},{7,31},{8,16},{9,... | collective-permute-start | bytes 884744 | tf_op jit(solution)/shard_map/ppermute | solution.py:609
  411.8 29.0 %copy-start.15 = (f32[24,3072]{1,0:T(8,128)}, f32[24,3072]{1,0:T(8,128)S(1)}, u32[]{:S(2)}) copy-start(f32[24,3072]{1,0:T(8,128)S(1)} %collective-permute-done.19.refs_9_) | copy-start | bytes 884740
  411.8 29.0 %copy-start.16 = (f32[24,3072]{1,0:T(8,128)}, f32[24,3072]{1,0:T(8,128)S(1)}, u32[]{:S(2)}) copy-start(f32[24,3072]{1,0:T(8,128)S(1)} %collective-permute-done.20.refs_10_) | copy-start | bytes 884740
  420.1 20.7 %copy-start.17 = (f32[24,3072]{1,0:T(8,128)}, f32[24,3072]{1,0:T(8,128)S(1)}, u32[]{:S(2)}) copy-start(f32[24,3072]{1,0:T(8,128)S(1)} %collective-permute-done.21.refs_11_) | copy-start | bytes 884740
  425.3 12.1 %collective-permute-start.25 = (f32[4,1,24,1152]{3,2,0,1:T(8,128)}, f32[4,1,24,1152]{3,2,0,1:T(8,128)S(1)}, u32[]{:S(2)}, u32[]{:S(2)}) collective-permute-start(f32[4,1,24,1152]{3,2,0,1:T(8,128)} %bitcast.164), channel_id=1, source_target_pairs={{0,4},{1,5},{2,6},{3,7},{4,0},{5,1},{6,2},{7,3},{8,12},{9,13},{10,... | collective-permute-start | bytes 1327112 | tf_op jit(solution)/shard_map/ppermute | solution.py:571
  426.0 11.5 %collective-permute-start.26 = (f32[4,1,24,1152]{3,2,0,1:T(8,128)}, f32[4,1,24,1152]{3,2,0,1:T(8,128)S(1)}, u32[]{:S(2)}, u32[]{:S(2)}) collective-permute-start(f32[4,1,24,1152]{3,2,0,1:T(8,128)} %bitcast.163), channel_id=1, source_target_pairs={{0,2},{1,3},{2,0},{3,1},{4,6},{5,7},{6,4},{7,5},{8,10},{9,11},{10,... | collective-permute-start | bytes 1327112 | tf_op jit(solution)/shard_map/ppermute | solution.py:571
  427.1 10.3 %collective-permute-start.27 = (f32[4,1,24,128]{3,2,0,1:T(8,128)}, f32[4,1,24,128]{3,2,0,1:T(8,128)S(1)}, u32[]{:S(2)}, u32[]{:S(2)}) collective-permute-start(f32[4,1,24,128]{3,2,0,1:T(8,128)} %bitcast.165), channel_id=1, source_target_pairs={{0,4},{1,5},{2,6},{3,7},{4,0},{5,1},{6,2},{7,3},{8,12},{9,13},{10,... | collective-permute-start | bytes 147464 | tf_op jit(solution)/shard_map/ppermute | solution.py:571
  440.9 17.1 %collective-permute-start.28 = (f32[24,2432]{1,0:T(8,128)}, f32[24,2432]{1,0:T(8,128)S(1)}, u32[]{:S(2)}, u32[]{:S(2)}) collective-permute-start(f32[24,2432]{1,0:T(8,128)} %get-tuple-element.364), channel_id=1, source_target_pairs={{0,8},{1,9},{2,10},{3,11},{4,12},{5,13},{6,14},{7,15},{8,0},{9,1},... | collective-permute-start | bytes 700424 | tf_op jit(solution)/shard_map/ppermute | solution.py:609
  449.0 19.7 %collective-permute-start.29 = (f32[24,2432]{1,0:T(8,128)}, f32[24,2432]{1,0:T(8,128)S(1)}, u32[]{:S(2)}, u32[]{:S(2)}) collective-permute-start(f32[24,2432]{1,0:T(8,128)} %get-tuple-element.365), channel_id=1, source_target_pairs={{0,16},{1,17},{2,18},{3,19},{4,20},{5,21},{6,22},{7,23},{8,24},{9,... | collective-permute-start | bytes 700424 | tf_op jit(solution)/shard_map/ppermute | solution.py:609
  450.0 18.7 %collective-permute-start.30 = (f32[24,2432]{1,0:T(8,128)}, f32[24,2432]{1,0:T(8,128)S(1)}, u32[]{:S(2)}, u32[]{:S(2)}) collective-permute-start(f32[24,2432]{1,0:T(8,128)} %get-tuple-element.366), channel_id=1, source_target_pairs={{0,24},{1,25},{2,26},{3,27},{4,28},{5,29},{6,30},{7,31},{8,16},{9,... | collective-permute-start | bytes 700424 | tf_op jit(solution)/shard_map/ppermute | solution.py:609
  458.0 10.8 %copy-start.18 = (f32[24,2432]{1,0:T(8,128)}, f32[24,2432]{1,0:T(8,128)S(1)}, u32[]{:S(2)}) copy-start(f32[24,2432]{1,0:T(8,128)S(1)} %collective-permute-done.28.refs_13_) | copy-start | bytes 700420
  (9 other events, 8.4 us)

commit v2 on v1

--- a/solution.py
+++ b/solution.py
@@ -448,14 +448,14 @@
         out_specs=[r,r,r,tile,tile],
         out_shape=[sd((S,D),F32),sd((S,D),BF),sd((S,D),BF),sd((n//2,24,128),F32),sd((n//2,24,128),F32)],
         scratch_shapes=[pltpu.VMEM((24,D+128),F32),pltpu.VMEM((8,FF+128),F32),pltpu.VMEM((16,256),F32),pltpu.VMEM((n,24,128),F32)],
-        compiler_params=params(1),name="tail",cost_estimate=cost(6*S*D*D,6*D*D+S*D*18))(core,fac,hs,x,gx1,gq,gk,gv,wq,wk,wv,g,b,va,vb,vf,gb,ds)
+        compiler_params=params(1),name="tail",cost_estimate=cost(1000,1000))(core,fac,hs,x,gx1,gq,gk,gv,wq,wk,wv,g,b,va,vb,vf,gb,ds)
 def memory_kernel(k_ref,v_ref,ck,cv,o):
     o[...]=nt(k_ref[...],ck[...])+nt(v_ref[...],cv[...])
 def memory_grad(gk,gv,ck,cv,T=256):
     S,D=gk.shape
     r=rows_of(T,D); w=whole((D,D))
     return pl.pallas_call(memory_kernel,grid=(S//T,),in_specs=[r,r,w,w],out_specs=r,out_shape=jax.ShapeDtypeStruct((S,D),F32),
-        compiler_params=params(1),name="memory",cost_estimate=cost(1000,1000))(gk,gv,ck,cv)
+        compiler_params=params(1),name="memory",cost_estimate=cost(4*S*D*D,4*D*D+S*D*8))(gk,gv,ck,cv)
 
 def part_rows(scr,core,keep_o,send_o):
     groups,r=keep_o.shape[:2]
@@ -659,18 +659,19 @@
     gx1,=after([r_fi[0]],gx1)
     gt,h1,gqs1,keep,send=tail(n,core,fac,head_scale,x,gx1,gq1,gk1,gv1,self_query,self_key,self_value,self_norm_gain,self_norm_bias,va,vb,vf,gb,ds)
     sv=Halving(n,keep,send,order_a)
-    h1,=after([send]+r_fo[1:],h1)
+    h1,=after([send,ga.got,gb_.got]+r_fo[1:],h1)
     keep,send=wgrad_cols(core,fac,[(h1,gqs1),(h1,gv1),(h1,gk1)],n)
     g3_=Halving(n,keep,send,[])
     t=[send]
     while ga.order: t=step(t,index,ga,gb_)
+    sa,sb=g3_.split([order_a,order_b])
+    t=step(t,index,sa,sb,sv)
     gk2,=after(t+r_fi[1:],gk2)
     gm=memory_grad(gk2,gv2,cross_key,cross_value)
-    sa,sb=g3_.split([order_a,order_b])
-    t=step([gm,ga.got,gb_.got],index,sa,sb,sv)
-    r_g2=last_step(t,index,zs,ga,gb_)
-    t=r_g2
+    r_g2=last_step([gm],index,zs,ga,gb_)
+    t=r_g2[:1]
     while sa.order: t=step(t,index,sa,sb,sv)
+    t=t+r_g2[1:]
     FF=feed_inner.shape[1]
     if sv.keep.shape[-2]==sa.keep.shape[-2]:
         groups=[last_step(t,index,zs,sa,sb,sv)]

time: 482 us -> 431 us (0.89)
  waiting for transfers between devices: 96.1 us -> 59.6 us
  starting transfers between devices: 54.9 us -> 44.4 us
    ppermute x19, waiting for transfers between devices: 47.3 us -> 12.9 us  [swap(): return lax.ppermute(x, 'dp', [(j, j ^ 1 << bit) for j in range(n)])]
    ppermute x12, starting transfers between devices: 31 us -> 19.9 us  [last_step(): lax.ppermute(s, 'dp', [(j, j ^ m + 1 << zs[0]) for j in range(n)])]
  transfers between devices with their start and end apart: 32 -> 32, of which waited for: 9 -> 9; matrix products, arithmetic and copies ran while one was open for 0% -> 0% of each run, Pallas kernels for 46% -> 53%
where the time goes in v2:
time: 431 us; the launch traced here: 423 us
  Pallas kernels  312 us (72%)
  waiting for transfers between devices  59.6 us (14%)
  starting transfers between devices  44.4 us (10%)
    pallas_call x3, Pallas kernels, attn_bwd(): pl.pallas_call(functools.partial(bwd_kernel, causal, p0, before is not No...  67.2 us
    pallas_call x1, Pallas kernels, mid(): pl.pallas_call(functools.partial(mid_kernel, n), grid=(S // T,), in_specs...  56.7 us
    ppermute x12, waiting for transfers between devices, last_step(): lax.ppermute(s, 'dp', [(j, j ^ m + 1 << zs[0]) for j in range(n)])  46.7 us
    pallas_call x8, Pallas kernels, halve(): pl.pallas_call(functools.partial(halve_kernel, len(chains)), grid_spec=gs...  41.1 us
    pallas_call x2, Pallas kernels, attn_fwd(): pl.pallas_call(functools.partial(fwd_kernel, causal), grid_spec=grid_spec...  35.2 us
    pallas_call x3, Pallas kernels, wgrad_cols(): pl.pallas_call(functools.partial(wcol_kernel, plan), grid=(at,), in_specs...  35 us
    ppermute x12, starting transfers between devices, last_step(): lax.ppermute(s, 'dp', [(j, j ^ m + 1 << zs[0]) for j in range(n)])  19.9 us
    ppermute x19, starting transfers between devices, swap(): return lax.ppermute(x, 'dp', [(j, j ^ 1 << bit) for j in range(n)])  17 us
  transfers between devices with their start and end apart: 32, of which 9 were waited for; matrix products, arithmetic and copies ran while one was open for 0% of the time, Pallas kernels for 53%

profile of v2, /device:TPU:0, one launch (start us, length us, event | category | flops | bytes accessed | tf_op | source)
XLA Modules:
  0.0 423.3 jit_solution(10610000793784444383)
XLA Ops:
  2.0 7.4 %all-to-all-start = ((f32[32,8,128]{2,1,0:T(8,128)}), f32[32,8,128]{2,1,0:T(8,128)}, u32[]{:S(2)}, u32[]{:S(2)}) async-start(f32[32,8,128]{2,1,0:T(8,128)} %broadcast_in_dim.17), calls=%async_computation | async-start | bytes 262144 | tf_op jit(solution)/shard_map/all_to_all | solution.py:625
  10.1 11.9 %pre.1 = (bf16[1024,768]{1,0:T(8,128)(2,1)}, bf16[1024,768]{1,0:T(8,128)(2,1)}, bf16[1024,768]{1,0:T(8,128)(2,1)}, bf16[1024,768]{1,0:T(8,128)(2,1)}, bf16[1024,768]{1,0:T(8,128)(2,1)}) custom-call(bf16[1024,768]{1,0:T(8,128)(2,1)} %bitcast.120, bf16[1024,768]{1,0:T(8,128)(2,1)} %bitcast.139, f32[768]{0:T(1024)} %g_ref.3, f32[768]{0:T(1024)} %b_ref.3, ...), custom_call_target="tpu_custom_call" | custom-call | flops 1207959552000 | bytes 3381657600 | tf_op jit(solution)/shard_map/pre/pallas_call | solution.py:246
  22.0 15.7 %attn_fwd.2 = (bf16[1024,768]{1,0:T(8,128)(2,1)}, f32[6,2,1024]{2,1,0:T(2,128)}) custom-call(s32[1]{0:T(128)S(6)} %copy.91.limit_ref.dec_ref, f32[12]{0:T(128)} %hs_ref.13, f32[12,256]{1,0:T(8,128)} %bias_ref.9, bf16[1024,768]{1,0:T(8,128)(2,1)} %get-tuple-element.217.q_ref, bf16[1024,768]{1,0:T(8,128)(2,1)} %get-tuple-element.218.k_ref, ...), custom_call_target="tpu_custom_call" | custom-call | flops 644245094400 | bytes 1258291200 | tf_op jit(solution)/shard_map/attn_fwd/pallas_call | solution.py:107
  37.7 9.3 %post.1 = (f32[1024,768]{1,0:T(8,128)}, bf16[1024,768]{1,0:T(8,128)(2,1)}, bf16[1024,768]{1,0:T(8,128)(2,1)}, f32[1024,1]{1,0:T(8,128)}) custom-call(bf16[1024,768]{1,0:T(8,128)(2,1)} %get-tuple-element.220.a_ref.refs_5_, bf16[1024,768]{1,0:T(8,128)(2,1)} %bitcast.121, bf16[768,768]{1,0:T(8,128)(2,1)} %wo.3, f32[768]{0:T(1024)} %bo.2, f32[768]{0:T(1024)} %spg.1, ...), custom_call_target="tpu_custom_call" | custom-call | flops 483183820800 | bytes 2359296000 | tf_op jit(solution)/shard_map/post/pallas_call | solution.py:262
  47.0 19.5 %attn_fwd.3 = (bf16[1024,768]{1,0:T(8,128)(2,1)}, f32[6,2,1024]{2,1,0:T(2,128)}) custom-call(s32[1]{0:T(128)S(6)} %copy.92.limit_ref, f32[12]{0:T(128)} %hs_ref.13, f32[12,256]{1,0:T(8,128)} %bias_ref.9, bf16[1024,768]{1,0:T(8,128)(2,1)} %get-tuple-element.221.q_ref, bf16[1024,768]{1,0:T(8,128)(2,1)} %get-tuple-element.222.k_ref, ...), custom_call_target="tpu_custom_call" | custom-call | flops 1288490188800 | bytes 1258291200 | tf_op jit(solution)/shard_map/attn_fwd/pallas_call | solution.py:107
  66.5 56.7 %mid.1 = (bf16[1024,768]{1,0:T(8,128)(2,1)}, f32[1024,768]{1,0:T(8,128)}, bf16[1024,768]{1,0:T(8,128)(2,1)}, bf16[1024,3072]{1,0:T(8,128)(2,1)}, bf16[1024,3072]...) custom-call(s32[1]{0:T(128)S(6)} %copy.91.limit_ref.dec_ref, ...), custom_call_target="tpu_custom_call" | custom-call | flops 4348654387200 | bytes 7785676800 | tf_op jit(solution)/shard_map/mid/pallas_call | solution.py:356
  123.2 13.4 %wgrad.4 = (f32[16,24,3840]{2,1,0:T(8,128)}, f32[16,24,3840]{2,1,0:T(8,128)}) custom-call(s32[1]{0:T(128)S(6)} %and.9.core_ref, f32[8,128]{1,0:T(8,128)} %get-tuple-element.227.fac_ref, bf16[1024,768]{1,0:T(8,128)(2,1)} %get-tuple-element.230.refs_0_, bf16[1024,3072]{1,0:T(8,128)(2,1)} %get-tuple-element.231.refs_1_, ...), custom_call_target="tpu_custom_call" | custom-call | flops 2415919104000 | bytes 3617587200 | tf_op jit(solution)/shard_map/wgrad/pallas_call | solution.py:501
  136.9 10.4 %wgrad.5 = (f32[16,96,768]{2,1,0:T(8,128)}, f32[16,96,768]{2,1,0:T(8,128)}) custom-call(s32[1]{0:T(128)S(6)} %and.9.core_ref, f32[8,128]{1,0:T(8,128)} %get-tuple-element.227.fac_ref, bf16[1024,3072]{1,0:T(8,128)(2,1)} %get-tuple-element.234.l_ref, bf16[1024,768]{1,0:T(8,128)(2,1)} %get-tuple-element.235.r_ref), custom_call_target="tpu_custom_call" | custom-call | flops 1932735283200 | bytes 3460300800 | tf_op jit(solution)/shard_map/wgrad/pallas_call | solution.py:477
  148.2 7.5 %halve.8 = (f32[4,2,24,3840]{3,2,1,0:T(8,128)}, f32[4,2,24,3840]{3,2,1,0:T(8,128)}) custom-call(s32[1]{0:T(128)} %bitcast.7.bit_ref, f32[4,2,2,24,3840]{4,3,2,1,0:T(8,128)} %bitcast.76, f32[4,2,2,24,3840]{4,3,2,1,0:T(8,128)} %bitcast.77, f32[4,2,2,24,3840]{4,3,2,1,0:T(8,128)} %bitcast.9.refs_2_.refs_3_, f32[4,2,2,24,3840]{4,3,2,1,0:T(8,128)} %bitcast.9.refs_2_.refs_3_), custom_call_target="tpu_custom_call" | custom-call | flops 200000 | bytes 200000 | tf_op jit(solution)/shard_map/halve/pallas_call | solution.py:524
  155.7 1.7 collective-permute-start.2
  157.4 5.9 %halve.9 = (f32[8,1,96,768]{3,2,1,0:T(8,128)}, f32[8,1,96,768]{3,2,1,0:T(8,128)}) custom-call(s32[1]{0:T(128)} %bitcast.6.bit_ref, f32[8,2,1,96,768]{4,3,2,1,0:T(8,128)} %bitcast.82, f32[8,2,1,96,768]{4,3,2,1,0:T(8,128)} %bitcast.83, f32[8,2,1,96,768]{4,3,2,1,0:T(8,128)} %bitcast.11.refs_2_.refs_3_, f32[8,2,1,96,768]{4,3,2,1,0:T(8,128)} %bitcast.11.refs_2_.refs_3_), custom_call_target="tpu_custom_call" | custom-call | flops 200000 | bytes 200000 | tf_op jit(solution)/shard_map/halve/pallas_call | solution.py:524
  164.7 37.2 %attn_bwd.3 = (bf16[1024,768]{1,0:T(8,128)(2,1)}, bf16[1024,768]{1,0:T(8,128)(2,1)}, bf16[1024,768]{1,0:T(8,128)(2,1)}, f32[6,2,128]{2,1,0:T(2,128)}) custom-call(s32[1]{0:T(128)S(6)} %copy.92.limit_ref, f32[12]{0:T(128)} %hs_ref.13, f32[12,256]{1,0:T(8,128)} %bias_ref.9, bf16[1024,768]{1,0:T(8,128)(2,1)} %get-tuple-element.221.q_ref, ...), custom_call_target="tpu_custom_call" | custom-call | flops 3221225472000 | bytes 2516582400 | tf_op jit(solution)/shard_map/attn_bwd/pallas_call | solution.py:210
  201.9 12.1 %cross_back.1 = (f32[1024,768]{1,0:T(8,128)}, bf16[1024,768]{1,0:T(8,128)(2,1)}, bf16[1024,768]{1,0:T(8,128)(2,1)}, bf16[1024,768]{1,0:T(8,128)(2,1)}, bf16[1024,768]{1,0:T(8,128)(2,1)}, /*index=5*/f32[8,768]{1,0:T(8,128)}) custom-call(f32[12]{0:T(128)} %hs_ref.13, bf16[1024,768]{1,0:T(8,128)(2,1)} %get-tuple-element.247.gq_ref, ...), custom_call_target="tpu_custom_call" | custom-call | flops 483183820800 | bytes 4875878400 | tf_op jit(solution)/shard_map/cross_back/pallas_call | solution.py:393
  214.1 2.5 collective-permute-done.3
  216.6 3.5 halve.10
  220.4 12.3 %wgrad.6 = (f32[16,24,3072]{2,1,0:T(8,128)}, f32[16,24,3072]{2,1,0:T(8,128)}) custom-call(s32[1]{0:T(128)S(6)} %and.9.core_ref, f32[8,128]{1,0:T(8,128)} %get-tuple-element.227.fac_ref, bf16[1024,768]{1,0:T(8,128)(2,1)} %get-tuple-element.260.refs_0_, bf16[1024,768]{1,0:T(8,128)(2,1)} %get-tuple-element.261.refs_1_, bf16[1024,768]{1,0:T(8,128)(2,1)} %bitcast.140, ...), custom_call_target="tpu_custom_call" | custom-call | flops 1932735283200 | bytes 4089446400 | tf_op jit(solution)/shard_map/wgrad/pallas_call | solution.py:501
  232.7 4.0 halve.11
  236.7 1.7 collective-permute-start.4
  238.4 14.9 %attn_bwd.4 = (bf16[1024,768]{1,0:T(8,128)(2,1)}, bf16[1024,768]{1,0:T(8,128)(2,1)}, bf16[1024,768]{1,0:T(8,128)(2,1)}, f32[6,2,128]{2,1,0:T(2,128)}, f32[6,2,256]{2,1,0:T(2,128)}) custom-call(s32[1]{0:T(128)S(6)} %copy.91.limit_ref.dec_ref, f32[12]{0:T(128)} %hs_ref.13, f32[12,256]{1,0:T(8,128)} %bias_ref.9, bf16[1024,768]{1,0:T(8,128)(2,1)} %get-tuple-element.217.q_ref, ...), custom_call_target="tpu_custom_call" | custom-call | flops 805306368000 | bytes 1258291200 | tf_op jit(solution)/shard_map/attn_bwd/pallas_call | solution.py:210
  253.3 2.6 deal.4
  255.9 2.4 collective-permute-start.10
  259.8 6.7 %halve.12 = (f32[8,1,24,1536]{3,2,1,0:T(8,128)}, f32[8,1,24,1536]{3,2,1,0:T(8,128)}, f32[4,2,24,1536]{3,2,1,0:T(8,128)}, f32[4,2,24,1536]{3,2,1,0:T(8,128)}) custom-call(s32[2]{0:T(128)} %get-tuple-element.434.bit_ref, f32[8,2,1,24,3072]{4,3,2,1,0:T(8,128)} %bitcast.60, f32[8,2,1,24,3072]{4,3,2,1,0:T(8,128)} %bitcast.61, ...), custom_call_target="tpu_custom_call" | custom-call | flops 200000 | bytes 200000 | tf_op jit(solution)/shard_map/halve/pallas_call | solution.py:524
  267.1 5.0 %collective-permute-done.4 = f32[4,1,24,3840]{3,2,0,1:T(8,128)} collective-permute-done((f32[4,1,24,3840]{3,2,0,1:T(8,128)}, f32[4,1,24,3840]{3,2,0,1:T(8,128)}, u32[]{:S(2)}, u32[]{:S(2)}) %collective-permute-start.4) | collective-permute-done | bytes 1474592 | tf_op jit(solution)/shard_map/ppermute | solution.py:571
  272.1 1.7 collective-permute-start.8
  273.8 15.1 %attn_bwd.5 = (bf16[1024,768]{1,0:T(8,128)(2,1)}, bf16[1024,768]{1,0:T(8,128)(2,1)}, bf16[1024,768]{1,0:T(8,128)(2,1)}, f32[6,2,128]{2,1,0:T(2,128)}, f32[6,2,256]{2,1,0:T(2,128)}) custom-call(s32[1]{0:T(128)S(6)} %copy.91.limit_ref.dec_ref, f32[12]{0:T(128)} %hs_ref.13, ...), custom_call_target="tpu_custom_call", output_to_operand_aliasing={{0}: (9, {}), {1}: (10, {}), {2}: (11, {}), {3}: (12, {}), ... | custom-call | flops 805306368000 | bytes 1258291200 | tf_op jit(solution)/shard_map/attn_bwd/pallas_call | solution.py:210
  288.8 3.0 deal.5
  291.8 11.7 %tail.1 = (f32[1024,768]{1,0:T(8,128)}, bf16[1024,768]{1,0:T(8,128)(2,1)}, bf16[1024,768]{1,0:T(8,128)(2,1)}, f32[16,24,128]{2,1,0:T(8,128)}, f32[16,24,128]{2,1,0:T(8,128)}) custom-call(s32[1]{0:T(128)S(6)} %and.9.core_ref, f32[8,128]{1,0:T(8,128)} %get-tuple-element.227.fac_ref, f32[12]{0:T(128)} %hs_ref.13, bf16[1024,768]{1,0:T(8,128)(2,1)} %bitcast.122, ...), custom_call_target="tpu_custom_call" | custom-call | flops 200000 | bytes 200000 | tf_op jit(solution)/shard_map/tail/pallas_call | solution.py:446
  303.5 9.3 %wgrad.7 = (f32[16,24,2304]{2,1,0:T(8,128)}, f32[16,24,2304]{2,1,0:T(8,128)}) custom-call(s32[1]{0:T(128)S(6)} %and.9.core_ref, f32[8,128]{1,0:T(8,128)} %get-tuple-element.227.fac_ref, bf16[1024,768]{1,0:T(8,128)(2,1)} %get-tuple-element.306.refs_0_, bf16[1024,768]{1,0:T(8,128)(2,1)} %get-tuple-element.307.refs_1_, ...), custom_call_target="tpu_custom_call" | custom-call | flops 1449551462400 | bytes 2673868800 | tf_op jit(solution)/shard_map/wgrad/pallas_call | solution.py:501
  312.8 1.5 collective-permute-start.14
  314.4 2.4 collective-permute-start.15
  317.9 4.3 %halve.13 = (f32[4,1,24,1536]{3,2,1,0:T(8,128)}, f32[4,1,24,1536]{3,2,1,0:T(8,128)}, f32[4,1,24,1536]{3,2,1,0:T(8,128)}, f32[4,1,24,1536]{3,2,1,0:T(8,128)}) custom-call(s32[2]{0:T(128)} %get-tuple-element.435.bit_ref, f32[4,2,1,24,1536]{4,3,2,1,0:T(8,128)} %bitcast.112, f32[4,2,1,24,1536]{4,3,2,1,0:T(8,128)} %bitcast.113, ...), custom_call_target="tpu_custom_call" | custom-call | flops 200000 | bytes 200000 | tf_op jit(solution)/shard_map/halve/pallas_call | solution.py:524
  322.6 1.7 collective-permute-start.18
  324.4 5.4 %halve.14 = (f32[8,1,24,1152]{3,2,1,0:T(8,128)}, f32[8,1,24,1152]{3,2,1,0:T(8,128)}, f32[4,2,24,1152]{3,2,1,0:T(8,128)}, f32[4,2,24,1152]{3,2,1,0:T(8,128)}, f32...) custom-call(s32[3]{0:T(128)} %get-tuple-element.436.bit_ref, f32[8,2,1,24,2304]{4,3,2,1,0:T(8,128)} %bitcast.64, ...), custom_call_target="tpu_custom_call" | custom-call | flops 200000 | bytes 200000 | tf_op jit(solution)/shard_map/halve/pallas_call | solution.py:524
  332.7 9.8 %collective-permute-done.15.refs_6_ = f32[24,3840]{1,0:T(8,128)S(1)} collective-permute-done((f32[24,3840]{1,0:T(8,128)S(1)}, f32[24,3840]{1,0:T(8,128)S(1)}, u32[]{:S(2)}, u32[]{:S(2)}) %collective-permute-start.15) | collective-permute-done | bytes 368672 | tf_op jit(solution)/shard_map/ppermute | solution.py:609
  344.6 6.7 %memory.1 = f32[1024,768]{1,0:T(8,128)} custom-call(bf16[1024,768]{1,0:T(8,128)(2,1)} %get-tuple-element.331.refs_4_.k_ref, bf16[1024,768]{1,0:T(8,128)(2,1)} %get-tuple-element.251.gv_ref.refs_3_.v_ref, bf16[768,768]{1,0:T(8,128)(2,1)} %ck.3, bf16[768,768]{1,0:T(8,128)(2,1)} %cv.3), custom_call_target="tpu_custom_call" | custom-call | flops 483183820800 | bytes 1730150400 | tf_op jit(solution)/shard_map/memory/pallas_call | solution.py:457
  351.3 2.8 deal.6
  354.1 5.4 %collective-permute-done.24 = f32[8,1,24,128]{3,2,1,0:T(8,128)} collective-permute-done((f32[8,1,24,128]{3,2,1,0:T(8,128)}, f32[8,1,24,128]{3,2,1,0:T(8,128)}, u32[]{:S(2)}, u32[]{:S(2)}) %collective-permute-start.24) | collective-permute-done | bytes 98336 | tf_op jit(solution)/shard_map/ppermute | solution.py:571
  359.4 4.0 halve.15
  363.4 1.7 collective-permute-start.25
  366.6 1.6 collective-permute-start.19
  368.2 3.8 collective-permute-start.20
  372.0 6.9 %collective-permute-done.19.refs_9_ = f32[24,3072]{1,0:T(8,128)S(1)} collective-permute-done((f32[24,3072]{1,0:T(8,128)S(1)}, f32[24,3072]{1,0:T(8,128)S(1)}, u32[]{:S(2)}, u32[]{:S(2)}) %collective-permute-start.19) | collective-permute-done | bytes 294944 | tf_op jit(solution)/shard_map/ppermute | solution.py:609
  379.1 13.0 %collective-permute-done.20.refs_10_ = f32[24,3072]{1,0:T(8,128)S(1)} collective-permute-done((f32[24,3072]{1,0:T(8,128)S(1)}, f32[24,3072]{1,0:T(8,128)S(1)}, u32[]{:S(2)}, u32[]{:S(2)}) %collective-permute-start.20) | collective-permute-done | bytes 294944 | tf_op jit(solution)/shard_map/ppermute | solution.py:609
  393.1 2.5 deal.7
  395.6 3.8 collective-permute-start.28
  401.8 4.0 collective-permute-done.28.refs_13_
  405.9 11.5 %collective-permute-done.29.refs_14_ = f32[24,2432]{1,0:T(8,128)S(1)} collective-permute-done((f32[24,2432]{1,0:T(8,128)}, f32[24,2432]{1,0:T(8,128)S(1)}, u32[]{:S(2)}, u32[]{:S(2)}) %collective-permute-start.29) | collective-permute-done | bytes 233504 | tf_op jit(solution)/shard_map/ppermute | solution.py:609
  418.2 3.6 finish.1
  (90 shorter events, 19.7 us)
Async XLA Ops:
  2.0 64.5 %all-to-all-start = ((f32[32,8,128]{2,1,0:T(8,128)}), f32[32,8,128]{2,1,0:T(8,128)}, u32[]{:S(2)}, u32[]{:S(2)}) async-start(f32[32,8,128]{2,1,0:T(8,128)} %broadcast_in_dim.17), calls=%async_computation | async-start | bytes 262144 | tf_op jit(solution)/shard_map/all_to_all | solution.py:625
  136.7 11.5 %collective-permute-start.1 = (f32[16,24,3840]{2,1,0:T(8,128)}, f32[16,24,3840]{2,1,0:T(8,128)}, u32[]{:S(2)}, u32[]{:S(2)}) collective-permute-start(f32[16,24,3840]{2,1,0:T(8,128)} %get-tuple-element.233), channel_id=1, source_target_pairs={{0,1},{1,0},{2,3},{3,2},{4,5},{5,4},{6,7},{7,6},{8,9},{9,8},{10,11... | collective-permute-start | bytes 17694728 | tf_op jit(solution)/shard_map/ppermute | solution.py:571
  147.3 10.1 %collective-permute-start = (f32[16,96,768]{2,1,0:T(8,128)}, f32[16,96,768]{2,1,0:T(8,128)}, u32[]{:S(2)}, u32[]{:S(2)}) collective-permute-start(f32[16,96,768]{2,1,0:T(8,128)} %get-tuple-element.237), channel_id=1, source_target_pairs={{0,1},{1,0},{2,3},{3,2},{4,5},{5,4},{6,7},{7,6},{8,9},{9,8},{10,11... | collective-permute-start | bytes 14155784 | tf_op jit(solution)/shard_map/ppermute | solution.py:571
  155.7 77.0 %collective-permute-start.2 = (f32[4,2,24,3840]{3,2,1,0:T(8,128)}, f32[4,2,24,3840]{3,2,1,0:T(8,128)}, u32[]{:S(2)}, u32[]{:S(2)}) collective-permute-start(f32[4,2,24,3840]{3,2,1,0:T(8,128)} %get-tuple-element.241), channel_id=1, source_target_pairs={{0,4},{1,5},{2,6},{3,7},{4,0},{5,1},{6,2},{7,3},{8,12},{9,13},{10,... | collective-permute-start | bytes 8847368 | tf_op jit(solution)/shard_map/ppermute | solution.py:571
  163.3 53.3 %collective-permute-start.3 = (f32[8,1,96,768]{3,2,1,0:T(8,128)}, f32[8,1,96,768]{3,2,1,0:T(8,128)}, u32[]{:S(2)}, u32[]{:S(2)}) collective-permute-start(f32[8,1,96,768]{3,2,1,0:T(8,128)} %get-tuple-element.244), channel_id=1, source_target_pairs={{0,2},{1,3},{2,0},{3,1},{4,6},{5,7},{6,4},{7,5},{8,10},{9,11},{10,... | collective-permute-start | bytes 7077896 | tf_op jit(solution)/shard_map/ppermute | solution.py:571
  220.1 33.2 %collective-permute-start.6 = (f32[4,1,96,768]{3,2,0,1:T(8,128)}, f32[4,1,96,768]{3,2,0,1:T(8,128)}, u32[]{:S(2)}, u32[]{:S(2)}) collective-permute-start(f32[4,1,96,768]{3,2,0,1:T(8,128)} %bitcast.142), channel_id=1, source_target_pairs={{0,4},{1,5},{2,6},{3,7},{4,0},{5,1},{6,2},{7,3},{8,12},{9,13},{10,... | collective-permute-start | bytes 3538952 | tf_op jit(solution)/shard_map/ppermute | solution.py:571
  232.7 27.2 %collective-permute-start.5 = (f32[16,24,3072]{2,1,0:T(8,128)}, f32[16,24,3072]{2,1,0:T(8,128)}, u32[]{:S(2)}, u32[]{:S(2)}) collective-permute-start(f32[16,24,3072]{2,1,0:T(8,128)} %get-tuple-element.264), channel_id=1, source_target_pairs={{0,1},{1,0},{2,3},{3,2},{4,5},{5,4},{6,7},{7,6},{8,9},{9,8},{10,11... | collective-permute-start | bytes 14155784 | tf_op jit(solution)/shard_map/ppermute | solution.py:571
  236.7 35.4 %collective-permute-start.4 = (f32[4,1,24,3840]{3,2,0,1:T(8,128)}, f32[4,1,24,3840]{3,2,0,1:T(8,128)}, u32[]{:S(2)}, u32[]{:S(2)}) collective-permute-start(f32[4,1,24,3840]{3,2,0,1:T(8,128)} %bitcast.141), channel_id=1, source_target_pairs={{0,2},{1,3},{2,0},{3,1},{4,6},{5,7},{6,4},{7,5},{8,10},{9,11},{10,... | collective-permute-start | bytes 4423688 | tf_op jit(solution)/shard_map/ppermute | solution.py:571
  255.9 47.5 %collective-permute-start.10 = (f32[96,768]{1,0:T(8,128)}, f32[96,768]{1,0:T(8,128)}, u32[]{:S(2)}, u32[]{:S(2)}) collective-permute-start(f32[96,768]{1,0:T(8,128)} %get-tuple-element.304), channel_id=1, source_target_pairs={{0,16},{1,17},{2,18},{3,19},{4,20},{5,21},{6,22},{7,23},{8,24},{9,... | collective-permute-start | bytes 884744 | tf_op jit(solution)/shard_map/ppermute | solution.py:609
  258.3 45.2 %collective-permute-start.11 = (f32[96,768]{1,0:T(8,128)}, f32[96,768]{1,0:T(8,128)}, u32[]{:S(2)}, u32[]{:S(2)}) collective-permute-start(f32[96,768]{1,0:T(8,128)} %get-tuple-element.305), channel_id=1, source_target_pairs={{0,24},{1,25},{2,26},{3,27},{4,28},{5,29},{6,30},{7,31},{8,16},{9,... | collective-permute-start | bytes 884744 | tf_op jit(solution)/shard_map/ppermute | solution.py:609
  259.8 43.7 %collective-permute-start.9 = (f32[96,768]{1,0:T(8,128)}, f32[96,768]{1,0:T(8,128)}, u32[]{:S(2)}, u32[]{:S(2)}) collective-permute-start(f32[96,768]{1,0:T(8,128)} %get-tuple-element.303), channel_id=1, source_target_pairs={{0,8},{1,9},{2,10},{3,11},{4,12},{5,13},{6,14},{7,15},{8,0},{9,1},... | collective-permute-start | bytes 884744 | tf_op jit(solution)/shard_map/ppermute | solution.py:609
  266.5 37.0 %collective-permute-start.7 = (f32[8,1,24,1536]{3,2,1,0:T(8,128)}, f32[8,1,24,1536]{3,2,1,0:T(8,128)}, u32[]{:S(2)}, u32[]{:S(2)}) collective-permute-start(f32[8,1,24,1536]{3,2,1,0:T(8,128)} %get-tuple-element.282), channel_id=1, source_target_pairs={{0,2},{1,3},{2,0},{3,1},{4,6},{5,7},{6,4},{7,5},{8,10},{9,11},{10,... | collective-permute-start | bytes 3538952 | tf_op jit(solution)/shard_map/ppermute | solution.py:571
  272.1 31.4 %collective-permute-start.8 = (f32[4,2,24,1536]{3,2,1,0:T(8,128)}, f32[4,2,24,1536]{3,2,1,0:T(8,128)}, u32[]{:S(2)}, u32[]{:S(2)}) collective-permute-start(f32[4,2,24,1536]{3,2,1,0:T(8,128)} %get-tuple-element.283), channel_id=1, source_target_pairs={{0,4},{1,5},{2,6},{3,7},{4,0},{5,1},{6,2},{7,3},{8,12},{9,13},{10,... | collective-permute-start | bytes 3538952 | tf_op jit(solution)/shard_map/ppermute | solution.py:571
  303.5 9.3 %copy-start.16 = (f32[24,3840]{1,0:T(8,128)S(1)}, f32[24,3840]{1,0:T(8,128)}, u32[]{:S(2)}) copy-start(f32[24,3840]{1,0:T(8,128)} %get-tuple-element.328) | copy-start | bytes 1105924
  303.5 10.8 %copy-start.15 = (f32[24,3840]{1,0:T(8,128)S(1)}, f32[24,3840]{1,0:T(8,128)}, u32[]{:S(2)}) copy-start(f32[24,3840]{1,0:T(8,128)} %get-tuple-element.329) | copy-start | bytes 1105924
  303.5 13.3 %copy-start.14 = (f32[24,3840]{1,0:T(8,128)S(1)}, f32[24,3840]{1,0:T(8,128)}, u32[]{:S(2)}) copy-start(f32[24,3840]{1,0:T(8,128)} %get-tuple-element.330) | copy-start | bytes 1105924
  303.5 13.7 %copy-start.20 = (f32[16,24,128]{2,1,0:T(8,128)S(1)}, f32[16,24,128]{2,1,0:T(8,128)}, u32[]{:S(2)}) copy-start(f32[16,24,128]{2,1,0:T(8,128)} %get-tuple-element.302) | copy-start | bytes 589828
  312.8 9.8 %collective-permute-start.12 = (f32[16,24,2304]{2,1,0:T(8,128)}, f32[16,24,2304]{2,1,0:T(8,128)S(1)}, u32[]{:S(2)}, u32[]{:S(2)}) collective-permute-start(f32[16,24,2304]{2,1,0:T(8,128)} %get-tuple-element.309), channel_id=1, source_target_pairs={{0,1},{1,0},{2,3},{3,2},{4,5},{5,4},{6,7},{7,6},{8,9},{9,8},{10,11... | collective-permute-start | bytes 10616840 | tf_op jit(solution)/shard_map/ppermute | solution.py:571
  312.8 18.4 %collective-permute-start.14 = (f32[24,3840]{1,0:T(8,128)S(1)}, f32[24,3840]{1,0:T(8,128)S(1)}, u32[]{:S(2)}, u32[]{:S(2)}) collective-permute-start(f32[24,3840]{1,0:T(8,128)S(1)} %copy-done.16), channel_id=1, source_target_pairs={{0,8},{1,9},{2,10},{3,11},{4,12},{5,13},{6,14},{7,15},{8,0},{9,1},... | collective-permute-start | bytes 1105928 | tf_op jit(solution)/shard_map/ppermute | solution.py:609
  314.4 28.2 %collective-permute-start.15 = (f32[24,3840]{1,0:T(8,128)S(1)}, f32[24,3840]{1,0:T(8,128)S(1)}, u32[]{:S(2)}, u32[]{:S(2)}) collective-permute-start(f32[24,3840]{1,0:T(8,128)S(1)} %copy-done.15), channel_id=1, source_target_pairs={{0,16},{1,17},{2,18},{3,19},{4,20},{5,21},{6,22},{7,23},{8,24},{9,... | collective-permute-start | bytes 1105928 | tf_op jit(solution)/shard_map/ppermute | solution.py:609
  316.8 26.3 %collective-permute-start.16 = (f32[24,3840]{1,0:T(8,128)S(1)}, f32[24,3840]{1,0:T(8,128)S(1)}, u32[]{:S(2)}, u32[]{:S(2)}) collective-permute-start(f32[24,3840]{1,0:T(8,128)S(1)} %copy-done.14), channel_id=1, source_target_pairs={{0,24},{1,25},{2,26},{3,27},{4,28},{5,29},{6,30},{7,31},{8,16},{9,... | collective-permute-start | bytes 1105928 | tf_op jit(solution)/shard_map/ppermute | solution.py:609
  317.3 4.9 %collective-permute-start.13 = (f32[16,24,128]{2,1,0:T(8,128)S(1)}, f32[16,24,128]{2,1,0:T(8,128)S(1)}, u32[]{:S(2)}, u32[]{:S(2)}) collective-permute-start(f32[16,24,128]{2,1,0:T(8,128)S(1)} %copy-done.20), channel_id=1, source_target_pairs={{0,1},{1,0},{2,3},{3,2},{4,5},{5,4},{6,7},{7,6},{8,9},{9,8},{10,11... | collective-permute-start | bytes 589832 | tf_op jit(solution)/shard_map/ppermute | solution.py:571
  322.1 2.1 copy-start.3
  322.2 29.1 %collective-permute-start.17 = (f32[4,1,24,1536]{3,2,0,1:T(8,128)}, f32[4,1,24,1536]{3,2,0,1:T(8,128)}, u32[]{:S(2)}, u32[]{:S(2)}) collective-permute-start(f32[4,1,24,1536]{3,2,0,1:T(8,128)} %bitcast.144), channel_id=1, source_target_pairs={{0,4},{1,5},{2,6},{3,7},{4,0},{5,1},{6,2},{7,3},{8,12},{9,13},{10,... | collective-permute-start | bytes 1769480 | tf_op jit(solution)/shard_map/ppermute | solution.py:571
  322.6 1.8 copy-start
  322.6 28.7 %collective-permute-start.18 = (f32[4,1,24,1536]{3,2,0,1:T(8,128)}, f32[4,1,24,1536]{3,2,0,1:T(8,128)}, u32[]{:S(2)}, u32[]{:S(2)}) collective-permute-start(f32[4,1,24,1536]{3,2,0,1:T(8,128)} %bitcast.143), channel_id=1, source_target_pairs={{0,2},{1,3},{2,0},{3,1},{4,6},{5,7},{6,4},{7,5},{8,10},{9,11},{10,... | collective-permute-start | bytes 1769480 | tf_op jit(solution)/shard_map/ppermute | solution.py:571
  331.2 20.0 %copy-start.5 = (f32[24,3840]{1,0:T(8,128)}, f32[24,3840]{1,0:T(8,128)S(1)}, u32[]{:S(2)}) copy-start(f32[24,3840]{1,0:T(8,128)S(1)} %collective-permute-done.14.refs_5_) | copy-start | bytes 1105924
  331.2 28.2 %collective-permute-start.22 = (f32[8,1,24,1152]{3,2,1,0:T(8,128)}, f32[8,1,24,1152]{3,2,1,0:T(8,128)}, u32[]{:S(2)}, u32[]{:S(2)}) collective-permute-start(f32[8,1,24,1152]{3,2,1,0:T(8,128)} %get-tuple-element.325), channel_id=1, source_target_pairs={{0,2},{1,3},{2,0},{3,1},{4,6},{5,7},{6,4},{7,5},{8,10},{9,11},{10,... | collective-permute-start | bytes 2654216 | tf_op jit(solution)/shard_map/ppermute | solution.py:571
  342.5 8.7 %copy-start.6 = (f32[24,3840]{1,0:T(8,128)}, f32[24,3840]{1,0:T(8,128)S(1)}, u32[]{:S(2)}) copy-start(f32[24,3840]{1,0:T(8,128)S(1)} %collective-permute-done.15.refs_6_) | copy-start | bytes 1105924
  342.5 16.9 %collective-permute-start.23 = (f32[4,2,24,1152]{3,2,1,0:T(8,128)}, f32[4,2,24,1152]{3,2,1,0:T(8,128)}, u32[]{:S(2)}, u32[]{:S(2)}) collective-permute-start(f32[4,2,24,1152]{3,2,1,0:T(8,128)} %get-tuple-element.326), channel_id=1, source_target_pairs={{0,4},{1,5},{2,6},{3,7},{4,0},{5,1},{6,2},{7,3},{8,12},{9,13},{10,... | collective-permute-start | bytes 2654216 | tf_op jit(solution)/shard_map/ppermute | solution.py:571
  343.1 8.2 %copy-start.7 = (f32[24,3840]{1,0:T(8,128)}, f32[24,3840]{1,0:T(8,128)S(1)}, u32[]{:S(2)}) copy-start(f32[24,3840]{1,0:T(8,128)S(1)} %collective-permute-done.16.refs_7_) | copy-start | bytes 1105924
  343.1 16.3 %collective-permute-start.24 = (f32[8,1,24,128]{3,2,1,0:T(8,128)}, f32[8,1,24,128]{3,2,1,0:T(8,128)}, u32[]{:S(2)}, u32[]{:S(2)}) collective-permute-start(f32[8,1,24,128]{3,2,1,0:T(8,128)} %get-tuple-element.327), channel_id=1, source_target_pairs={{0,2},{1,3},{2,0},{3,1},{4,6},{5,7},{6,4},{7,5},{8,10},{9,11},{10,... | collective-permute-start | bytes 294920 | tf_op jit(solution)/shard_map/ppermute | solution.py:571
  354.1 12.5 %copy-start.19 = (f32[24,3072]{1,0:T(8,128)S(1)}, f32[24,3072]{1,0:T(8,128)}, u32[]{:S(2)}) copy-start(f32[24,3072]{1,0:T(8,128)} %get-tuple-element.339) | copy-start | bytes 884740
  354.1 14.1 %copy-start.18 = (f32[24,3072]{1,0:T(8,128)S(1)}, f32[24,3072]{1,0:T(8,128)}, u32[]{:S(2)}) copy-start(f32[24,3072]{1,0:T(8,128)} %get-tuple-element.340) | copy-start | bytes 884740
  354.1 17.9 %copy-start.17 = (f32[24,3072]{1,0:T(8,128)S(1)}, f32[24,3072]{1,0:T(8,128)}, u32[]{:S(2)}) copy-start(f32[24,3072]{1,0:T(8,128)} %get-tuple-element.341) | copy-start | bytes 884740
  363.4 28.7 %collective-permute-start.25 = (f32[4,1,24,1152]{3,2,0,1:T(8,128)}, f32[4,1,24,1152]{3,2,0,1:T(8,128)S(1)}, u32[]{:S(2)}, u32[]{:S(2)}) collective-permute-start(f32[4,1,24,1152]{3,2,0,1:T(8,128)} %bitcast.146), channel_id=1, source_target_pairs={{0,4},{1,5},{2,6},{3,7},{4,0},{5,1},{6,2},{7,3},{8,12},{9,13},{10,... | collective-permute-start | bytes 1327112 | tf_op jit(solution)/shard_map/ppermute | solution.py:571
  365.1 27.0 %collective-permute-start.26 = (f32[4,1,24,1152]{3,2,0,1:T(8,128)}, f32[4,1,24,1152]{3,2,0,1:T(8,128)S(1)}, u32[]{:S(2)}, u32[]{:S(2)}) collective-permute-start(f32[4,1,24,1152]{3,2,0,1:T(8,128)} %bitcast.145), channel_id=1, source_target_pairs={{0,2},{1,3},{2,0},{3,1},{4,6},{5,7},{6,4},{7,5},{8,10},{9,11},{10,... | collective-permute-start | bytes 1327112 | tf_op jit(solution)/shard_map/ppermute | solution.py:571
  366.6 12.2 %collective-permute-start.19 = (f32[24,3072]{1,0:T(8,128)S(1)}, f32[24,3072]{1,0:T(8,128)S(1)}, u32[]{:S(2)}, u32[]{:S(2)}) collective-permute-start(f32[24,3072]{1,0:T(8,128)S(1)} %copy-done.19), channel_id=1, source_target_pairs={{0,8},{1,9},{2,10},{3,11},{4,12},{5,13},{6,14},{7,15},{8,0},{9,1},... | collective-permute-start | bytes 884744 | tf_op jit(solution)/shard_map/ppermute | solution.py:609
  368.2 23.9 %collective-permute-start.20 = (f32[24,3072]{1,0:T(8,128)S(1)}, f32[24,3072]{1,0:T(8,128)S(1)}, u32[]{:S(2)}, u32[]{:S(2)}) collective-permute-start(f32[24,3072]{1,0:T(8,128)S(1)} %copy-done.18), channel_id=1, source_target_pairs={{0,16},{1,17},{2,18},{3,19},{4,20},{5,21},{6,22},{7,23},{8,24},{9,... | collective-permute-start | bytes 884744 | tf_op jit(solution)/shard_map/ppermute | solution.py:609
  372.0 20.1 %collective-permute-start.21 = (f32[24,3072]{1,0:T(8,128)S(1)}, f32[24,3072]{1,0:T(8,128)S(1)}, u32[]{:S(2)}, u32[]{:S(2)}) collective-permute-start(f32[24,3072]{1,0:T(8,128)S(1)} %copy-done.17), channel_id=1, source_target_pairs={{0,24},{1,25},{2,26},{3,27},{4,28},{5,29},{6,30},{7,31},{8,16},{9,... | collective-permute-start | bytes 884744 | tf_op jit(solution)/shard_map/ppermute | solution.py:609
  378.8 38.5 %copy-start.8 = (f32[24,3072]{1,0:T(8,128)}, f32[24,3072]{1,0:T(8,128)S(1)}, u32[]{:S(2)}) copy-start(f32[24,3072]{1,0:T(8,128)S(1)} %collective-permute-done.19.refs_9_) | copy-start | bytes 884740
  378.8 13.3 %collective-permute-start.27 = (f32[4,1,24,128]{3,2,0,1:T(8,128)}, f32[4,1,24,128]{3,2,0,1:T(8,128)S(1)}, u32[]{:S(2)}, u32[]{:S(2)}) collective-permute-start(f32[4,1,24,128]{3,2,0,1:T(8,128)} %bitcast.147), channel_id=1, source_target_pairs={{0,4},{1,5},{2,6},{3,7},{4,0},{5,1},{6,2},{7,3},{8,12},{9,13},{10,... | collective-permute-start | bytes 147464 | tf_op jit(solution)/shard_map/ppermute | solution.py:571
  392.1 25.3 %copy-start.9 = (f32[24,3072]{1,0:T(8,128)}, f32[24,3072]{1,0:T(8,128)S(1)}, u32[]{:S(2)}) copy-start(f32[24,3072]{1,0:T(8,128)S(1)} %collective-permute-done.20.refs_10_) | copy-start | bytes 884740
  392.1 25.3 %copy-start.10 = (f32[24,3072]{1,0:T(8,128)}, f32[24,3072]{1,0:T(8,128)S(1)}, u32[]{:S(2)}) copy-start(f32[24,3072]{1,0:T(8,128)S(1)} %collective-permute-done.21.refs_11_) | copy-start | bytes 884740
  395.6 10.2 %collective-permute-start.28 = (f32[24,2432]{1,0:T(8,128)}, f32[24,2432]{1,0:T(8,128)S(1)}, u32[]{:S(2)}, u32[]{:S(2)}) collective-permute-start(f32[24,2432]{1,0:T(8,128)} %get-tuple-element.364), channel_id=1, source_target_pairs={{0,8},{1,9},{2,10},{3,11},{4,12},{5,13},{6,14},{7,15},{8,0},{9,1},... | collective-permute-start | bytes 700424 | tf_op jit(solution)/shard_map/ppermute | solution.py:609
  399.4 17.9 %collective-permute-start.29 = (f32[24,2432]{1,0:T(8,128)}, f32[24,2432]{1,0:T(8,128)S(1)}, u32[]{:S(2)}, u32[]{:S(2)}) collective-permute-start(f32[24,2432]{1,0:T(8,128)} %get-tuple-element.365), channel_id=1, source_target_pairs={{0,16},{1,17},{2,18},{3,19},{4,20},{5,21},{6,22},{7,23},{8,24},{9,... | collective-permute-start | bytes 700424 | tf_op jit(solution)/shard_map/ppermute | solution.py:609
  400.4 16.9 %collective-permute-start.30 = (f32[24,2432]{1,0:T(8,128)}, f32[24,2432]{1,0:T(8,128)S(1)}, u32[]{:S(2)}, u32[]{:S(2)}) collective-permute-start(f32[24,2432]{1,0:T(8,128)} %get-tuple-element.366), channel_id=1, source_target_pairs={{0,24},{1,25},{2,26},{3,27},{4,28},{5,29},{6,30},{7,31},{8,16},{9,... | collective-permute-start | bytes 700424 | tf_op jit(solution)/shard_map/ppermute | solution.py:609
  405.9 11.5 %copy-start.11 = (f32[24,2432]{1,0:T(8,128)}, f32[24,2432]{1,0:T(8,128)S(1)}, u32[]{:S(2)}) copy-start(f32[24,2432]{1,0:T(8,128)S(1)} %collective-permute-done.28.refs_13_) | copy-start | bytes 700420
  (5 other events, 4.0 us)

commit v3 on v2

--- a/solution.py
+++ b/solution.py
@@ -266,15 +266,15 @@
 SQH=0.7071067811865476
 ERFC=(-1.26551223,1.00002368,0.37409196,0.09678418,-0.18628806,0.27886807,-1.13520398,1.48851587,-0.82215223,0.17087277)
 def gelu_parts(f):
-    z=jnp.abs(f)*SQH
-    t=1.0/(1.0+0.5*z)
+    t=1.0/(1.0+jnp.abs(f)*(0.5*SQH))
     poly=jnp.full_like(t,ERFC[9]*LOG2E)
-    for c in ERFC[8::-1]:
+    for c in ERFC[8:0:-1]:
         poly=poly*t+c*LOG2E
-    zz=z*z*LOG2E
-    half=0.5*t*jnp.exp2(poly-zz)
+    poly=poly*t+(ERFC[0]*LOG2E-1.0)
+    zz=f*f*(0.5*LOG2E)
+    half=t*jnp.exp2(poly-zz)
     phi=jnp.where(f<0.0,half,1.0-half)
-    dens=jnp.exp2(-zz)*0.3989422804014327
+    dens=jnp.exp2(-1.3257480647361595-zz)
     return f*phi, phi+f*dens
 
 CH=256
@@ -511,7 +511,7 @@
 def halve(bits,chains):
     specs=[];ins=[];outs=[];shapes=[]
     size=sum(4*keep.size//parts for keep,got,part,parts in chains)
-    steps=min([4 if size>8e6 else 2]+[keep.shape[0] for keep,*_ in chains])
+    steps=min([4 if size>8e6 else 2 if size>3e6 else 1]+[keep.shape[0] for keep,*_ in chains])
     for c,(keep,got,part,parts) in enumerate(chains):
         A,_,B,r,C=keep.shape
         C=C//parts; K=A//steps

time: 431 us -> 431 us (level)
  no operation moved by 1% of the time
where the time goes in v3:
time: 431 us; the launch traced here: 423 us
  Pallas kernels  312 us (72%)
  waiting for transfers between devices  60 us (14%)
  starting transfers between devices  43.9 us (10%)
    pallas_call x3, Pallas kernels, attn_bwd(): pl.pallas_call(functools.partial(bwd_kernel, causal, p0, before is not No...  67.2 us
    pallas_call x1, Pallas kernels, mid(): pl.pallas_call(functools.partial(mid_kernel, n), grid=(S // T,), in_specs...  55.5 us
    ppermute x12, waiting for transfers between devices, last_step(): lax.ppermute(s, 'dp', [(j, j ^ m + 1 << zs[0]) for j in range(n)])  46.7 us
    pallas_call x8, Pallas kernels, halve(): pl.pallas_call(functools.partial(halve_kernel, len(chains)), grid_spec=gs...  42.3 us
    pallas_call x2, Pallas kernels, attn_fwd(): pl.pallas_call(functools.partial(fwd_kernel, causal), grid_spec=grid_spec...  35.2 us
    pallas_call x3, Pallas kernels, wgrad_cols(): pl.pallas_call(functools.partial(wcol_kernel, plan), grid=(at,), in_specs...  35 us
    ppermute x12, starting transfers between devices, last_step(): lax.ppermute(s, 'dp', [(j, j ^ m + 1 << zs[0]) for j in range(n)])  19.5 us
    ppermute x19, starting transfers between devices, swap(): return lax.ppermute(x, 'dp', [(j, j ^ 1 << bit) for j in range(n)])  17 us
  transfers between devices with their start and end apart: 32, of which 9 were waited for; matrix products, arithmetic and copies ran while one was open for 0% of the time, Pallas kernels for 53%

profile of v3, /device:TPU:0, one launch (start us, length us, event | category | flops | bytes accessed | tf_op | source)
XLA Modules:
  0.0 423.2 jit_solution(12214902232573366074)
XLA Ops:
  2.0 7.4 %all-to-all-start = ((f32[32,8,128]{2,1,0:T(8,128)}), f32[32,8,128]{2,1,0:T(8,128)}, u32[]{:S(2)}, u32[]{:S(2)}) async-start(f32[32,8,128]{2,1,0:T(8,128)} %broadcast_in_dim.17), calls=%async_computation | async-start | bytes 262144 | tf_op jit(solution)/shard_map/all_to_all | solution.py:625
  10.1 11.9 %pre.1 = (bf16[1024,768]{1,0:T(8,128)(2,1)}, bf16[1024,768]{1,0:T(8,128)(2,1)}, bf16[1024,768]{1,0:T(8,128)(2,1)}, bf16[1024,768]{1,0:T(8,128)(2,1)}, bf16[1024,768]{1,0:T(8,128)(2,1)}) custom-call(bf16[1024,768]{1,0:T(8,128)(2,1)} %bitcast.120, bf16[1024,768]{1,0:T(8,128)(2,1)} %bitcast.139, f32[768]{0:T(1024)} %g_ref.3, f32[768]{0:T(1024)} %b_ref.3, ...), custom_call_target="tpu_custom_call" | custom-call | flops 1207959552000 | bytes 3381657600 | tf_op jit(solution)/shard_map/pre/pallas_call | solution.py:246
  22.0 15.7 %attn_fwd.2 = (bf16[1024,768]{1,0:T(8,128)(2,1)}, f32[6,2,1024]{2,1,0:T(2,128)}) custom-call(s32[1]{0:T(128)S(6)} %copy.91.limit_ref.dec_ref, f32[12]{0:T(128)} %hs_ref.13, f32[12,256]{1,0:T(8,128)} %bias_ref.9, bf16[1024,768]{1,0:T(8,128)(2,1)} %get-tuple-element.217.q_ref, bf16[1024,768]{1,0:T(8,128)(2,1)} %get-tuple-element.218.k_ref, ...), custom_call_target="tpu_custom_call" | custom-call | flops 644245094400 | bytes 1258291200 | tf_op jit(solution)/shard_map/attn_fwd/pallas_call | solution.py:107
  37.7 9.3 %post.1 = (f32[1024,768]{1,0:T(8,128)}, bf16[1024,768]{1,0:T(8,128)(2,1)}, bf16[1024,768]{1,0:T(8,128)(2,1)}, f32[1024,1]{1,0:T(8,128)}) custom-call(bf16[1024,768]{1,0:T(8,128)(2,1)} %get-tuple-element.220.a_ref.refs_5_, bf16[1024,768]{1,0:T(8,128)(2,1)} %bitcast.121, bf16[768,768]{1,0:T(8,128)(2,1)} %wo.3, f32[768]{0:T(1024)} %bo.2, f32[768]{0:T(1024)} %spg.1, ...), custom_call_target="tpu_custom_call" | custom-call | flops 483183820800 | bytes 2359296000 | tf_op jit(solution)/shard_map/post/pallas_call | solution.py:262
  47.0 19.5 %attn_fwd.3 = (bf16[1024,768]{1,0:T(8,128)(2,1)}, f32[6,2,1024]{2,1,0:T(2,128)}) custom-call(s32[1]{0:T(128)S(6)} %copy.92.limit_ref, f32[12]{0:T(128)} %hs_ref.13, f32[12,256]{1,0:T(8,128)} %bias_ref.9, bf16[1024,768]{1,0:T(8,128)(2,1)} %get-tuple-element.221.q_ref, bf16[1024,768]{1,0:T(8,128)(2,1)} %get-tuple-element.222.k_ref, ...), custom_call_target="tpu_custom_call" | custom-call | flops 1288490188800 | bytes 1258291200 | tf_op jit(solution)/shard_map/attn_fwd/pallas_call | solution.py:107
  66.5 55.5 %mid.1 = (bf16[1024,768]{1,0:T(8,128)(2,1)}, f32[1024,768]{1,0:T(8,128)}, bf16[1024,768]{1,0:T(8,128)(2,1)}, bf16[1024,3072]{1,0:T(8,128)(2,1)}, bf16[1024,3072]...) custom-call(s32[1]{0:T(128)S(6)} %copy.91.limit_ref.dec_ref, ...), custom_call_target="tpu_custom_call" | custom-call | flops 4348654387200 | bytes 7785676800 | tf_op jit(solution)/shard_map/mid/pallas_call | solution.py:356
  122.0 13.4 %wgrad.4 = (f32[16,24,3840]{2,1,0:T(8,128)}, f32[16,24,3840]{2,1,0:T(8,128)}) custom-call(s32[1]{0:T(128)S(6)} %and.9.core_ref, f32[8,128]{1,0:T(8,128)} %get-tuple-element.227.fac_ref, bf16[1024,768]{1,0:T(8,128)(2,1)} %get-tuple-element.230.refs_0_, bf16[1024,3072]{1,0:T(8,128)(2,1)} %get-tuple-element.231.refs_1_, ...), custom_call_target="tpu_custom_call" | custom-call | flops 2415919104000 | bytes 3617587200 | tf_op jit(solution)/shard_map/wgrad/pallas_call | solution.py:501
  135.6 10.4 %wgrad.5 = (f32[16,96,768]{2,1,0:T(8,128)}, f32[16,96,768]{2,1,0:T(8,128)}) custom-call(s32[1]{0:T(128)S(6)} %and.9.core_ref, f32[8,128]{1,0:T(8,128)} %get-tuple-element.227.fac_ref, bf16[1024,3072]{1,0:T(8,128)(2,1)} %get-tuple-element.234.l_ref, bf16[1024,768]{1,0:T(8,128)(2,1)} %get-tuple-element.235.r_ref), custom_call_target="tpu_custom_call" | custom-call | flops 1932735283200 | bytes 3460300800 | tf_op jit(solution)/shard_map/wgrad/pallas_call | solution.py:477
  146.9 7.5 %halve.8 = (f32[4,2,24,3840]{3,2,1,0:T(8,128)}, f32[4,2,24,3840]{3,2,1,0:T(8,128)}) custom-call(s32[1]{0:T(128)} %bitcast.7.bit_ref, f32[4,2,2,24,3840]{4,3,2,1,0:T(8,128)} %bitcast.76, f32[4,2,2,24,3840]{4,3,2,1,0:T(8,128)} %bitcast.77, f32[4,2,2,24,3840]{4,3,2,1,0:T(8,128)} %bitcast.9.refs_2_.refs_3_, f32[4,2,2,24,3840]{4,3,2,1,0:T(8,128)} %bitcast.9.refs_2_.refs_3_), custom_call_target="tpu_custom_call" | custom-call | flops 200000 | bytes 200000 | tf_op jit(solution)/shard_map/halve/pallas_call | solution.py:524
  154.4 1.7 collective-permute-start.2
  156.1 5.9 %halve.9 = (f32[8,1,96,768]{3,2,1,0:T(8,128)}, f32[8,1,96,768]{3,2,1,0:T(8,128)}) custom-call(s32[1]{0:T(128)} %bitcast.6.bit_ref, f32[8,2,1,96,768]{4,3,2,1,0:T(8,128)} %bitcast.82, f32[8,2,1,96,768]{4,3,2,1,0:T(8,128)} %bitcast.83, f32[8,2,1,96,768]{4,3,2,1,0:T(8,128)} %bitcast.11.refs_2_.refs_3_, f32[8,2,1,96,768]{4,3,2,1,0:T(8,128)} %bitcast.11.refs_2_.refs_3_), custom_call_target="tpu_custom_call" | custom-call | flops 200000 | bytes 200000 | tf_op jit(solution)/shard_map/halve/pallas_call | solution.py:524
  163.5 37.2 %attn_bwd.3 = (bf16[1024,768]{1,0:T(8,128)(2,1)}, bf16[1024,768]{1,0:T(8,128)(2,1)}, bf16[1024,768]{1,0:T(8,128)(2,1)}, f32[6,2,128]{2,1,0:T(2,128)}) custom-call(s32[1]{0:T(128)S(6)} %copy.92.limit_ref, f32[12]{0:T(128)} %hs_ref.13, f32[12,256]{1,0:T(8,128)} %bias_ref.9, bf16[1024,768]{1,0:T(8,128)(2,1)} %get-tuple-element.221.q_ref, ...), custom_call_target="tpu_custom_call" | custom-call | flops 3221225472000 | bytes 2516582400 | tf_op jit(solution)/shard_map/attn_bwd/pallas_call | solution.py:210
  200.7 12.1 %cross_back.1 = (f32[1024,768]{1,0:T(8,128)}, bf16[1024,768]{1,0:T(8,128)(2,1)}, bf16[1024,768]{1,0:T(8,128)(2,1)}, bf16[1024,768]{1,0:T(8,128)(2,1)}, bf16[1024,768]{1,0:T(8,128)(2,1)}, /*index=5*/f32[8,768]{1,0:T(8,128)}) custom-call(f32[12]{0:T(128)} %hs_ref.13, bf16[1024,768]{1,0:T(8,128)(2,1)} %get-tuple-element.247.gq_ref, ...), custom_call_target="tpu_custom_call" | custom-call | flops 483183820800 | bytes 4875878400 | tf_op jit(solution)/shard_map/cross_back/pallas_call | solution.py:393
  212.8 2.5 collective-permute-done.3
  215.3 3.8 halve.10
  219.5 12.3 %wgrad.6 = (f32[16,24,3072]{2,1,0:T(8,128)}, f32[16,24,3072]{2,1,0:T(8,128)}) custom-call(s32[1]{0:T(128)S(6)} %and.9.core_ref, f32[8,128]{1,0:T(8,128)} %get-tuple-element.227.fac_ref, bf16[1024,768]{1,0:T(8,128)(2,1)} %get-tuple-element.260.refs_0_, bf16[1024,768]{1,0:T(8,128)(2,1)} %get-tuple-element.261.refs_1_, bf16[1024,768]{1,0:T(8,128)(2,1)} %bitcast.140, ...), custom_call_target="tpu_custom_call" | custom-call | flops 1932735283200 | bytes 4089446400 | tf_op jit(solution)/shard_map/wgrad/pallas_call | solution.py:501
  231.8 4.5 %halve.11 = (f32[4,1,24,3840]{3,2,1,0:T(8,128)}, f32[4,1,24,3840]{3,2,1,0:T(8,128)}) custom-call(s32[1]{0:T(128)} %bitcast.6.bit_ref, f32[4,2,1,24,3840]{4,3,2,1,0:T(8,128)} %bitcast.84, f32[4,2,1,24,3840]{4,3,2,1,0:T(8,128)} %bitcast.85, f32[4,2,1,24,3840]{4,3,2,1,0:T(8,128)} %bitcast.16.refs_2_.refs_3_, f32[4,2,1,24,3840]{4,3,2,1,0:T(8,128)} %bitcast.16.refs_2_.refs_3_), custom_call_target="tpu_custom_call" | custom-call | flops 200000 | bytes 200000 | tf_op jit(solution)/shard_map/halve/pallas_call | solution.py:524
  236.3 1.7 collective-permute-start.4
  238.0 14.9 %attn_bwd.4 = (bf16[1024,768]{1,0:T(8,128)(2,1)}, bf16[1024,768]{1,0:T(8,128)(2,1)}, bf16[1024,768]{1,0:T(8,128)(2,1)}, f32[6,2,128]{2,1,0:T(2,128)}, f32[6,2,256]{2,1,0:T(2,128)}) custom-call(s32[1]{0:T(128)S(6)} %copy.91.limit_ref.dec_ref, f32[12]{0:T(128)} %hs_ref.13, f32[12,256]{1,0:T(8,128)} %bias_ref.9, bf16[1024,768]{1,0:T(8,128)(2,1)} %get-tuple-element.217.q_ref, ...), custom_call_target="tpu_custom_call" | custom-call | flops 805306368000 | bytes 1258291200 | tf_op jit(solution)/shard_map/attn_bwd/pallas_call | solution.py:210
  252.9 2.6 deal.4
  255.5 2.4 collective-permute-start.10
  259.4 6.7 %halve.12 = (f32[8,1,24,1536]{3,2,1,0:T(8,128)}, f32[8,1,24,1536]{3,2,1,0:T(8,128)}, f32[4,2,24,1536]{3,2,1,0:T(8,128)}, f32[4,2,24,1536]{3,2,1,0:T(8,128)}) custom-call(s32[2]{0:T(128)} %get-tuple-element.434.bit_ref, f32[8,2,1,24,3072]{4,3,2,1,0:T(8,128)} %bitcast.60, f32[8,2,1,24,3072]{4,3,2,1,0:T(8,128)} %bitcast.61, ...), custom_call_target="tpu_custom_call" | custom-call | flops 200000 | bytes 200000 | tf_op jit(solution)/shard_map/halve/pallas_call | solution.py:524
  266.7 5.0 %collective-permute-done.4 = f32[4,1,24,3840]{3,2,0,1:T(8,128)} collective-permute-done((f32[4,1,24,3840]{3,2,0,1:T(8,128)}, f32[4,1,24,3840]{3,2,0,1:T(8,128)}, u32[]{:S(2)}, u32[]{:S(2)}) %collective-permute-start.4) | collective-permute-done | bytes 1474592 | tf_op jit(solution)/shard_map/ppermute | solution.py:571
  271.7 1.7 collective-permute-start.8
  273.4 15.1 %attn_bwd.5 = (bf16[1024,768]{1,0:T(8,128)(2,1)}, bf16[1024,768]{1,0:T(8,128)(2,1)}, bf16[1024,768]{1,0:T(8,128)(2,1)}, f32[6,2,128]{2,1,0:T(2,128)}, f32[6,2,256]{2,1,0:T(2,128)}) custom-call(s32[1]{0:T(128)S(6)} %copy.91.limit_ref.dec_ref, f32[12]{0:T(128)} %hs_ref.13, ...), custom_call_target="tpu_custom_call", output_to_operand_aliasing={{0}: (9, {}), {1}: (10, {}), {2}: (11, {}), {3}: (12, {}), ... | custom-call | flops 805306368000 | bytes 1258291200 | tf_op jit(solution)/shard_map/attn_bwd/pallas_call | solution.py:210
  288.4 3.0 deal.5
  291.4 11.7 %tail.1 = (f32[1024,768]{1,0:T(8,128)}, bf16[1024,768]{1,0:T(8,128)(2,1)}, bf16[1024,768]{1,0:T(8,128)(2,1)}, f32[16,24,128]{2,1,0:T(8,128)}, f32[16,24,128]{2,1,0:T(8,128)}) custom-call(s32[1]{0:T(128)S(6)} %and.9.core_ref, f32[8,128]{1,0:T(8,128)} %get-tuple-element.227.fac_ref, f32[12]{0:T(128)} %hs_ref.13, bf16[1024,768]{1,0:T(8,128)(2,1)} %bitcast.122, ...), custom_call_target="tpu_custom_call" | custom-call | flops 200000 | bytes 200000 | tf_op jit(solution)/shard_map/tail/pallas_call | solution.py:446
  303.2 9.3 %wgrad.7 = (f32[16,24,2304]{2,1,0:T(8,128)}, f32[16,24,2304]{2,1,0:T(8,128)}) custom-call(s32[1]{0:T(128)S(6)} %and.9.core_ref, f32[8,128]{1,0:T(8,128)} %get-tuple-element.227.fac_ref, bf16[1024,768]{1,0:T(8,128)(2,1)} %get-tuple-element.306.refs_0_, bf16[1024,768]{1,0:T(8,128)(2,1)} %get-tuple-element.307.refs_1_, ...), custom_call_target="tpu_custom_call" | custom-call | flops 1449551462400 | bytes 2673868800 | tf_op jit(solution)/shard_map/wgrad/pallas_call | solution.py:501
  312.4 1.5 collective-permute-start.14
  314.0 2.4 collective-permute-start.15
  317.5 4.7 %halve.13 = (f32[4,1,24,1536]{3,2,1,0:T(8,128)}, f32[4,1,24,1536]{3,2,1,0:T(8,128)}, f32[4,1,24,1536]{3,2,1,0:T(8,128)}, f32[4,1,24,1536]{3,2,1,0:T(8,128)}) custom-call(s32[2]{0:T(128)} %get-tuple-element.435.bit_ref, f32[4,2,1,24,1536]{4,3,2,1,0:T(8,128)} %bitcast.112, f32[4,2,1,24,1536]{4,3,2,1,0:T(8,128)} %bitcast.113, ...), custom_call_target="tpu_custom_call" | custom-call | flops 200000 | bytes 200000 | tf_op jit(solution)/shard_map/halve/pallas_call | solution.py:524
  322.6 1.7 collective-permute-start.18
  324.4 5.4 %halve.14 = (f32[8,1,24,1152]{3,2,1,0:T(8,128)}, f32[8,1,24,1152]{3,2,1,0:T(8,128)}, f32[4,2,24,1152]{3,2,1,0:T(8,128)}, f32[4,2,24,1152]{3,2,1,0:T(8,128)}, f32...) custom-call(s32[3]{0:T(128)} %get-tuple-element.436.bit_ref, f32[8,2,1,24,2304]{4,3,2,1,0:T(8,128)} %bitcast.64, ...), custom_call_target="tpu_custom_call" | custom-call | flops 200000 | bytes 200000 | tf_op jit(solution)/shard_map/halve/pallas_call | solution.py:524
  330.8 1.5 collective-permute-start.22
  332.3 9.8 %collective-permute-done.15.refs_6_ = f32[24,3840]{1,0:T(8,128)S(1)} collective-permute-done((f32[24,3840]{1,0:T(8,128)S(1)}, f32[24,3840]{1,0:T(8,128)S(1)}, u32[]{:S(2)}, u32[]{:S(2)}) %collective-permute-start.15) | collective-permute-done | bytes 368672 | tf_op jit(solution)/shard_map/ppermute | solution.py:609
  344.2 6.7 %memory.1 = f32[1024,768]{1,0:T(8,128)} custom-call(bf16[1024,768]{1,0:T(8,128)(2,1)} %get-tuple-element.331.refs_4_.k_ref, bf16[1024,768]{1,0:T(8,128)(2,1)} %get-tuple-element.251.gv_ref.refs_3_.v_ref, bf16[768,768]{1,0:T(8,128)(2,1)} %ck.3, bf16[768,768]{1,0:T(8,128)(2,1)} %cv.3), custom_call_target="tpu_custom_call" | custom-call | flops 483183820800 | bytes 1730150400 | tf_op jit(solution)/shard_map/memory/pallas_call | solution.py:457
  350.9 2.8 deal.6
  353.7 5.8 %collective-permute-done.24 = f32[8,1,24,128]{3,2,1,0:T(8,128)} collective-permute-done((f32[8,1,24,128]{3,2,1,0:T(8,128)}, f32[8,1,24,128]{3,2,1,0:T(8,128)}, u32[]{:S(2)}, u32[]{:S(2)}) %collective-permute-start.24) | collective-permute-done | bytes 98336 | tf_op jit(solution)/shard_map/ppermute | solution.py:571
  359.4 3.9 halve.15
  363.4 1.7 collective-permute-start.25
  367.7 3.8 collective-permute-start.20
  371.5 7.4 %collective-permute-done.19.refs_9_ = f32[24,3072]{1,0:T(8,128)S(1)} collective-permute-done((f32[24,3072]{1,0:T(8,128)S(1)}, f32[24,3072]{1,0:T(8,128)S(1)}, u32[]{:S(2)}, u32[]{:S(2)}) %collective-permute-start.19) | collective-permute-done | bytes 294944 | tf_op jit(solution)/shard_map/ppermute | solution.py:609
  379.1 12.9 %collective-permute-done.20.refs_10_ = f32[24,3072]{1,0:T(8,128)S(1)} collective-permute-done((f32[24,3072]{1,0:T(8,128)S(1)}, f32[24,3072]{1,0:T(8,128)S(1)}, u32[]{:S(2)}, u32[]{:S(2)}) %collective-permute-start.20) | collective-permute-done | bytes 294944 | tf_op jit(solution)/shard_map/ppermute | solution.py:609
  393.0 2.5 deal.7
  395.5 3.8 collective-permute-start.28
  401.7 4.0 collective-permute-done.28.refs_13_
  405.8 11.5 %collective-permute-done.29.refs_14_ = f32[24,2432]{1,0:T(8,128)S(1)} collective-permute-done((f32[24,2432]{1,0:T(8,128)}, f32[24,2432]{1,0:T(8,128)S(1)}, u32[]{:S(2)}, u32[]{:S(2)}) %collective-permute-start.29) | collective-permute-done | bytes 233504 | tf_op jit(solution)/shard_map/ppermute | solution.py:609
  418.0 3.6 finish.1
  (90 shorter events, 19.0 us)
Async XLA Ops:
  2.0 64.5 %all-to-all-start = ((f32[32,8,128]{2,1,0:T(8,128)}), f32[32,8,128]{2,1,0:T(8,128)}, u32[]{:S(2)}, u32[]{:S(2)}) async-start(f32[32,8,128]{2,1,0:T(8,128)} %broadcast_in_dim.17), calls=%async_computation | async-start | bytes 262144 | tf_op jit(solution)/shard_map/all_to_all | solution.py:625
  135.4 11.5 %collective-permute-start.1 = (f32[16,24,3840]{2,1,0:T(8,128)}, f32[16,24,3840]{2,1,0:T(8,128)}, u32[]{:S(2)}, u32[]{:S(2)}) collective-permute-start(f32[16,24,3840]{2,1,0:T(8,128)} %get-tuple-element.233), channel_id=1, source_target_pairs={{0,1},{1,0},{2,3},{3,2},{4,5},{5,4},{6,7},{7,6},{8,9},{9,8},{10,11... | collective-permute-start | bytes 17694728 | tf_op jit(solution)/shard_map/ppermute | solution.py:571
  146.0 10.1 %collective-permute-start = (f32[16,96,768]{2,1,0:T(8,128)}, f32[16,96,768]{2,1,0:T(8,128)}, u32[]{:S(2)}, u32[]{:S(2)}) collective-permute-start(f32[16,96,768]{2,1,0:T(8,128)} %get-tuple-element.237), channel_id=1, source_target_pairs={{0,1},{1,0},{2,3},{3,2},{4,5},{5,4},{6,7},{7,6},{8,9},{9,8},{10,11... | collective-permute-start | bytes 14155784 | tf_op jit(solution)/shard_map/ppermute | solution.py:571
  154.4 77.4 %collective-permute-start.2 = (f32[4,2,24,3840]{3,2,1,0:T(8,128)}, f32[4,2,24,3840]{3,2,1,0:T(8,128)}, u32[]{:S(2)}, u32[]{:S(2)}) collective-permute-start(f32[4,2,24,3840]{3,2,1,0:T(8,128)} %get-tuple-element.241), channel_id=1, source_target_pairs={{0,4},{1,5},{2,6},{3,7},{4,0},{5,1},{6,2},{7,3},{8,12},{9,13},{10,... | collective-permute-start | bytes 8847368 | tf_op jit(solution)/shard_map/ppermute | solution.py:571
  162.0 53.3 %collective-permute-start.3 = (f32[8,1,96,768]{3,2,1,0:T(8,128)}, f32[8,1,96,768]{3,2,1,0:T(8,128)}, u32[]{:S(2)}, u32[]{:S(2)}) collective-permute-start(f32[8,1,96,768]{3,2,1,0:T(8,128)} %get-tuple-element.244), channel_id=1, source_target_pairs={{0,2},{1,3},{2,0},{3,1},{4,6},{5,7},{6,4},{7,5},{8,10},{9,11},{10,... | collective-permute-start | bytes 7077896 | tf_op jit(solution)/shard_map/ppermute | solution.py:571
  219.2 33.7 %collective-permute-start.6 = (f32[4,1,96,768]{3,2,0,1:T(8,128)}, f32[4,1,96,768]{3,2,0,1:T(8,128)}, u32[]{:S(2)}, u32[]{:S(2)}) collective-permute-start(f32[4,1,96,768]{3,2,0,1:T(8,128)} %bitcast.142), channel_id=1, source_target_pairs={{0,4},{1,5},{2,6},{3,7},{4,0},{5,1},{6,2},{7,3},{8,12},{9,13},{10,... | collective-permute-start | bytes 3538952 | tf_op jit(solution)/shard_map/ppermute | solution.py:571
  231.8 27.6 %collective-permute-start.5 = (f32[16,24,3072]{2,1,0:T(8,128)}, f32[16,24,3072]{2,1,0:T(8,128)}, u32[]{:S(2)}, u32[]{:S(2)}) collective-permute-start(f32[16,24,3072]{2,1,0:T(8,128)} %get-tuple-element.264), channel_id=1, source_target_pairs={{0,1},{1,0},{2,3},{3,2},{4,5},{5,4},{6,7},{7,6},{8,9},{9,8},{10,11... | collective-permute-start | bytes 14155784 | tf_op jit(solution)/shard_map/ppermute | solution.py:571
  236.3 35.4 %collective-permute-start.4 = (f32[4,1,24,3840]{3,2,0,1:T(8,128)}, f32[4,1,24,3840]{3,2,0,1:T(8,128)}, u32[]{:S(2)}, u32[]{:S(2)}) collective-permute-start(f32[4,1,24,3840]{3,2,0,1:T(8,128)} %bitcast.141), channel_id=1, source_target_pairs={{0,2},{1,3},{2,0},{3,1},{4,6},{5,7},{6,4},{7,5},{8,10},{9,11},{10,... | collective-permute-start | bytes 4423688 | tf_op jit(solution)/shard_map/ppermute | solution.py:571
  255.5 47.5 %collective-permute-start.10 = (f32[96,768]{1,0:T(8,128)}, f32[96,768]{1,0:T(8,128)}, u32[]{:S(2)}, u32[]{:S(2)}) collective-permute-start(f32[96,768]{1,0:T(8,128)} %get-tuple-element.304), channel_id=1, source_target_pairs={{0,16},{1,17},{2,18},{3,19},{4,20},{5,21},{6,22},{7,23},{8,24},{9,... | collective-permute-start | bytes 884744 | tf_op jit(solution)/shard_map/ppermute | solution.py:609
  257.9 45.2 %collective-permute-start.11 = (f32[96,768]{1,0:T(8,128)}, f32[96,768]{1,0:T(8,128)}, u32[]{:S(2)}, u32[]{:S(2)}) collective-permute-start(f32[96,768]{1,0:T(8,128)} %get-tuple-element.305), channel_id=1, source_target_pairs={{0,24},{1,25},{2,26},{3,27},{4,28},{5,29},{6,30},{7,31},{8,16},{9,... | collective-permute-start | bytes 884744 | tf_op jit(solution)/shard_map/ppermute | solution.py:609
  259.4 43.7 %collective-permute-start.9 = (f32[96,768]{1,0:T(8,128)}, f32[96,768]{1,0:T(8,128)}, u32[]{:S(2)}, u32[]{:S(2)}) collective-permute-start(f32[96,768]{1,0:T(8,128)} %get-tuple-element.303), channel_id=1, source_target_pairs={{0,8},{1,9},{2,10},{3,11},{4,12},{5,13},{6,14},{7,15},{8,0},{9,1},... | collective-permute-start | bytes 884744 | tf_op jit(solution)/shard_map/ppermute | solution.py:609
  266.1 37.0 %collective-permute-start.7 = (f32[8,1,24,1536]{3,2,1,0:T(8,128)}, f32[8,1,24,1536]{3,2,1,0:T(8,128)}, u32[]{:S(2)}, u32[]{:S(2)}) collective-permute-start(f32[8,1,24,1536]{3,2,1,0:T(8,128)} %get-tuple-element.282), channel_id=1, source_target_pairs={{0,2},{1,3},{2,0},{3,1},{4,6},{5,7},{6,4},{7,5},{8,10},{9,11},{10,... | collective-permute-start | bytes 3538952 | tf_op jit(solution)/shard_map/ppermute | solution.py:571
  271.7 31.4 %collective-permute-start.8 = (f32[4,2,24,1536]{3,2,1,0:T(8,128)}, f32[4,2,24,1536]{3,2,1,0:T(8,128)}, u32[]{:S(2)}, u32[]{:S(2)}) collective-permute-start(f32[4,2,24,1536]{3,2,1,0:T(8,128)} %get-tuple-element.283), channel_id=1, source_target_pairs={{0,4},{1,5},{2,6},{3,7},{4,0},{5,1},{6,2},{7,3},{8,12},{9,13},{10,... | collective-permute-start | bytes 3538952 | tf_op jit(solution)/shard_map/ppermute | solution.py:571
  303.1 9.3 %copy-start.16 = (f32[24,3840]{1,0:T(8,128)S(1)}, f32[24,3840]{1,0:T(8,128)}, u32[]{:S(2)}) copy-start(f32[24,3840]{1,0:T(8,128)} %get-tuple-element.328) | copy-start | bytes 1105924
  303.1 10.8 %copy-start.15 = (f32[24,3840]{1,0:T(8,128)S(1)}, f32[24,3840]{1,0:T(8,128)}, u32[]{:S(2)}) copy-start(f32[24,3840]{1,0:T(8,128)} %get-tuple-element.329) | copy-start | bytes 1105924
  303.1 13.3 %copy-start.14 = (f32[24,3840]{1,0:T(8,128)S(1)}, f32[24,3840]{1,0:T(8,128)}, u32[]{:S(2)}) copy-start(f32[24,3840]{1,0:T(8,128)} %get-tuple-element.330) | copy-start | bytes 1105924
  303.1 13.7 %copy-start.20 = (f32[16,24,128]{2,1,0:T(8,128)S(1)}, f32[16,24,128]{2,1,0:T(8,128)}, u32[]{:S(2)}) copy-start(f32[16,24,128]{2,1,0:T(8,128)} %get-tuple-element.302) | copy-start | bytes 589828
  312.4 10.2 %collective-permute-start.12 = (f32[16,24,2304]{2,1,0:T(8,128)}, f32[16,24,2304]{2,1,0:T(8,128)S(1)}, u32[]{:S(2)}, u32[]{:S(2)}) collective-permute-start(f32[16,24,2304]{2,1,0:T(8,128)} %get-tuple-element.309), channel_id=1, source_target_pairs={{0,1},{1,0},{2,3},{3,2},{4,5},{5,4},{6,7},{7,6},{8,9},{9,8},{10,11... | collective-permute-start | bytes 10616840 | tf_op jit(solution)/shard_map/ppermute | solution.py:571
  312.4 18.4 %collective-permute-start.14 = (f32[24,3840]{1,0:T(8,128)S(1)}, f32[24,3840]{1,0:T(8,128)S(1)}, u32[]{:S(2)}, u32[]{:S(2)}) collective-permute-start(f32[24,3840]{1,0:T(8,128)S(1)} %copy-done.16), channel_id=1, source_target_pairs={{0,8},{1,9},{2,10},{3,11},{4,12},{5,13},{6,14},{7,15},{8,0},{9,1},... | collective-permute-start | bytes 1105928 | tf_op jit(solution)/shard_map/ppermute | solution.py:609
  314.0 28.2 %collective-permute-start.15 = (f32[24,3840]{1,0:T(8,128)S(1)}, f32[24,3840]{1,0:T(8,128)S(1)}, u32[]{:S(2)}, u32[]{:S(2)}) collective-permute-start(f32[24,3840]{1,0:T(8,128)S(1)} %copy-done.15), channel_id=1, source_target_pairs={{0,16},{1,17},{2,18},{3,19},{4,20},{5,21},{6,22},{7,23},{8,24},{9,... | collective-permute-start | bytes 1105928 | tf_op jit(solution)/shard_map/ppermute | solution.py:609
  316.4 26.3 %collective-permute-start.16 = (f32[24,3840]{1,0:T(8,128)S(1)}, f32[24,3840]{1,0:T(8,128)S(1)}, u32[]{:S(2)}, u32[]{:S(2)}) collective-permute-start(f32[24,3840]{1,0:T(8,128)S(1)} %copy-done.14), channel_id=1, source_target_pairs={{0,24},{1,25},{2,26},{3,27},{4,28},{5,29},{6,30},{7,31},{8,16},{9,... | collective-permute-start | bytes 1105928 | tf_op jit(solution)/shard_map/ppermute | solution.py:609
  316.9 5.3 %collective-permute-start.13 = (f32[16,24,128]{2,1,0:T(8,128)S(1)}, f32[16,24,128]{2,1,0:T(8,128)S(1)}, u32[]{:S(2)}, u32[]{:S(2)}) collective-permute-start(f32[16,24,128]{2,1,0:T(8,128)S(1)} %copy-done.20), channel_id=1, source_target_pairs={{0,1},{1,0},{2,3},{3,2},{4,5},{5,4},{6,7},{7,6},{8,9},{9,8},{10,11... | collective-permute-start | bytes 589832 | tf_op jit(solution)/shard_map/ppermute | solution.py:571
  322.1 2.1 copy-start.3
  322.1 28.7 %collective-permute-start.17 = (f32[4,1,24,1536]{3,2,0,1:T(8,128)}, f32[4,1,24,1536]{3,2,0,1:T(8,128)}, u32[]{:S(2)}, u32[]{:S(2)}) collective-permute-start(f32[4,1,24,1536]{3,2,0,1:T(8,128)} %bitcast.144), channel_id=1, source_target_pairs={{0,4},{1,5},{2,6},{3,7},{4,0},{5,1},{6,2},{7,3},{8,12},{9,13},{10,... | collective-permute-start | bytes 1769480 | tf_op jit(solution)/shard_map/ppermute | solution.py:571
  322.6 1.8 copy-start
  322.6 28.3 %collective-permute-start.18 = (f32[4,1,24,1536]{3,2,0,1:T(8,128)}, f32[4,1,24,1536]{3,2,0,1:T(8,128)}, u32[]{:S(2)}, u32[]{:S(2)}) collective-permute-start(f32[4,1,24,1536]{3,2,0,1:T(8,128)} %bitcast.143), channel_id=1, source_target_pairs={{0,2},{1,3},{2,0},{3,1},{4,6},{5,7},{6,4},{7,5},{8,10},{9,11},{10,... | collective-permute-start | bytes 1769480 | tf_op jit(solution)/shard_map/ppermute | solution.py:571
  330.8 20.0 %copy-start.5 = (f32[24,3840]{1,0:T(8,128)}, f32[24,3840]{1,0:T(8,128)S(1)}, u32[]{:S(2)}) copy-start(f32[24,3840]{1,0:T(8,128)S(1)} %collective-permute-done.14.refs_5_) | copy-start | bytes 1105924
  330.8 28.6 %collective-permute-start.22 = (f32[8,1,24,1152]{3,2,1,0:T(8,128)}, f32[8,1,24,1152]{3,2,1,0:T(8,128)}, u32[]{:S(2)}, u32[]{:S(2)}) collective-permute-start(f32[8,1,24,1152]{3,2,1,0:T(8,128)} %get-tuple-element.325), channel_id=1, source_target_pairs={{0,2},{1,3},{2,0},{3,1},{4,6},{5,7},{6,4},{7,5},{8,10},{9,11},{10,... | collective-permute-start | bytes 2654216 | tf_op jit(solution)/shard_map/ppermute | solution.py:571
  342.1 8.7 %copy-start.6 = (f32[24,3840]{1,0:T(8,128)}, f32[24,3840]{1,0:T(8,128)S(1)}, u32[]{:S(2)}) copy-start(f32[24,3840]{1,0:T(8,128)S(1)} %collective-permute-done.15.refs_6_) | copy-start | bytes 1105924
  342.1 17.3 %collective-permute-start.23 = (f32[4,2,24,1152]{3,2,1,0:T(8,128)}, f32[4,2,24,1152]{3,2,1,0:T(8,128)}, u32[]{:S(2)}, u32[]{:S(2)}) collective-permute-start(f32[4,2,24,1152]{3,2,1,0:T(8,128)} %get-tuple-element.326), channel_id=1, source_target_pairs={{0,4},{1,5},{2,6},{3,7},{4,0},{5,1},{6,2},{7,3},{8,12},{9,13},{10,... | collective-permute-start | bytes 2654216 | tf_op jit(solution)/shard_map/ppermute | solution.py:571
  342.7 8.2 %copy-start.7 = (f32[24,3840]{1,0:T(8,128)}, f32[24,3840]{1,0:T(8,128)S(1)}, u32[]{:S(2)}) copy-start(f32[24,3840]{1,0:T(8,128)S(1)} %collective-permute-done.16.refs_7_) | copy-start | bytes 1105924
  342.7 16.7 %collective-permute-start.24 = (f32[8,1,24,128]{3,2,1,0:T(8,128)}, f32[8,1,24,128]{3,2,1,0:T(8,128)}, u32[]{:S(2)}, u32[]{:S(2)}) collective-permute-start(f32[8,1,24,128]{3,2,1,0:T(8,128)} %get-tuple-element.327), channel_id=1, source_target_pairs={{0,2},{1,3},{2,0},{3,1},{4,6},{5,7},{6,4},{7,5},{8,10},{9,11},{10,... | collective-permute-start | bytes 294920 | tf_op jit(solution)/shard_map/ppermute | solution.py:571
  353.7 12.8 %copy-start.19 = (f32[24,3072]{1,0:T(8,128)S(1)}, f32[24,3072]{1,0:T(8,128)}, u32[]{:S(2)}) copy-start(f32[24,3072]{1,0:T(8,128)} %get-tuple-element.339) | copy-start | bytes 884740
  353.7 14.0 %copy-start.18 = (f32[24,3072]{1,0:T(8,128)S(1)}, f32[24,3072]{1,0:T(8,128)}, u32[]{:S(2)}) copy-start(f32[24,3072]{1,0:T(8,128)} %get-tuple-element.340) | copy-start | bytes 884740
  353.7 17.8 %copy-start.17 = (f32[24,3072]{1,0:T(8,128)S(1)}, f32[24,3072]{1,0:T(8,128)}, u32[]{:S(2)}) copy-start(f32[24,3072]{1,0:T(8,128)} %get-tuple-element.341) | copy-start | bytes 884740
  363.4 28.7 %collective-permute-start.25 = (f32[4,1,24,1152]{3,2,0,1:T(8,128)}, f32[4,1,24,1152]{3,2,0,1:T(8,128)S(1)}, u32[]{:S(2)}, u32[]{:S(2)}) collective-permute-start(f32[4,1,24,1152]{3,2,0,1:T(8,128)} %bitcast.146), channel_id=1, source_target_pairs={{0,4},{1,5},{2,6},{3,7},{4,0},{5,1},{6,2},{7,3},{8,12},{9,13},{10,... | collective-permute-start | bytes 1327112 | tf_op jit(solution)/shard_map/ppermute | solution.py:571
  365.0 27.0 %collective-permute-start.26 = (f32[4,1,24,1152]{3,2,0,1:T(8,128)}, f32[4,1,24,1152]{3,2,0,1:T(8,128)S(1)}, u32[]{:S(2)}, u32[]{:S(2)}) collective-permute-start(f32[4,1,24,1152]{3,2,0,1:T(8,128)} %bitcast.145), channel_id=1, source_target_pairs={{0,2},{1,3},{2,0},{3,1},{4,6},{5,7},{6,4},{7,5},{8,10},{9,11},{10,... | collective-permute-start | bytes 1327112 | tf_op jit(solution)/shard_map/ppermute | solution.py:571
  366.5 12.4 %collective-permute-start.19 = (f32[24,3072]{1,0:T(8,128)S(1)}, f32[24,3072]{1,0:T(8,128)S(1)}, u32[]{:S(2)}, u32[]{:S(2)}) collective-permute-start(f32[24,3072]{1,0:T(8,128)S(1)} %copy-done.19), channel_id=1, source_target_pairs={{0,8},{1,9},{2,10},{3,11},{4,12},{5,13},{6,14},{7,15},{8,0},{9,1},... | collective-permute-start | bytes 884744 | tf_op jit(solution)/shard_map/ppermute | solution.py:609
  367.7 24.3 %collective-permute-start.20 = (f32[24,3072]{1,0:T(8,128)S(1)}, f32[24,3072]{1,0:T(8,128)S(1)}, u32[]{:S(2)}, u32[]{:S(2)}) collective-permute-start(f32[24,3072]{1,0:T(8,128)S(1)} %copy-done.18), channel_id=1, source_target_pairs={{0,16},{1,17},{2,18},{3,19},{4,20},{5,21},{6,22},{7,23},{8,24},{9,... | collective-permute-start | bytes 884744 | tf_op jit(solution)/shard_map/ppermute | solution.py:609
  371.5 20.5 %collective-permute-start.21 = (f32[24,3072]{1,0:T(8,128)S(1)}, f32[24,3072]{1,0:T(8,128)S(1)}, u32[]{:S(2)}, u32[]{:S(2)}) collective-permute-start(f32[24,3072]{1,0:T(8,128)S(1)} %copy-done.17), channel_id=1, source_target_pairs={{0,24},{1,25},{2,26},{3,27},{4,28},{5,29},{6,30},{7,31},{8,16},{9,... | collective-permute-start | bytes 884744 | tf_op jit(solution)/shard_map/ppermute | solution.py:609
  378.9 38.4 %copy-start.8 = (f32[24,3072]{1,0:T(8,128)}, f32[24,3072]{1,0:T(8,128)S(1)}, u32[]{:S(2)}) copy-start(f32[24,3072]{1,0:T(8,128)S(1)} %collective-permute-done.19.refs_9_) | copy-start | bytes 884740
  378.9 13.2 %collective-permute-start.27 = (f32[4,1,24,128]{3,2,0,1:T(8,128)}, f32[4,1,24,128]{3,2,0,1:T(8,128)S(1)}, u32[]{:S(2)}, u32[]{:S(2)}) collective-permute-start(f32[4,1,24,128]{3,2,0,1:T(8,128)} %bitcast.147), channel_id=1, source_target_pairs={{0,4},{1,5},{2,6},{3,7},{4,0},{5,1},{6,2},{7,3},{8,12},{9,13},{10,... | collective-permute-start | bytes 147464 | tf_op jit(solution)/shard_map/ppermute | solution.py:571
  392.0 25.3 %copy-start.9 = (f32[24,3072]{1,0:T(8,128)}, f32[24,3072]{1,0:T(8,128)S(1)}, u32[]{:S(2)}) copy-start(f32[24,3072]{1,0:T(8,128)S(1)} %collective-permute-done.20.refs_10_) | copy-start | bytes 884740
  392.0 25.3 %copy-start.10 = (f32[24,3072]{1,0:T(8,128)}, f32[24,3072]{1,0:T(8,128)S(1)}, u32[]{:S(2)}) copy-start(f32[24,3072]{1,0:T(8,128)S(1)} %collective-permute-done.21.refs_11_) | copy-start | bytes 884740
  395.5 10.2 %collective-permute-start.28 = (f32[24,2432]{1,0:T(8,128)}, f32[24,2432]{1,0:T(8,128)S(1)}, u32[]{:S(2)}, u32[]{:S(2)}) collective-permute-start(f32[24,2432]{1,0:T(8,128)} %get-tuple-element.364), channel_id=1, source_target_pairs={{0,8},{1,9},{2,10},{3,11},{4,12},{5,13},{6,14},{7,15},{8,0},{9,1},... | collective-permute-start | bytes 700424 | tf_op jit(solution)/shard_map/ppermute | solution.py:609
  399.3 17.9 %collective-permute-start.29 = (f32[24,2432]{1,0:T(8,128)}, f32[24,2432]{1,0:T(8,128)S(1)}, u32[]{:S(2)}, u32[]{:S(2)}) collective-permute-start(f32[24,2432]{1,0:T(8,128)} %get-tuple-element.365), channel_id=1, source_target_pairs={{0,16},{1,17},{2,18},{3,19},{4,20},{5,21},{6,22},{7,23},{8,24},{9,... | collective-permute-start | bytes 700424 | tf_op jit(solution)/shard_map/ppermute | solution.py:609
  400.3 16.9 %collective-permute-start.30 = (f32[24,2432]{1,0:T(8,128)}, f32[24,2432]{1,0:T(8,128)S(1)}, u32[]{:S(2)}, u32[]{:S(2)}) collective-permute-start(f32[24,2432]{1,0:T(8,128)} %get-tuple-element.366), channel_id=1, source_target_pairs={{0,24},{1,25},{2,26},{3,27},{4,28},{5,29},{6,30},{7,31},{8,16},{9,... | collective-permute-start | bytes 700424 | tf_op jit(solution)/shard_map/ppermute | solution.py:609
  405.8 11.5 %copy-start.11 = (f32[24,2432]{1,0:T(8,128)}, f32[24,2432]{1,0:T(8,128)S(1)}, u32[]{:S(2)}) copy-start(f32[24,2432]{1,0:T(8,128)S(1)} %collective-permute-done.28.refs_13_) | copy-start | bytes 700420
  (5 other events, 4.0 us)
